TPU v7x, 32 devices: a whole 2x2x4 slice. The times are simulated.
32 devices in a mesh: dp: 4 (over y, x), ctx: 8 (over z, core).
Axes of the slice: x: 2, y: 2, z: 4, core: 2. Of those that a mesh axis runs over, the one named last changes fastest.
Arguments:
- query_matrix: bfloat16 [4, 1024, 2048], P('dp', 'ctx'), may hold values from -16 to 16
- key_matrix: bfloat16 [4, 1024, 512], P('dp', 'ctx'), may hold values from -16 to 16
- value_matrix: bfloat16 [4, 1024, 512], P('dp', 'ctx'), may hold values from -6 to 6
- output_gradient: bfloat16 [4, 1024, 2048], P('dp', 'ctx'), may hold values from -6 to 6
- hidden_in: bfloat16 [4, 1024, 4096], P('dp', 'ctx'), may hold values from -6 to 6
- doc_lengths: int32 [4, 16], P('dp'), may hold values from 1 to 768, 1024 in all within a row
- querya: bfloat16 [16, 4096], replicated, may hold values from -0.09375 to 0.09375
- queryb: bfloat16 [16, 2048], replicated, may hold values from -1.5 to 1.5
- valuea: bfloat16 [16, 4096], replicated, may hold values from -0.09375 to 0.09375
- valueb: bfloat16 [16, 512], replicated, may hold values from -1.5 to 1.5
Outputs:
- query_grad: bfloat16 [4, 1024, 2048], P('dp', 'ctx')
- key_grad: bfloat16 [4, 1024, 512], P('dp', 'ctx')
- value_gradient: bfloat16 [4, 1024, 512], P('dp', 'ctx')
- querya_grad: float32 [16, 4096], replicated
- queryb_grad: float32 [16, 2048], replicated
- valuea_grad: float32 [16, 4096], replicated
- valueb_grad: float32 [16, 512], replicated
Inputs may be any that keep to these rules, and one draw needn't show every extreme that they name: `doc_lengths`: row b lists, in order, the lengths of the 16 documents packed into sequence b; they sum to 1024.
All inputs are finite; a program needn't handle non-finite values.
Results may differ from a plain program's by a relative error of at most 0.022.
Values may be sent and summed in bfloat16 or wider, within the bound.
No kernel may reach another device: no remote copies, remote signals or barrier semaphores. Data moves between devices by JAX's collectives and lax.ppermute only.
A program may use at most 128 MiB of HBM per device.

v0:
```python
import functools

import jax
import jax.numpy as jnp
from jax import lax
from jax.experimental import pallas as pl
from jax.experimental.pallas import tpu as pltpu
from jax.sharding import PartitionSpec as P


QUERY_HEADS = 16
KEY_VALUE_HEADS = 4
HEAD_WIDTH = 128
NEG_FILL = -1e30
ADAPTER_SCALE = 2.0


F32 = jnp.float32
BF16 = jnp.bfloat16
VM = pl.BlockSpec(memory_space=pltpu.VMEM)
SM = pl.BlockSpec(memory_space=pltpu.SMEM)
AN = pl.BlockSpec(memory_space=pl.ANY)

CORE_HEADS = KEY_VALUE_HEADS // 2
GROUP = QUERY_HEADS // KEY_VALUE_HEADS
Q_HALF = QUERY_HEADS * HEAD_WIDTH // 2
KV_HALF = CORE_HEADS * HEAD_WIDTH


def dot_nn(a, b):
    return lax.dot_general(a, b, (((1,), (0,)), ((), ())), preferred_element_type=F32)


def dot_nt(a, b):
    return lax.dot_general(a, b, (((1,), (1,)), ((), ())), preferred_element_type=F32)


def dot_tn(a, b):
    return lax.dot_general(a, b, (((0,), (0,)), ((), ())), preferred_element_type=F32)


def half_of(ref, core, width):
    return ref[:, pl.ds(pl.multiple_of(core * width, 128), width)]


def call(body, outs, args, scratch=(), flops=0, smem=(), after=()):
    size = sum(a.size * a.dtype.itemsize for a in args)
    size += sum(o.size * o.dtype.itemsize for o in outs)
    return kernel_call(body, outs, args, scratch, flops, size, smem, after)


def kernel_call(body, outs, args, scratch, flops, size, smem, after):
    return pl.pallas_call(
        body,
        out_shape=outs,
        in_specs=[SM if i in smem else AN if i in after else VM for i in range(len(args))],
        out_specs=[VM] * len(outs),
        scratch_shapes=list(scratch),
        compiler_params=pltpu.CompilerParams(vmem_limit_bytes=60 << 20),
        cost_estimate=pl.CostEstimate(flops=flops, bytes_accessed=size, transcendentals=0),
    )(*args)


def split_kv(k_ref, v_ref, hidden_ref, qa_ref, va_ref, own_ref, send_ref):
    core = lax.axis_index("ctx") % 2
    rows = k_ref.shape[0]
    for i, ref in enumerate((k_ref, v_ref)):
        columns = slice(i * KV_HALF, (i + 1) * KV_HALF)
        own_ref[:rows, columns] = half_of(ref, core, KV_HALF)
        send_ref[:rows, columns] = half_of(ref, 1 - core, KV_HALF)
    at = 0
    for ref in (qa_ref, va_ref):
        down = dot_nt(ref[...], hidden_ref[...]).astype(BF16)
        for first in range(0, ref.shape[0], 8):
            own_ref[rows:, at : at + rows] = down[first : first + 8]
            send_ref[rows:, at : at + rows] = down[first : first + 8]
            at += rows


def split_rest(q_ref, g_ref, hidden_ref, _, pack_ref, send_ref):
    core = lax.axis_index("ctx") % 2
    pack_ref[:, :Q_HALF] = half_of(q_ref, 1 - core, Q_HALF)
    pack_ref[:, Q_HALF:] = half_of(g_ref, 1 - core, Q_HALF)
    send_ref[...] = half_of(hidden_ref, 1 - core, hidden_ref.shape[1] // 2)


def split_hidden(own_ref, far_ref, *outs):
    index = lax.axis_index("ctx")
    core, chip = index % 2, index // 2
    rows, width = far_ref.shape
    piece = width // 2
    for k in range(2):
        at = (chip % 2 ^ k) * piece
        outs[k][:rows] = own_ref[:, pl.ds(pl.multiple_of(core * width + at, 128), piece)]
        outs[k][rows:] = far_ref[:, pl.ds(pl.multiple_of(at, 128), piece)]


def attention(n_chips, rank, tail, *refs):
    lens_ref, q_ref, g_ref, pack_ref, qb_ref, vb_ref = refs[:6]
    kv_in = refs[6 : 6 + n_chips]
    refs = refs[6 + n_chips :]
    dq_own_ref, dq_send_ref = refs[:2]
    dkv_out = refs[2 : 2 + n_chips]
    message_out = refs[2 + n_chips : 2 + 2 * n_chips]
    kv, proj, dkv, vl, e_ref, dp_ref, stats, p_ref, ds_ref, qs, gs, dqt, ups, low_ref = refs[2 + 2 * n_chips :]
    rows = q_ref.shape[0]
    chip_rows = 2 * rows
    head_scale = HEAD_WIDTH ** (-0.5)
    index = lax.axis_index("ctx")
    core, chip = index % 2, index // 2
    block_rows = kv_in[0].shape[0] // 2

    for k in range(n_chips):
        for side in (0, 1):
            first = side * block_rows
            kv[k, side * rows : (side + 1) * rows] = kv_in[k][first : first + rows]
            for i in range(2 * rank // 8):
                proj[k, 8 * i : 8 * i + 8, side * rows : (side + 1) * rows] = kv_in[k][
                    first + rows : first + block_rows, i * rows : (i + 1) * rows
                ]
    for i in range(CORE_HEADS * GROUP):
        g, j = i // GROUP, i % GROUP
        at = pl.multiple_of(core * Q_HALF + i * HEAD_WIDTH, 128)
        top = slice(j * chip_rows, j * chip_rows + rows)
        low = slice(j * chip_rows + rows, (j + 1) * chip_rows)
        qs[g, top] = q_ref[:, pl.ds(at, HEAD_WIDTH)]
        qs[g, low] = pack_ref[:, i * HEAD_WIDTH : (i + 1) * HEAD_WIDTH]
        gs[g, top] = g_ref[:, pl.ds(at, HEAD_WIDTH)]
        gs[g, low] = pack_ref[:, Q_HALF + i * HEAD_WIDTH : Q_HALF + (i + 1) * HEAD_WIDTH]
    dkv[...] = jnp.zeros_like(dkv)
    vl[...] = jnp.zeros_like(vl)

    def local(t):
        return jnp.where(t < rows, core * rows + t, (1 - core) * rows + t - rows)

    row_pos = chip * chip_rows + local(lax.broadcasted_iota(jnp.int32, (1, chip_rows), 1))
    row_begin = jnp.zeros_like(row_pos)
    first_pos = chip * chip_rows
    first_begin = jnp.int32(0)
    begin = jnp.int32(0)
    for i in range(lens_ref.shape[1]):
        row_begin = jnp.where(row_pos >= begin, jnp.maximum(row_begin, begin), row_begin)
        first_begin = jnp.where(first_pos >= begin, jnp.maximum(first_begin, begin), first_begin)
        begin = begin + lens_ref[0, i]
    key_local = local(lax.broadcasted_iota(jnp.int32, (chip_rows, 1), 0))
    reach = (first_pos - first_begin + chip_rows - 1) // chip_rows + 1
    seen = jnp.minimum(reach, chip + 1)
    parts = [slice(j * chip_rows, (j + 1) * chip_rows) for j in range(GROUP)]

    def one_group(g, _):
        at_k = pl.multiple_of(g * HEAD_WIDTH, 128)
        at_v = pl.multiple_of(KV_HALF + g * HEAD_WIDTH, 128)

        def scores(k, carry):
            keys = kv[k, :, pl.ds(at_k, HEAD_WIDTH)]
            values = kv[k, :, pl.ds(at_v, HEAD_WIDTH)]
            key_pos = (chip - k) * chip_rows + key_local
            visible = (key_pos <= row_pos) & (key_pos >= row_begin)
            new = []
            for part, (top, total, delta) in zip(parts, carry):
                s = dot_nt(keys, qs[g, part]) * head_scale
                s = jnp.where(visible, s, NEG_FILL)
                own_top = jnp.max(s, axis=0, keepdims=True)
                e = jnp.exp(s - own_top)
                dp = dot_nt(values, gs[g, part])
                e_ref[k, :, part] = e
                dp_ref[k, :, part] = dp
                stats[k, :, part] = own_top
                new_top = jnp.maximum(top, own_top)
                old, now = jnp.exp(top - new_top), jnp.exp(own_top - new_top)
                total = total * old + jnp.sum(e, axis=0, keepdims=True) * now
                delta = delta * old + jnp.sum(e * dp, axis=0, keepdims=True) * now
                new.append((new_top, total, delta))
            return tuple(new)

        zero = jnp.zeros((1, chip_rows), F32)
        carry = ((jnp.full((1, chip_rows), NEG_FILL, F32), zero, zero),) * GROUP
        carry = lax.fori_loop(0, seen, scores, carry)
        inverse = [1.0 / total for _, total, _ in carry]
        delta = [d * i for (_, _, d), i in zip(carry, inverse)]
        dqt[...] = jnp.zeros_like(dqt)

        def gradients(k, _):
            keys = kv[k, :, pl.ds(at_k, HEAD_WIDTH)]
            for j, part in enumerate(parts):
                factor = jnp.exp(stats[k, :, part] - carry[j][0]) * inverse[j]
                p = e_ref[k, :, part] * factor
                p_ref[:, part] = p.astype(BF16)
                ds = p * (dp_ref[k, :, part] - delta[j]) * head_scale
                ds_ref[:, part] = ds.astype(BF16)
            ds = ds_ref[...]
            dv = dot_nn(p_ref[...], gs[g]).astype(BF16)
            dkv[k, :, pl.ds(at_k, HEAD_WIDTH)] = dot_nn(ds, qs[g]).astype(BF16)
            dkv[k, :, pl.ds(at_v, HEAD_WIDTH)] = dv
            dqt[...] += dot_tn(keys, ds)
            at_b = pl.multiple_of(core * KV_HALF + g * HEAD_WIDTH, 128)
            vl[chip - k] += dot_nt(vb_ref[:, pl.ds(at_b, HEAD_WIDTH)], dv)
            return 0

        lax.fori_loop(0, seen, gradients, 0)
        at_b = pl.multiple_of(core * Q_HALF + g * GROUP * HEAD_WIDTH, 128)
        for j, part in enumerate(parts):
            up = qb_ref[:, pl.ds(pl.multiple_of(at_b + j * HEAD_WIDTH, 128), HEAD_WIDTH)]
            low_ref[...] += dot_nn(up, dqt[:, part].astype(BF16))
            dq = jnp.transpose(dqt[:, part]).astype(BF16)
            at = pl.ds(pl.multiple_of((g * GROUP + j) * HEAD_WIDTH, 128), HEAD_WIDTH)
            dq_own_ref[:, at] = dq[:rows]
            dq_send_ref[:, at] = dq[rows:]
            ups[:, at] = dot_nn(proj[0, :rank], dq)
        return 0

    low_ref[...] = jnp.zeros_like(low_ref)
    ups[...] = jnp.zeros_like(ups)
    lax.fori_loop(0, CORE_HEADS, one_group, 0)
    total = jnp.zeros((rank, KV_HALF), F32)
    for k in range(n_chips):
        total = total + dot_nn(proj[k, rank:], dkv[k, :, KV_HALF:])
        dkv_out[k][...] = dkv[k]
    ups[:, Q_HALF : Q_HALF + KV_HALF] = total
    for k in range(n_chips):
        message_out[k][:, :chip_rows] = low_ref[...].astype(BF16)
        for i in range(2):
            message_out[k][:, (i + 1) * chip_rows : (i + 2) * chip_rows] = vl[chip ^ k ^ i].astype(BF16)
        at = pl.multiple_of((chip ^ k) * tail, 128)
        message_out[k][:, 3 * chip_rows :] = ups[:, pl.ds(at, tail)].astype(BF16)


def adapters(n_chips, rank, *refs):
    own, far = refs[:n_chips], refs[n_chips : 2 * n_chips]
    hidden = refs[2 * n_chips : 2 * n_chips + 2]
    out_ref = refs[-1]
    chip_rows, width = hidden[0].shape
    rows = chip_rows // 2
    query, value = jnp.zeros((rank, width), F32), jnp.zeros((rank, width), F32)
    for k in range(2):
        for first, other in ((0, rows), (rows, 0)):
            tokens = hidden[k][first : first + rows]
            low = own[k][:, first : first + rows].astype(F32) + far[k][:, other : other + rows].astype(F32)
            query += dot_nn(low.astype(BF16), tokens)
            at = (k + 1) * chip_rows
            low = sum(ref[:, at + first : at + first + rows].astype(F32) for ref in own)
            low += sum(ref[:, at + other : at + other + rows].astype(F32) for ref in far)
            value += dot_nn(low.astype(BF16), tokens)
    out_ref[:, :width] = (ADAPTER_SCALE * query).astype(BF16)
    out_ref[:, width : 2 * width] = (ADAPTER_SCALE * value).astype(BF16)
    tail = sum(ref[:, 3 * chip_rows :].astype(F32) for ref in own)
    out_ref[:, 2 * width :] = (ADAPTER_SCALE * tail).astype(BF16)


def finish_adapters(n_chips, tail, *refs):
    own, far = refs[:n_chips], refs[n_chips : 2 * n_chips]
    qa_ref, qb_ref, va_ref, vb_ref, buffer = refs[-5:]
    index = lax.axis_index("ctx")
    core, chip = index % 2, index // 2
    width = qa_ref.shape[1] // 4
    for half, pieces in ((core, own), (1 - core, far)):
        for side in (0, 1):
            total = tree_sum([ref[:, : 2 * width].astype(F32) for ref in pieces[side::2]])
            at = pl.ds(pl.multiple_of((2 * half + (chip % 2 ^ side)) * width, 128), width)
            qa_ref[:, at] = total[:, :width]
            va_ref[:, at] = total[:, width:]
        for k in range(n_chips):
            at = pl.ds(pl.multiple_of((chip ^ k) * tail, 128), tail)
            buffer[:, at] = pieces[k][:, 2 * width :].astype(F32)
        qb_ref[:, pl.ds(pl.multiple_of(half * Q_HALF, 128), Q_HALF)] = buffer[:, :Q_HALF]
        vb_ref[:, pl.ds(pl.multiple_of(half * KV_HALF, 128), KV_HALF)] = buffer[:, Q_HALF : Q_HALF + KV_HALF]


def join_rows(own_ref, far_ref, out_ref):
    core = lax.axis_index("ctx") % 2
    width = own_ref.shape[1]
    out_ref[:, pl.ds(pl.multiple_of(core * width, 128), width)] = own_ref[...]
    out_ref[:, pl.ds(pl.multiple_of((1 - core) * width, 128), width)] = far_ref[...]


def join_kv(own_ref, far_ref, dk_ref, dv_ref):
    core = lax.axis_index("ctx") % 2
    rows = far_ref.shape[0]
    for i, ref in enumerate((dk_ref, dv_ref)):
        columns = slice(i * KV_HALF, (i + 1) * KV_HALF)
        ref[:, pl.ds(pl.multiple_of(core * KV_HALF, 128), KV_HALF)] = own_ref[:rows, columns]
        ref[:, pl.ds(pl.multiple_of((1 - core) * KV_HALF, 128), KV_HALF)] = far_ref[:, columns]


def tree_sum(parts):
    while len(parts) > 1:
        parts = [a + b for a, b in zip(parts[::2], parts[1::2])]
    return parts[0]


def step(query, key, value, gradient, hidden, doc_lengths, querya, queryb, valuea, valueb):
    n_ctx, n_dp = lax.axis_size("ctx"), lax.axis_size("dp")
    n_chips = n_ctx // 2
    q, k, v, g, x = query[0], key[0], value[0], gradient[0], hidden[0]
    rows, width = x.shape[0], x.shape[1] // 2
    rank = querya.shape[0]
    chip_rows = 2 * rows
    lanes = GROUP * chip_rows
    sds = jax.ShapeDtypeStruct

    def swap(a):
        return lax.ppermute(a, "ctx", [(i, i ^ 1) for i in range(n_ctx)])

    def up(a, step):
        return lax.ppermute(a, "ctx", [(i, (i + 2 * step) % n_ctx) for i in range(n_ctx)])

    def down(a, step):
        return up(a, -step)

    def across(a, bit):
        return lax.ppermute(a, "dp", [(i, i ^ bit) for i in range(n_dp)])

    def along(a, bit):
        return lax.ppermute(a, "ctx", [(i, i ^ (2 * bit)) for i in range(n_ctx)])

    block = sds((rows + 2 * rank * rows // (2 * KV_HALF), 2 * KV_HALF), BF16)
    kv_own, kv_send = call(split_kv, [block] * 2, (k, v, x, querya, valuea))
    kv = [jnp.concatenate([kv_own, swap(kv_send)], axis=0)]
    if n_chips > 1:
        last = up(kv[0], n_chips - 1)
        for _ in range(1, n_chips - 1):
            kv.append(up(kv[-1], 1))
        kv.append(last)

    pack, hidden_far = call(
        split_rest,
        [sds((rows, 2 * Q_HALF), BF16), sds((rows, width), BF16)],
        (q, g, x, kv[0]),
        after=(3,),
    )
    pack, hidden_far = swap(pack), swap(hidden_far)
    hiddens = call(split_hidden, [sds((chip_rows, width // 2), BF16)] * 2, (x, hidden_far))
    hiddens = [hiddens[0], along(hiddens[1], 1)]

    tail = -(-(Q_HALF + KV_HALF) // (128 * n_chips)) * 128
    outs = (
        [sds((rows, Q_HALF), BF16)] * 2
        + [sds((chip_rows, 2 * KV_HALF), BF16)] * n_chips
        + [sds((rank, 3 * chip_rows + tail), BF16)] * n_chips
    )
    result = call(
        functools.partial(attention, n_chips, rank, tail),
        outs,
        (doc_lengths, q, g, pack, queryb, valueb, *kv),
        scratch=[
            pltpu.VMEM((n_chips, chip_rows, 2 * KV_HALF), BF16),
            pltpu.VMEM((n_chips, 2 * rank, chip_rows), BF16),
            pltpu.VMEM((n_chips, chip_rows, 2 * KV_HALF), BF16),
            pltpu.VMEM((n_chips, rank, chip_rows), F32),
            pltpu.VMEM((n_chips, chip_rows, lanes), F32),
            pltpu.VMEM((n_chips, chip_rows, lanes), F32),
            pltpu.VMEM((n_chips, 1, lanes), F32),
            pltpu.VMEM((chip_rows, lanes), BF16),
            pltpu.VMEM((chip_rows, lanes), BF16),
            pltpu.VMEM((CORE_HEADS, lanes, HEAD_WIDTH), BF16),
            pltpu.VMEM((CORE_HEADS, lanes, HEAD_WIDTH), BF16),
            pltpu.VMEM((HEAD_WIDTH, lanes), F32),
            pltpu.VMEM((rank, tail * n_chips), F32),
            pltpu.VMEM((rank, chip_rows), F32),
        ],
        flops=10 * CORE_HEADS * n_chips * chip_rows * lanes * HEAD_WIDTH,
        smem=(0,),
    )
    dq_own, dq_send = result[:2]
    dkv = result[2 : 2 + n_chips]
    messages = result[2 + n_chips :]

    own = [messages[0]] + [along(messages[bit], bit) for bit in range(1, n_chips)]
    far = [swap(a) for a in own]

    if n_chips > 1:
        last = down(dkv[n_chips - 1], n_chips - 1)
        total = dkv[n_chips - 2]
        for step in range(n_chips - 2, 0, -1):
            total = down(total, 1).astype(F32) + dkv[step - 1].astype(F32)
            total = (total if step > 1 else total + last.astype(F32)).astype(BF16)
    else:
        total = dkv[0]
    (query_grad,) = call(join_rows, [sds((rows, 2 * Q_HALF), BF16)], (dq_own, swap(dq_send)))
    dkv_far = swap(total[rows:])
    key_grad, value_grad = call(join_kv, [sds((rows, 2 * KV_HALF), BF16)] * 2, (total, dkv_far))

    (part,) = call(
        functools.partial(adapters, n_chips, rank),
        [sds((rank, width + tail), BF16)],
        (*own, *far, *hiddens, query_grad),
        after=(2 * n_chips + 2,),
    )
    got = [part] + [across(part, bit) for bit in range(1, n_dp)]
    part = tree_sum([a.astype(F32) for a in got]).astype(BF16)
    own = [part] + [along(part, bit) for bit in range(1, n_chips)]
    far = [swap(a) for a in own]
    qa_grad, qb_grad, va_grad, vb_grad = call(
        functools.partial(finish_adapters, n_chips, tail),
        [
            sds((rank, 2 * width), F32),
            sds((rank, 2 * Q_HALF), F32),
            sds((rank, 2 * width), F32),
            sds((rank, 2 * KV_HALF), F32),
        ],
        (*own, *far, key_grad, value_grad),
        scratch=[pltpu.VMEM((rank, tail * n_chips), F32)],
        after=(2 * n_chips, 2 * n_chips + 1),
    )
    return (
        query_grad[None],
        key_grad[None],
        value_grad[None],
        qa_grad,
        qb_grad,
        va_grad,
        vb_grad,
    )


def solution(mesh):
    tokens = P("dp", "ctx", None)
    return jax.shard_map(
        step,
        mesh=mesh,
        in_specs=(tokens,) * 5 + (P("dp", None),) + (P(),) * 4,
        out_specs=(tokens,) * 3 + (P(),) * 4,
        check_vma=False,
    )
```

profile of v0, /device:TPU:0, one launch (start us, length us, event | category | flops | bytes accessed | tf_op | source)
XLA Modules:
  0.0 91.6 jit_solution(10377184019953822937)
XLA Ops:
  0.6 2.8 %shard_map.153 = (bf16[136,512]{1,0:T(8,128)(2,1)}, bf16[136,512]{1,0:T(8,128)(2,1)}) custom-call(bf16[128,512]{1,0:T(8,128)(2,1)} %bitcast.16, bf16[128,512]{1,0:T(8,128)(2,1)} %bitcast.17, bf16[128,4096]{1,0:T(8,128)(2,1)} %bitcast.8, bf16[16,4096]{1,0:T(8,128)(2,1)} %qa_ref.1, bf16[16,4096]{1,0:T(8,128)(2,1)} %va_ref.1), custom_call_target="tpu_custom_call" | custom-call | bytes 1851392 | tf_op jit(solution)/shard_map/pallas_call | solution.py:53
  3.4 0.5 collective-permute-start
  3.9 0.9 %constant_dynamic-update-slice_fusion.1 = bf16[272,512]{1,0:T(8,128)(2,1)S(1)} fusion(bf16[136,512]{1,0:T(8,128)(2,1)} %get-tuple-element.29), kind=kLoop, calls=%fused_computation.4 | loop fusion | bytes 278528
  4.8 0.3 collective-permute-done
  5.2 3.0 %collective-permute-start.2 = (bf16[272,512]{1,0:T(8,128)(2,1)S(1)}, bf16[272,512]{1,0:T(8,128)(2,1)S(1)}, u32[]{:S(2)}, u32[]{:S(2)}) collective-permute-start(bf16[272,512]{1,0:T(8,128)(2,1)S(1)} %constant_dynamic-update-slice_fusion._.refs_6_), channel_id=1, source_target_pairs={{0,2},{1,3},{2,4},{3,5},{4,6},{5,7},{6,0},{7,1},{8,10},{9,11},{10,... | collective-permute-start | bytes 835592 | tf_op jit(solution)/shard_map/ppermute | solution.py:305
  8.1 2.6 %shard_map.154 = (bf16[128,2048]{1,0:T(8,128)(2,1)}, bf16[128,2048]{1,0:T(8,128)(2,1)}) custom-call(bf16[128,2048]{1,0:T(8,128)(2,1)} %bitcast.12, bf16[128,2048]{1,0:T(8,128)(2,1)} %bitcast.14, bf16[128,4096]{1,0:T(8,128)(2,1)} %bitcast.9, bf16[272,512]{1,0:T(8,128)(2,1)} %copy-done.1), custom_call_target="tpu_custom_call" | custom-call | bytes 3424256 | tf_op jit(solution)/shard_map/pallas_call | solution.py:53
  10.7 0.0 collective-permute-start.17
  10.7 0.5 collective-permute-start.1
  11.2 2.7 %collective-permute-start.4 = (bf16[272,512]{1,0:T(8,128)(2,1)}, bf16[272,512]{1,0:T(8,128)(2,1)S(1)}, u32[]{:S(2)}, u32[]{:S(2)}) collective-permute-start(bf16[272,512]{1,0:T(8,128)(2,1)} %copy-done.1), channel_id=1, source_target_pairs={{0,6},{1,7},{2,0},{3,1},{4,2},{5,3},{6,4},{7,5},{8,14},{9,15},{10,... | collective-permute-start | bytes 835592 | tf_op jit(solution)/shard_map/ppermute | solution.py:305
  13.9 3.7 %collective-permute-done.2.refs_7_ = bf16[272,512]{1,0:T(8,128)(2,1)S(1)} collective-permute-done((bf16[272,512]{1,0:T(8,128)(2,1)S(1)}, bf16[272,512]{1,0:T(8,128)(2,1)S(1)}, u32[]{:S(2)}, u32[]{:S(2)}) %collective-permute-start.2) | collective-permute-done | bytes 278560 | tf_op jit(solution)/shard_map/ppermute | solution.py:305
  17.7 0.0 collective-permute-start.3
  17.7 0.8 copy-done.2
  18.5 2.4 %shard_map.158 = (bf16[256,1024]{1,0:T(8,128)(2,1)}, bf16[256,1024]{1,0:T(8,128)(2,1)}) custom-call(bf16[128,4096]{1,0:T(8,128)(2,1)} %bitcast.10, bf16[128,2048]{1,0:T(8,128)(2,1)} %copy-done.2), custom_call_target="tpu_custom_call" | custom-call | bytes 2621440 | tf_op jit(solution)/shard_map/pallas_call | solution.py:53
  20.9 0.7 collective-permute-start.18
  21.6 2.1 %collective-permute-done.4.refs_9_ = bf16[272,512]{1,0:T(8,128)(2,1)S(1)} collective-permute-done((bf16[272,512]{1,0:T(8,128)(2,1)}, bf16[272,512]{1,0:T(8,128)(2,1)S(1)}, u32[]{:S(2)}, u32[]{:S(2)}) %collective-permute-start.4) | collective-permute-done | bytes 278560 | tf_op jit(solution)/shard_map/ppermute | solution.py:305
  23.7 8.0 %collective-permute-done.3.refs_8_ = bf16[272,512]{1,0:T(8,128)(2,1)S(1)} collective-permute-done((bf16[272,512]{1,0:T(8,128)(2,1)S(1)}, bf16[272,512]{1,0:T(8,128)(2,1)S(1)}, u32[]{:S(2)}, u32[]{:S(2)}) %collective-permute-start.3) | collective-permute-done | bytes 278560 | tf_op jit(solution)/shard_map/ppermute | solution.py:305
  31.8 0.7 copy-done.27
  32.5 6.2 %shard_map.155 = (bf16[128,1024]{1,0:T(8,128)(2,1)}, bf16[128,1024]{1,0:T(8,128)(2,1)}, bf16[256,512]{1,0:T(8,128)(2,1)}, bf16[256,512]{1,0:T(8,128)(2,1)}, bf16...) custom-call(s32[1,16]{1,0:T(1,128)} %refs_0_.1, ...), custom_call_target="tpu_custom_call" | custom-call | flops 2684354560 | bytes 4489280 | tf_op jit(solution)/shard_map/pallas_call | solution.py:53
  38.7 0.1 collective-permute-start.5
  38.7 6.7 %collective-permute-start.6 = (bf16[256,512]{1,0:T(8,128)(2,1)}, bf16[256,512]{1,0:T(8,128)(2,1)S(1)}, u32[]{:S(2)}, u32[]{:S(2)}) collective-permute-start(bf16[256,512]{1,0:T(8,128)(2,1)} %get-tuple-element.34), channel_id=1, source_target_pairs={{0,6},{1,7},{2,0},{3,1},{4,2},{5,3},{6,4},{7,5},{8,14},{9,15},{10,... | collective-permute-start | bytes 786440 | tf_op jit(solution)/shard_map/ppermute | solution.py:305
  45.4 0.0 collective-permute-start.10
  45.4 0.6 collective-permute-start.11
  46.1 7.1 %collective-permute-done.10.refs_1_ = bf16[16,1152]{1,0:T(8,128)(2,1)S(1)} collective-permute-done((bf16[16,1152]{1,0:T(8,128)(2,1)}, bf16[16,1152]{1,0:T(8,128)(2,1)S(1)}, u32[]{:S(2)}, u32[]{:S(2)}) %collective-permute-start.10) | collective-permute-done | bytes 36896 | tf_op jit(solution)/shard_map/ppermute | solution.py:314
  53.2 0.1 collective-permute-start.12
  53.3 0.6 collective-permute-done.11.refs_2_
  53.8 5.4 %collective-permute-done.12.refs_3_ = bf16[16,1152]{1,0:T(8,128)(2,1)S(1)} collective-permute-done((bf16[16,1152]{1,0:T(8,128)(2,1)}, bf16[16,1152]{1,0:T(8,128)(2,1)S(1)}, u32[]{:S(2)}, u32[]{:S(2)}) %collective-permute-start.12) | collective-permute-done | bytes 36896 | tf_op jit(solution)/shard_map/ppermute | solution.py:314
  59.2 0.0 collective-permute-start.14
  59.2 0.0 collective-permute-done.13.refs_4_
  59.2 0.5 collective-permute-start.15
  59.7 0.0 collective-permute-done.5.far_ref
  59.7 0.1 collective-permute-start.16
  59.8 0.6 copy-done.8
  60.4 1.9 %shard_map.156.refs_10_ = bf16[128,2048]{1,0:T(8,128)(2,1)} custom-call(bf16[128,1024]{1,0:T(8,128)(2,1)} %get-tuple-element.32.own_ref, bf16[128,1024]{1,0:T(8,128)(2,1)} %copy-done.8), custom_call_target="tpu_custom_call" | custom-call | bytes 1048576 | tf_op jit(solution)/shard_map/pallas_call | solution.py:53
  62.3 0.0 collective-permute-done.14.refs_5_
  62.3 0.0 copy-start.21
  62.4 1.0 %collective-permute-start.8 = (bf16[256,512]{1,0:T(8,128)(2,1)S(1)}, bf16[256,512]{1,0:T(8,128)(2,1)S(1)}, u32[]{:S(2)}, u32[]{:S(2)}) collective-permute-start(bf16[256,512]{1,0:T(8,128)(2,1)S(1)} %copy-done.28), channel_id=1, source_target_pairs={{0,2},{1,3},{2,4},{3,5},{4,6},{5,7},{6,0},{7,1},{8,10},{9,11},{10,... | collective-permute-start | bytes 786440 | tf_op jit(solution)/shard_map/ppermute | solution.py:305
  63.4 0.6 copy-done.22
  64.0 0.0 copy-done.23
  64.0 0.2 copy-done.3
  64.2 2.4 %shard_map.159 = bf16[16,2432]{1,0:T(8,128)(2,1)} custom-call(bf16[16,1152]{1,0:T(8,128)(2,1)} %get-tuple-element.40.refs_0_, bf16[16,1152]{1,0:T(8,128)(2,1)} %copy-done.17, bf16[16,1152]{1,0:T(8,128)(2,1)} %copy-done.18, bf16[16,1152]{1,0:T(8,128)(2,1)} %copy-done.19, bf16[16,1152]{1,0:T(8,128)(2,1)} %copy-done.20, bf16[16,1152]{1,0:T(8,128)(2,1)} %copy-done.21, ...), custom_call_target="tpu_custom_call" | custom-call | bytes 1945600 | tf_op jit(solution)/shard_map/pallas_call | solution.py:53
  66.6 4.7 %collective-permute-start.21 = (bf16[16,2432]{1,0:T(8,128)(2,1)}, bf16[16,2432]{1,0:T(8,128)(2,1)S(1)}, u32[]{:S(2)}, u32[]{:S(2)}) collective-permute-start(bf16[16,2432]{1,0:T(8,128)(2,1)} %shard_map.159), channel_id=1, source_target_pairs={{0,24},{8,16},{16,8},{24,0},{1,25},{9,17},{17,9},{25,1},{2,26},{10... | collective-permute-start | bytes 233480 | tf_op jit(solution)/shard_map/ppermute | solution.py:311
  71.3 0.5 collective-permute-start.20
  71.8 0.1 collective-permute-start.19
  71.9 0.1 add_convert_fusion.1
  72.0 3.0 %collective-permute-start.7 = (bf16[256,512]{1,0:T(8,128)(2,1)S(1)}, bf16[256,512]{1,0:T(8,128)(2,1)S(1)}, u32[]{:S(2)}, u32[]{:S(2)}) collective-permute-start(bf16[256,512]{1,0:T(8,128)(2,1)S(1)} %add_convert_fusion.1), channel_id=1, source_target_pairs={{0,6},{1,7},{2,0},{3,1},{4,2},{5,3},{6,4},{7,5},{8,14},{9,15},{10,... | collective-permute-start | bytes 786440 | tf_op jit(solution)/shard_map/ppermute | solution.py:305
  74.9 1.0 %collective-permute-done.20 = bf16[16,2432]{1,0:T(8,128)(2,1)S(1)} collective-permute-done((bf16[16,2432]{1,0:T(8,128)(2,1)}, bf16[16,2432]{1,0:T(8,128)(2,1)S(1)}, u32[]{:S(2)}, u32[]{:S(2)}) %collective-permute-start.20) | collective-permute-done | bytes 77856 | tf_op jit(solution)/shard_map/ppermute | solution.py:311
  75.9 0.5 collective-permute-done.19
  76.5 3.0 %collective-permute-start.24 = (bf16[16,2432]{1,0:T(8,128)(2,1)S(1)}, bf16[16,2432]{1,0:T(8,128)(2,1)S(1)}, u32[]{:S(2)}, u32[]{:S(2)}) collective-permute-start(bf16[16,2432]{1,0:T(8,128)(2,1)S(1)} %add_convert_fusion.2.refs_0_), channel_id=1, source_target_pairs={{0,6},{1,7},{2,4},{3,5},{4,2},{5,3},{6,0},{7,1},{8,14},{9,15},{10,... | collective-permute-start | bytes 233480 | tf_op jit(solution)/shard_map/ppermute | solution.py:314
  79.5 1.5 %collective-permute-start.22 = (bf16[16,2432]{1,0:T(8,128)(2,1)S(1)}, bf16[16,2432]{1,0:T(8,128)(2,1)S(1)}, u32[]{:S(2)}, u32[]{:S(2)}) collective-permute-start(bf16[16,2432]{1,0:T(8,128)(2,1)S(1)} %add_convert_fusion.2.refs_0_), channel_id=1, source_target_pairs={{0,2},{1,3},{2,0},{3,1},{4,6},{5,7},{6,4},{7,5},{8,10},{9,11},{10,... | collective-permute-start | bytes 233480 | tf_op jit(solution)/shard_map/ppermute | solution.py:314
  81.0 0.4 collective-permute-done.7
  81.4 0.1 add_convert_fusion.own_ref
  81.5 0.0 copy-start
  81.5 0.1 collective-permute-start.9
  81.6 0.5 collective-permute-start.25
  82.1 1.5 %collective-permute-done.24.refs_3_ = bf16[16,2432]{1,0:T(8,128)(2,1)S(1)} collective-permute-done((bf16[16,2432]{1,0:T(8,128)(2,1)S(1)}, bf16[16,2432]{1,0:T(8,128)(2,1)S(1)}, u32[]{:S(2)}, u32[]{:S(2)}) %collective-permute-start.24) | collective-permute-done | bytes 77856 | tf_op jit(solution)/shard_map/ppermute | solution.py:314
  83.6 2.3 %collective-permute-done.23.refs_2_ = bf16[16,2432]{1,0:T(8,128)(2,1)S(1)} collective-permute-done((bf16[16,2432]{1,0:T(8,128)(2,1)S(1)}, bf16[16,2432]{1,0:T(8,128)(2,1)S(1)}, u32[]{:S(2)}, u32[]{:S(2)}) %collective-permute-start.23) | collective-permute-done | bytes 77856 | tf_op jit(solution)/shard_map/ppermute | solution.py:314
  85.9 0.5 collective-permute-start.26
  86.4 0.7 copy-done.9
  87.1 1.7 %shard_map.157 = (bf16[128,512]{1,0:T(8,128)(2,1)}, bf16[128,512]{1,0:T(8,128)(2,1)}) custom-call(bf16[256,512]{1,0:T(8,128)(2,1)} %copy-done, bf16[128,512]{1,0:T(8,128)(2,1)} %copy-done.9), custom_call_target="tpu_custom_call" | custom-call | bytes 655360 | tf_op jit(solution)/shard_map/pallas_call | solution.py:53
  88.9 0.5 copy-done.13
  89.4 0.0 copy-done.14
  89.5 0.0 copy-done.15
  89.5 0.0 copy-done.16
  89.5 2.1 %shard_map.160 = (f32[16,4096]{1,0:T(8,128)}, f32[16,2048]{1,0:T(8,128)}, f32[16,4096]{1,0:T(8,128)}, f32[16,512]{1,0:T(8,128)}) custom-call(bf16[16,2432]{1,0:T(8,128)(2,1)} %copy-done.4, bf16[16,2432]{1,0:T(8,128)(2,1)} %copy-done.12, bf16[16,2432]{1,0:T(8,128)(2,1)} %copy-done.11, bf16[16,2432]{1,0:T(8,128)(2,1)} %copy-done.10, ...), custom_call_target="tpu_custom_call" | custom-call | bytes 1572864 | tf_op jit(solution)/shard_map/pallas_call | solution.py:53
  (66 shorter events, 0.2 us)
Async XLA Ops:
  3.4 1.7 %collective-permute-start = (bf16[136,512]{1,0:T(8,128)(2,1)}, bf16[136,512]{1,0:T(8,128)(2,1)S(1)}, u32[]{:S(2)}, u32[]{:S(2)}) collective-permute-start(bf16[136,512]{1,0:T(8,128)(2,1)} %get-tuple-element.30), channel_id=1, source_target_pairs={{0,1},{1,0},{2,3},{3,2},{4,5},{5,4},{6,7},{7,6},{8,9},{9,8},{10,11... | collective-permute-start | bytes 417800 | tf_op jit(solution)/shard_map/ppermute | solution.py:302
  5.1 3.0 %copy-start.1 = (bf16[272,512]{1,0:T(8,128)(2,1)}, bf16[272,512]{1,0:T(8,128)(2,1)S(1)}, u32[]{:S(2)}) copy-start(bf16[272,512]{1,0:T(8,128)(2,1)S(1)} %constant_dynamic-update-slice_fusion._.refs_6_) | copy-start | bytes 835588
  5.2 12.5 %collective-permute-start.2 = (bf16[272,512]{1,0:T(8,128)(2,1)S(1)}, bf16[272,512]{1,0:T(8,128)(2,1)S(1)}, u32[]{:S(2)}, u32[]{:S(2)}) collective-permute-start(bf16[272,512]{1,0:T(8,128)(2,1)S(1)} %constant_dynamic-update-slice_fusion._.refs_6_), channel_id=1, source_target_pairs={{0,2},{1,3},{2,4},{3,5},{4,6},{5,7},{6,0},{7,1},{8,10},{9,11},{10,... | collective-permute-start | bytes 835592 | tf_op jit(solution)/shard_map/ppermute | solution.py:305
  10.7 6.9 %collective-permute-start.17 = (bf16[128,2048]{1,0:T(8,128)(2,1)}, bf16[128,2048]{1,0:T(8,128)(2,1)S(1)}, u32[]{:S(2)}, u32[]{:S(2)}) collective-permute-start(bf16[128,2048]{1,0:T(8,128)(2,1)} %get-tuple-element.44), channel_id=1, source_target_pairs={{0,1},{1,0},{2,3},{3,2},{4,5},{5,4},{6,7},{7,6},{8,9},{9,8},{10,11... | collective-permute-start | bytes 1572872 | tf_op jit(solution)/shard_map/ppermute | solution.py:302
  10.7 13.0 %collective-permute-start.1 = (bf16[128,2048]{1,0:T(8,128)(2,1)}, bf16[128,2048]{1,0:T(8,128)(2,1)S(1)}, u32[]{:S(2)}, u32[]{:S(2)}) collective-permute-start(bf16[128,2048]{1,0:T(8,128)(2,1)} %get-tuple-element.31), channel_id=1, source_target_pairs={{0,1},{1,0},{2,3},{3,2},{4,5},{5,4},{6,7},{7,6},{8,9},{9,8},{10,11... | collective-permute-start | bytes 1572872 | tf_op jit(solution)/shard_map/ppermute | solution.py:302
  11.2 12.5 %collective-permute-start.4 = (bf16[272,512]{1,0:T(8,128)(2,1)}, bf16[272,512]{1,0:T(8,128)(2,1)S(1)}, u32[]{:S(2)}, u32[]{:S(2)}) collective-permute-start(bf16[272,512]{1,0:T(8,128)(2,1)} %copy-done.1), channel_id=1, source_target_pairs={{0,6},{1,7},{2,0},{3,1},{4,2},{5,3},{6,4},{7,5},{8,14},{9,15},{10,... | collective-permute-start | bytes 835592 | tf_op jit(solution)/shard_map/ppermute | solution.py:305
  17.7 14.1 %copy-start.25 = (bf16[272,512]{1,0:T(8,128)(2,1)}, bf16[272,512]{1,0:T(8,128)(2,1)S(1)}, u32[]{:S(2)}) copy-start(bf16[272,512]{1,0:T(8,128)(2,1)S(1)} %collective-permute-done.2.refs_7_) | copy-start | bytes 835588
  17.7 14.1 %collective-permute-start.3 = (bf16[272,512]{1,0:T(8,128)(2,1)S(1)}, bf16[272,512]{1,0:T(8,128)(2,1)S(1)}, u32[]{:S(2)}, u32[]{:S(2)}) collective-permute-start(bf16[272,512]{1,0:T(8,128)(2,1)S(1)} %collective-permute-done.2.refs_7_), channel_id=1, source_target_pairs={{0,2},{1,3},{2,4},{3,5},{4,6},{5,7},{6,0},{7,1},{8,10},{9,11},{10,... | collective-permute-start | bytes 835592 | tf_op jit(solution)/shard_map/ppermute | solution.py:305
  17.7 0.8 copy-start.2
  20.9 42.4 %collective-permute-start.18 = (bf16[256,1024]{1,0:T(8,128)(2,1)}, bf16[256,1024]{1,0:T(8,128)(2,1)S(1)}, u32[]{:S(2)}, u32[]{:S(2)}) collective-permute-start(bf16[256,1024]{1,0:T(8,128)(2,1)} %get-tuple-element.46), channel_id=1, source_target_pairs={{0,2},{1,3},{2,0},{3,1},{4,6},{5,7},{6,4},{7,5},{8,10},{9,11},{10,... | collective-permute-start | bytes 1572872 | tf_op jit(solution)/shard_map/ppermute | solution.py:314
  23.7 8.0 %copy-start.26 = (bf16[272,512]{1,0:T(8,128)(2,1)}, bf16[272,512]{1,0:T(8,128)(2,1)S(1)}, u32[]{:S(2)}) copy-start(bf16[272,512]{1,0:T(8,128)(2,1)S(1)} %collective-permute-done.4.refs_9_) | copy-start | bytes 835588
  23.7 8.0 %copy-start.24 = (bf16[128,2048]{1,0:T(8,128)(2,1)}, bf16[128,2048]{1,0:T(8,128)(2,1)S(1)}, u32[]{:S(2)}) copy-start(bf16[128,2048]{1,0:T(8,128)(2,1)S(1)} %collective-permute-done.1.refs_3_) | copy-start | bytes 1572868
  31.8 0.7 copy-start.27
  38.7 21.0 %collective-permute-start.5 = (bf16[128,1024]{1,0:T(8,128)(2,1)}, bf16[128,1024]{1,0:T(8,128)(2,1)S(1)}, u32[]{:S(2)}, u32[]{:S(2)}) collective-permute-start(bf16[128,1024]{1,0:T(8,128)(2,1)} %get-tuple-element.33), channel_id=1, source_target_pairs={{0,1},{1,0},{2,3},{3,2},{4,5},{5,4},{6,7},{7,6},{8,9},{9,8},{10,11... | collective-permute-start | bytes 786440 | tf_op jit(solution)/shard_map/ppermute | solution.py:302
  38.7 33.2 %collective-permute-start.6 = (bf16[256,512]{1,0:T(8,128)(2,1)}, bf16[256,512]{1,0:T(8,128)(2,1)S(1)}, u32[]{:S(2)}, u32[]{:S(2)}) collective-permute-start(bf16[256,512]{1,0:T(8,128)(2,1)} %get-tuple-element.34), channel_id=1, source_target_pairs={{0,6},{1,7},{2,0},{3,1},{4,2},{5,3},{6,4},{7,5},{8,14},{9,15},{10,... | collective-permute-start | bytes 786440 | tf_op jit(solution)/shard_map/ppermute | solution.py:305
  45.4 7.7 %collective-permute-start.10 = (bf16[16,1152]{1,0:T(8,128)(2,1)}, bf16[16,1152]{1,0:T(8,128)(2,1)S(1)}, u32[]{:S(2)}, u32[]{:S(2)}) collective-permute-start(bf16[16,1152]{1,0:T(8,128)(2,1)} %get-tuple-element.41), channel_id=1, source_target_pairs={{0,2},{1,3},{2,0},{3,1},{4,6},{5,7},{6,4},{7,5},{8,10},{9,11},{10,... | collective-permute-start | bytes 110600 | tf_op jit(solution)/shard_map/ppermute | solution.py:314
  45.4 8.4 %collective-permute-start.11 = (bf16[16,1152]{1,0:T(8,128)(2,1)}, bf16[16,1152]{1,0:T(8,128)(2,1)S(1)}, u32[]{:S(2)}, u32[]{:S(2)}) collective-permute-start(bf16[16,1152]{1,0:T(8,128)(2,1)} %get-tuple-element.42), channel_id=1, source_target_pairs={{0,4},{1,5},{2,6},{3,7},{4,0},{5,1},{6,2},{7,3},{8,12},{9,13},{10,... | collective-permute-start | bytes 110600 | tf_op jit(solution)/shard_map/ppermute | solution.py:314
  53.2 9.1 %copy-start.17 = (bf16[16,1152]{1,0:T(8,128)(2,1)}, bf16[16,1152]{1,0:T(8,128)(2,1)S(1)}, u32[]{:S(2)}) copy-start(bf16[16,1152]{1,0:T(8,128)(2,1)S(1)} %collective-permute-done.10.refs_1_) | copy-start | bytes 110596
  53.2 6.0 %collective-permute-start.12 = (bf16[16,1152]{1,0:T(8,128)(2,1)}, bf16[16,1152]{1,0:T(8,128)(2,1)S(1)}, u32[]{:S(2)}, u32[]{:S(2)}) collective-permute-start(bf16[16,1152]{1,0:T(8,128)(2,1)} %get-tuple-element.43), channel_id=1, source_target_pairs={{0,6},{1,7},{2,4},{3,5},{4,2},{5,3},{6,0},{7,1},{8,14},{9,15},{10,... | collective-permute-start | bytes 110600 | tf_op jit(solution)/shard_map/ppermute | solution.py:314
  53.8 8.5 %copy-start.18 = (bf16[16,1152]{1,0:T(8,128)(2,1)}, bf16[16,1152]{1,0:T(8,128)(2,1)S(1)}, u32[]{:S(2)}) copy-start(bf16[16,1152]{1,0:T(8,128)(2,1)S(1)} %collective-permute-done.11.refs_2_) | copy-start | bytes 110596
  53.8 5.4 %collective-permute-start.13 = (bf16[16,1152]{1,0:T(8,128)(2,1)}, bf16[16,1152]{1,0:T(8,128)(2,1)S(1)}, u32[]{:S(2)}, u32[]{:S(2)}) collective-permute-start(bf16[16,1152]{1,0:T(8,128)(2,1)} %get-tuple-element.40.refs_0_), channel_id=1, source_target_pairs={{0,1},{1,0},{2,3},{3,2},{4,5},{5,4},{6,7},{7,6},{8,9},{9,8},{10,11... | collective-permute-start | bytes 110600 | tf_op jit(solution)/shard_map/ppermute | solution.py:302
  59.2 3.1 %copy-start.19 = (bf16[16,1152]{1,0:T(8,128)(2,1)}, bf16[16,1152]{1,0:T(8,128)(2,1)S(1)}, u32[]{:S(2)}) copy-start(bf16[16,1152]{1,0:T(8,128)(2,1)S(1)} %collective-permute-done.12.refs_3_) | copy-start | bytes 110596
  59.2 3.2 %collective-permute-start.14 = (bf16[16,1152]{1,0:T(8,128)(2,1)S(1)}, bf16[16,1152]{1,0:T(8,128)(2,1)S(1)}, u32[]{:S(2)}, u32[]{:S(2)}) collective-permute-start(bf16[16,1152]{1,0:T(8,128)(2,1)S(1)} %collective-permute-done.10.refs_1_), channel_id=1, source_target_pairs={{0,1},{1,0},{2,3},{3,2},{4,5},{5,4},{6,7},{7,6},{8,9},{9,8},{10,11... | collective-permute-start | bytes 110600 | tf_op jit(solution)/shard_map/ppermute | solution.py:302
  59.2 3.1 %copy-start.20 = (bf16[16,1152]{1,0:T(8,128)(2,1)}, bf16[16,1152]{1,0:T(8,128)(2,1)S(1)}, u32[]{:S(2)}) copy-start(bf16[16,1152]{1,0:T(8,128)(2,1)S(1)} %collective-permute-done.13.refs_4_) | copy-start | bytes 110596
  59.2 4.1 %collective-permute-start.15 = (bf16[16,1152]{1,0:T(8,128)(2,1)S(1)}, bf16[16,1152]{1,0:T(8,128)(2,1)S(1)}, u32[]{:S(2)}, u32[]{:S(2)}) collective-permute-start(bf16[16,1152]{1,0:T(8,128)(2,1)S(1)} %collective-permute-done.11.refs_2_), channel_id=1, source_target_pairs={{0,1},{1,0},{2,3},{3,2},{4,5},{5,4},{6,7},{7,6},{8,9},{9,8},{10,11... | collective-permute-start | bytes 110600 | tf_op jit(solution)/shard_map/ppermute | solution.py:302
  59.7 0.7 copy-start.8
  59.7 3.6 %collective-permute-start.16 = (bf16[16,1152]{1,0:T(8,128)(2,1)S(1)}, bf16[16,1152]{1,0:T(8,128)(2,1)S(1)}, u32[]{:S(2)}, u32[]{:S(2)}) collective-permute-start(bf16[16,1152]{1,0:T(8,128)(2,1)S(1)} %collective-permute-done.12.refs_3_), channel_id=1, source_target_pairs={{0,1},{1,0},{2,3},{3,2},{4,5},{5,4},{6,7},{7,6},{8,9},{9,8},{10,11... | collective-permute-start | bytes 110600 | tf_op jit(solution)/shard_map/ppermute | solution.py:302
  60.4 2.0 %copy-start.28 = (bf16[256,512]{1,0:T(8,128)(2,1)S(1)}, bf16[256,512]{1,0:T(8,128)(2,1)}, u32[]{:S(2)}) copy-start(bf16[256,512]{1,0:T(8,128)(2,1)} %get-tuple-element.37) | copy-start | bytes 786436
  62.3 1.0 %copy-start.21 = (bf16[16,1152]{1,0:T(8,128)(2,1)}, bf16[16,1152]{1,0:T(8,128)(2,1)S(1)}, u32[]{:S(2)}) copy-start(bf16[16,1152]{1,0:T(8,128)(2,1)S(1)} %collective-permute-done.14.refs_5_) | copy-start | bytes 110596
  62.4 18.6 %collective-permute-start.8 = (bf16[256,512]{1,0:T(8,128)(2,1)S(1)}, bf16[256,512]{1,0:T(8,128)(2,1)S(1)}, u32[]{:S(2)}, u32[]{:S(2)}) collective-permute-start(bf16[256,512]{1,0:T(8,128)(2,1)S(1)} %copy-done.28), channel_id=1, source_target_pairs={{0,2},{1,3},{2,4},{3,5},{4,6},{5,7},{6,0},{7,1},{8,10},{9,11},{10,... | collective-permute-start | bytes 786440 | tf_op jit(solution)/shard_map/ppermute | solution.py:305
  63.3 0.6 copy-start.22
  63.3 0.6 copy-start.23
  63.4 0.8 copy-start.3
  64.2 7.7 %copy-start.6 = (bf16[256,512]{1,0:T(8,128)(2,1)S(1)}, bf16[256,512]{1,0:T(8,128)(2,1)}, u32[]{:S(2)}) copy-start(bf16[256,512]{1,0:T(8,128)(2,1)} %get-tuple-element.35) | copy-start | bytes 786436
  66.6 8.3 %collective-permute-start.21 = (bf16[16,2432]{1,0:T(8,128)(2,1)}, bf16[16,2432]{1,0:T(8,128)(2,1)S(1)}, u32[]{:S(2)}, u32[]{:S(2)}) collective-permute-start(bf16[16,2432]{1,0:T(8,128)(2,1)} %shard_map.159), channel_id=1, source_target_pairs={{0,24},{8,16},{16,8},{24,0},{1,25},{9,17},{17,9},{25,1},{2,26},{10... | collective-permute-start | bytes 233480 | tf_op jit(solution)/shard_map/ppermute | solution.py:311
  71.3 4.6 %collective-permute-start.20 = (bf16[16,2432]{1,0:T(8,128)(2,1)}, bf16[16,2432]{1,0:T(8,128)(2,1)S(1)}, u32[]{:S(2)}, u32[]{:S(2)}) collective-permute-start(bf16[16,2432]{1,0:T(8,128)(2,1)} %shard_map.159), channel_id=1, source_target_pairs={{0,16},{8,24},{16,0},{24,8},{1,17},{9,25},{17,1},{25,9},{2,18},{10... | collective-permute-start | bytes 233480 | tf_op jit(solution)/shard_map/ppermute | solution.py:311
  71.8 4.6 %collective-permute-start.19 = (bf16[16,2432]{1,0:T(8,128)(2,1)}, bf16[16,2432]{1,0:T(8,128)(2,1)S(1)}, u32[]{:S(2)}, u32[]{:S(2)}) collective-permute-start(bf16[16,2432]{1,0:T(8,128)(2,1)} %shard_map.159), channel_id=1, source_target_pairs={{0,8},{8,0},{16,24},{24,16},{1,9},{9,1},{17,25},{25,17},{2,10},{10... | collective-permute-start | bytes 233480 | tf_op jit(solution)/shard_map/ppermute | solution.py:311
  71.9 4.5 %copy-start.5 = (bf16[16,2432]{1,0:T(8,128)(2,1)S(1)}, bf16[16,2432]{1,0:T(8,128)(2,1)}, u32[]{:S(2)}) copy-start(bf16[16,2432]{1,0:T(8,128)(2,1)} %shard_map.159) | copy-start | bytes 233476
  72.0 9.4 %copy-start.7 = (bf16[256,512]{1,0:T(8,128)(2,1)S(1)}, bf16[256,512]{1,0:T(8,128)(2,1)}, u32[]{:S(2)}) copy-start(bf16[256,512]{1,0:T(8,128)(2,1)} %get-tuple-element.36) | copy-start | bytes 786436
  72.0 9.4 %collective-permute-start.7 = (bf16[256,512]{1,0:T(8,128)(2,1)S(1)}, bf16[256,512]{1,0:T(8,128)(2,1)S(1)}, u32[]{:S(2)}, u32[]{:S(2)}) collective-permute-start(bf16[256,512]{1,0:T(8,128)(2,1)S(1)} %add_convert_fusion.1), channel_id=1, source_target_pairs={{0,6},{1,7},{2,0},{3,1},{4,2},{5,3},{6,4},{7,5},{8,14},{9,15},{10,... | collective-permute-start | bytes 786440 | tf_op jit(solution)/shard_map/ppermute | solution.py:305
  76.5 5.1 %copy-start.4 = (bf16[16,2432]{1,0:T(8,128)(2,1)}, bf16[16,2432]{1,0:T(8,128)(2,1)S(1)}, u32[]{:S(2)}) copy-start(bf16[16,2432]{1,0:T(8,128)(2,1)S(1)} %add_convert_fusion.2.refs_0_) | copy-start | bytes 233476
  76.5 7.1 %collective-permute-start.24 = (bf16[16,2432]{1,0:T(8,128)(2,1)S(1)}, bf16[16,2432]{1,0:T(8,128)(2,1)S(1)}, u32[]{:S(2)}, u32[]{:S(2)}) collective-permute-start(bf16[16,2432]{1,0:T(8,128)(2,1)S(1)} %add_convert_fusion.2.refs_0_), channel_id=1, source_target_pairs={{0,6},{1,7},{2,4},{3,5},{4,2},{5,3},{6,0},{7,1},{8,14},{9,15},{10,... | collective-permute-start | bytes 233480 | tf_op jit(solution)/shard_map/ppermute | solution.py:314
  79.5 6.4 %collective-permute-start.23 = (bf16[16,2432]{1,0:T(8,128)(2,1)S(1)}, bf16[16,2432]{1,0:T(8,128)(2,1)S(1)}, u32[]{:S(2)}, u32[]{:S(2)}) collective-permute-start(bf16[16,2432]{1,0:T(8,128)(2,1)S(1)} %add_convert_fusion.2.refs_0_), channel_id=1, source_target_pairs={{0,4},{1,5},{2,6},{3,7},{4,0},{5,1},{6,2},{7,3},{8,12},{9,13},{10,... | collective-permute-start | bytes 233480 | tf_op jit(solution)/shard_map/ppermute | solution.py:314
  79.5 6.4 %collective-permute-start.22 = (bf16[16,2432]{1,0:T(8,128)(2,1)S(1)}, bf16[16,2432]{1,0:T(8,128)(2,1)S(1)}, u32[]{:S(2)}, u32[]{:S(2)}) collective-permute-start(bf16[16,2432]{1,0:T(8,128)(2,1)S(1)} %add_convert_fusion.2.refs_0_), channel_id=1, source_target_pairs={{0,2},{1,3},{2,0},{3,1},{4,6},{5,7},{6,4},{7,5},{8,10},{9,11},{10,... | collective-permute-start | bytes 233480 | tf_op jit(solution)/shard_map/ppermute | solution.py:314
  81.5 5.0 %copy-start = (bf16[256,512]{1,0:T(8,128)(2,1)}, bf16[256,512]{1,0:T(8,128)(2,1)S(1)}, u32[]{:S(2)}) copy-start(bf16[256,512]{1,0:T(8,128)(2,1)S(1)} %add_convert_fusion.own_ref) | copy-start | bytes 786436
  81.5 4.9 %collective-permute-start.9 = (bf16[128,512]{1,0:T(8,128)(2,1)S(1)}, bf16[128,512]{1,0:T(8,128)(2,1)S(1)}, u32[]{:S(2)}, u32[]{:S(2)}) collective-permute-start(bf16[128,512]{1,0:T(8,128)(2,1)S(1)} %slice.4), channel_id=1, source_target_pairs={{0,1},{1,0},{2,3},{3,2},{4,5},{5,4},{6,7},{7,6},{8,9},{9,8},{10,11... | collective-permute-start | bytes 393224 | tf_op jit(solution)/shard_map/ppermute | solution.py:302
  81.6 7.2 %collective-permute-start.25 = (bf16[16,2432]{1,0:T(8,128)(2,1)S(1)}, bf16[16,2432]{1,0:T(8,128)(2,1)S(1)}, u32[]{:S(2)}, u32[]{:S(2)}) collective-permute-start(bf16[16,2432]{1,0:T(8,128)(2,1)S(1)} %add_convert_fusion.2.refs_0_), channel_id=1, source_target_pairs={{0,1},{1,0},{2,3},{3,2},{4,5},{5,4},{6,7},{7,6},{8,9},{9,8},{10,11... | collective-permute-start | bytes 233480 | tf_op jit(solution)/shard_map/ppermute | solution.py:302
  83.6 5.3 %copy-start.10 = (bf16[16,2432]{1,0:T(8,128)(2,1)}, bf16[16,2432]{1,0:T(8,128)(2,1)S(1)}, u32[]{:S(2)}) copy-start(bf16[16,2432]{1,0:T(8,128)(2,1)S(1)} %collective-permute-done.24.refs_3_) | copy-start | bytes 233476
  83.6 5.2 %collective-permute-start.28 = (bf16[16,2432]{1,0:T(8,128)(2,1)S(1)}, bf16[16,2432]{1,0:T(8,128)(2,1)S(1)}, u32[]{:S(2)}, u32[]{:S(2)}) collective-permute-start(bf16[16,2432]{1,0:T(8,128)(2,1)S(1)} %collective-permute-done.24.refs_3_), channel_id=1, source_target_pairs={{0,1},{1,0},{2,3},{3,2},{4,5},{5,4},{6,7},{7,6},{8,9},{9,8},{10,11... | collective-permute-start | bytes 233480 | tf_op jit(solution)/shard_map/ppermute | solution.py:302
  85.9 3.0 %copy-start.11 = (bf16[16,2432]{1,0:T(8,128)(2,1)}, bf16[16,2432]{1,0:T(8,128)(2,1)S(1)}, u32[]{:S(2)}) copy-start(bf16[16,2432]{1,0:T(8,128)(2,1)S(1)} %collective-permute-done.23.refs_2_) | copy-start | bytes 233476
  85.9 2.9 %collective-permute-start.27 = (bf16[16,2432]{1,0:T(8,128)(2,1)S(1)}, bf16[16,2432]{1,0:T(8,128)(2,1)S(1)}, u32[]{:S(2)}, u32[]{:S(2)}) collective-permute-start(bf16[16,2432]{1,0:T(8,128)(2,1)S(1)} %collective-permute-done.23.refs_2_), channel_id=1, source_target_pairs={{0,1},{1,0},{2,3},{3,2},{4,5},{5,4},{6,7},{7,6},{8,9},{9,8},{10,11... | collective-permute-start | bytes 233480 | tf_op jit(solution)/shard_map/ppermute | solution.py:302
  85.9 3.0 %copy-start.12 = (bf16[16,2432]{1,0:T(8,128)(2,1)}, bf16[16,2432]{1,0:T(8,128)(2,1)S(1)}, u32[]{:S(2)}) copy-start(bf16[16,2432]{1,0:T(8,128)(2,1)S(1)} %collective-permute-done.22.refs_1_) | copy-start | bytes 233476
  85.9 2.9 %collective-permute-start.26 = (bf16[16,2432]{1,0:T(8,128)(2,1)S(1)}, bf16[16,2432]{1,0:T(8,128)(2,1)S(1)}, u32[]{:S(2)}, u32[]{:S(2)}) collective-permute-start(bf16[16,2432]{1,0:T(8,128)(2,1)S(1)} %collective-permute-done.22.refs_1_), channel_id=1, source_target_pairs={{0,1},{1,0},{2,3},{3,2},{4,5},{5,4},{6,7},{7,6},{8,9},{9,8},{10,11... | collective-permute-start | bytes 233480 | tf_op jit(solution)/shard_map/ppermute | solution.py:302
  86.4 0.7 copy-start.9
  88.8 0.6 copy-start.13
  88.8 0.6 copy-start.14
  88.8 0.7 copy-start.15
  88.9 0.7 copy-start.16
where the time goes:
time: 92.3 us; the launch traced here: 91.6 us
  waiting for transfers between devices  32.9 us (36%)
  starting transfers between devices  30.2 us (33%)
  Pallas kernels  22.1 us (24%)
  local copies, waits for them, and re-layouts  5.22 us (6%)
  between operations  0.94 us (1%)
    pallas_call x8, Pallas kernels, kernel_call(): pl.pallas_call(body, out_shape=outs, in_specs=[SM if i in smem else AN if...  22.1 us
    ppermute x7, waiting for transfers between devices, along(): return lax.ppermute(a, 'ctx', [(i, i ^ 2 * bit) for i in range(n_ctx)])  16.8 us
    ppermute x6, starting transfers between devices, up(): lax.ppermute(a, 'ctx', [(i, (i + 2 * step) % n_ctx) for i in range(n_ctx)])  16.3 us
    ppermute x6, waiting for transfers between devices, up(): lax.ppermute(a, 'ctx', [(i, (i + 2 * step) % n_ctx) for i in range(n_ctx)])  14.2 us
    ppermute x7, starting transfers between devices, along(): return lax.ppermute(a, 'ctx', [(i, i ^ 2 * bit) for i in range(n_ctx)])  5.91 us
    ppermute x3, starting transfers between devices, across(): return lax.ppermute(a, 'dp', [(i, i ^ bit) for i in range(n_dp)])  5.28 us
    unnamed x59, local copies, waits for them, and re-layouts  5.2 us
    ppermute x13, starting transfers between devices, swap(): return lax.ppermute(a, 'ctx', [(i, i ^ 1) for i in range(n_ctx)])  2.72 us
  transfers between devices with their start and end apart: 29, of which 12 were waited for; matrix products, arithmetic and copies ran while one was open for 1% of the time, Pallas kernels for 19%

commit v1 on v0

v1 whole, which is shorter than its diff:
```python
import functools
import math

import jax
import jax.numpy as jnp
from jax import lax
from jax.experimental import pallas as pl
from jax.experimental.pallas import tpu as pltpu
from jax.sharding import PartitionSpec as P


QUERY_HEADS = 16
KEY_VALUE_HEADS = 4
HEAD_WIDTH = 128
NEG_FILL = -1e30
ADAPTER_SCALE = 2.0
VMEM_MOST = 67043328


F32 = jnp.float32
BF16 = jnp.bfloat16
VM = pl.BlockSpec(memory_space=pltpu.VMEM)
SM = pl.BlockSpec(memory_space=pltpu.SMEM)
HB = pl.BlockSpec(memory_space=pltpu.HBM)

CORE_HEADS = KEY_VALUE_HEADS // 2
GROUP = QUERY_HEADS // KEY_VALUE_HEADS
Q_HALF = QUERY_HEADS * HEAD_WIDTH // 2
KV_HALF = CORE_HEADS * HEAD_WIDTH


def dot_nn(a, b):
    return lax.dot_general(a, b, (((1,), (0,)), ((), ())), preferred_element_type=F32)


def dot_nt(a, b):
    return lax.dot_general(a, b, (((1,), (1,)), ((), ())), preferred_element_type=F32)


def dot_tn(a, b):
    return lax.dot_general(a, b, (((0,), (0,)), ((), ())), preferred_element_type=F32)


def half_of(ref, core, width):
    return ref[:, pl.ds(pl.multiple_of(core * width, 128), width)]


def call(body, outs, args, scratch=(), flops=0, smem=(), hbm=(), limit=None):
    size = sum(a.size * a.dtype.itemsize for a in args)
    size += sum(o.size * o.dtype.itemsize for o in outs)
    held = size + sum(
        math.prod(m.shape) * jnp.dtype(m.dtype).itemsize
        for m in scratch
        if m.memory_space == pltpu.MemorySpace.VMEM
    )
    limit = min(limit or held + (4 << 20), VMEM_MOST)
    return kernel_call(body, outs, args, scratch, flops, size, limit, smem, hbm)


def kernel_call(body, outs, args, scratch, flops, size, limit, smem, hbm):
    return pl.pallas_call(
        body,
        out_shape=outs,
        in_specs=[SM if i in smem else HB if i in hbm else VM for i in range(len(args))],
        out_specs=[VM] * len(outs),
        scratch_shapes=list(scratch),
        compiler_params=pltpu.CompilerParams(vmem_limit_bytes=limit),
        cost_estimate=pl.CostEstimate(flops=flops, bytes_accessed=size, transcendentals=0),
    )(*args)


def split_kv(k_hbm, v_hbm, hidden_hbm, qa_hbm, va_hbm, own_ref, send_ref, hidden_ref, qa_ref, va_ref, sems):
    core = lax.axis_index("ctx") % 2
    rows = k_hbm.shape[0]
    copies = [(hidden_hbm, hidden_ref), (qa_hbm, qa_ref), (va_hbm, va_ref)]
    for i, source in enumerate((k_hbm, v_hbm)):
        columns = pl.ds(i * KV_HALF, KV_HALF)
        for half, target in ((core, own_ref), (1 - core, send_ref)):
            at = pl.ds(pl.multiple_of(half * KV_HALF, 128), KV_HALF)
            copies.append((source.at[:, at], target.at[pl.ds(0, rows), columns]))
    copies = [pltpu.make_async_copy(a, b, sems.at[i]) for i, (a, b) in enumerate(copies)]
    for copy in copies:
        copy.start()
    for copy in copies:
        copy.wait()
    at = 0
    for ref in (qa_ref, va_ref):
        down = dot_nt(ref[...], hidden_ref[...]).astype(BF16)
        for first in range(0, ref.shape[0], 8):
            own_ref[rows:, at : at + rows] = down[first : first + 8]
            send_ref[rows:, at : at + rows] = down[first : first + 8]
            at += rows


def split_rest(q_ref, g_ref, hidden_ref, pack_ref, send_ref):
    core = lax.axis_index("ctx") % 2
    pack_ref[:, :Q_HALF] = half_of(q_ref, 1 - core, Q_HALF)
    pack_ref[:, Q_HALF:] = half_of(g_ref, 1 - core, Q_HALF)
    send_ref[...] = half_of(hidden_ref, 1 - core, hidden_ref.shape[1] // 2)


def split_hidden(own_ref, far_ref, *outs):
    index = lax.axis_index("ctx")
    core, chip = index % 2, index // 2
    rows, width = far_ref.shape
    piece = width // 2
    for k in range(2):
        at = (chip % 2 ^ k) * piece
        outs[k][:rows] = own_ref[:, pl.ds(pl.multiple_of(core * width + at, 128), piece)]
        outs[k][rows:] = far_ref[:, pl.ds(pl.multiple_of(at, 128), piece)]


class Places:
    def __init__(self, lens_ref, rows):
        index = lax.axis_index("ctx")
        self.core, self.chip = index % 2, index // 2
        self.rows, self.chip_rows = rows, 2 * rows
        first_pos = self.chip * self.chip_rows
        self.row_pos = first_pos + self.local((1, self.chip_rows), 1)
        self.row_begin = jnp.zeros_like(self.row_pos)
        first_begin = jnp.int32(0)
        begin = jnp.int32(0)
        for i in range(lens_ref.shape[1]):
            inside = self.row_pos >= begin
            self.row_begin = jnp.where(inside, jnp.maximum(self.row_begin, begin), self.row_begin)
            first_begin = jnp.where(first_pos >= begin, jnp.maximum(first_begin, begin), first_begin)
            begin = begin + lens_ref[0, i]
        reach = (first_pos - first_begin + self.chip_rows - 1) // self.chip_rows + 1
        self.seen = jnp.minimum(reach, self.chip + 1)

    def local(self, shape, axis):
        t = lax.broadcasted_iota(jnp.int32, shape, axis)
        return jnp.where(t < self.rows, self.core * self.rows + t, (1 - self.core) * self.rows + t - self.rows)

    def visible(self, k):
        key_pos = (self.chip - k) * self.chip_rows + self.local((self.chip_rows, 1), 0)
        return (key_pos <= self.row_pos) & (key_pos >= self.row_begin)


def stack_heads(q_ref, g_ref, pack_ref, qs_ref, gs_ref):
    core = lax.axis_index("ctx") % 2
    rows = q_ref.shape[0]
    for i in range(CORE_HEADS * GROUP):
        g, j = i // GROUP, i % GROUP
        at = pl.ds(pl.multiple_of(core * Q_HALF + i * HEAD_WIDTH, 128), HEAD_WIDTH)
        first = 2 * j * rows
        for ref, out, base in ((q_ref, qs_ref, 0), (g_ref, gs_ref, Q_HALF)):
            out[g, first : first + rows] = ref[:, at]
            far = slice(base + i * HEAD_WIDTH, base + (i + 1) * HEAD_WIDTH)
            out[g, first + rows : first + 2 * rows] = pack_ref[:, far]


def key_rows(kv_ref, rows, columns):
    block_rows = kv_ref.shape[0] // 2
    halves = [kv_ref[first : first + rows, columns] for first in (0, block_rows)]
    return jnp.concatenate(halves, axis=0)


def head_parts(chip_rows):
    return [slice(j * chip_rows, (j + 1) * chip_rows) for j in range(GROUP)]


def chunk_scores(k, rows, lens_ref, kv_ref, *refs):
    if k == 0:
        stack_heads(*refs[:3], *refs[6:8])
        (e_ref, dp_ref, stats_ref), (qs_ref, gs_ref) = refs[3:6], refs[6:8]
    else:
        qs_ref, gs_ref, e_ref, dp_ref, stats_ref = refs
    places = Places(lens_ref, rows)
    head_scale = HEAD_WIDTH ** (-0.5)

    @pl.when(k < places.seen)
    def _():
        visible = places.visible(k)

        def one_group(g, _):
            keys = key_rows(kv_ref, rows, pl.ds(pl.multiple_of(g * HEAD_WIDTH, 128), HEAD_WIDTH))
            values = key_rows(kv_ref, rows, pl.ds(pl.multiple_of(KV_HALF + g * HEAD_WIDTH, 128), HEAD_WIDTH))
            for part in head_parts(2 * rows):
                s = dot_nt(keys, qs_ref[g, part]) * head_scale
                s = jnp.where(visible, s, NEG_FILL)
                top = jnp.max(s, axis=0, keepdims=True)
                e = jnp.exp(s - top)
                dp = dot_nt(values, gs_ref[g, part])
                e_ref[g, :, part] = e.astype(e_ref.dtype)
                dp_ref[g, :, part] = dp.astype(dp_ref.dtype)
                stats_ref[g, 0:1, part] = top
                stats_ref[g, 1:2, part] = jnp.sum(e, axis=0, keepdims=True)
                stats_ref[g, 2:3, part] = jnp.sum(e * dp, axis=0, keepdims=True)
            return 0

        lax.fori_loop(0, CORE_HEADS, one_group, 0)

    @pl.when(k >= places.seen)
    def _():
        stats_ref[:, 0:1] = jnp.full_like(stats_ref[:, 0:1], NEG_FILL)
        stats_ref[:, 1:3] = jnp.zeros_like(stats_ref[:, 1:3])


def gradients(n_chips, rank, rows, tail, *refs):
    lens_ref, qs, gs, qb_ref, vb_ref = refs[:5]
    refs = refs[5:]
    kv, e_in, dp_in, stats = (refs[i * n_chips : (i + 1) * n_chips] for i in range(4))
    refs = refs[4 * n_chips :]
    dq_own_ref, dq_send_ref = refs[:2]
    dkv = refs[2 : 2 + n_chips]
    message_out = refs[2 + n_chips : 2 + 2 * n_chips]
    proj, vl, p_ref, ds_ref, dqt, ups, low_ref = refs[2 + 2 * n_chips :]
    places = Places(lens_ref, rows)
    core, chip, chip_rows = places.core, places.chip, places.chip_rows
    head_scale = HEAD_WIDTH ** (-0.5)
    parts = head_parts(chip_rows)
    block_rows = kv[0].shape[0] // 2

    for k in range(n_chips):
        for side in (0, 1):
            first = side * block_rows + rows
            for i in range(2 * rank // 8):
                proj[k, 8 * i : 8 * i + 8, side * rows : (side + 1) * rows] = kv[k][
                    first : first + 8, i * rows : (i + 1) * rows
                ]
        if k:

            @pl.when(k >= places.seen)
            def _():
                dkv[k][...] = jnp.zeros_like(dkv[k])

    vl[...] = jnp.zeros_like(vl)
    low_ref[...] = jnp.zeros_like(low_ref)
    ups[...] = jnp.zeros_like(ups)

    def one_group(g, _):
        at_k = pl.ds(pl.multiple_of(g * HEAD_WIDTH, 128), HEAD_WIDTH)
        at_v = pl.ds(pl.multiple_of(KV_HALF + g * HEAD_WIDTH, 128), HEAD_WIDTH)
        top = functools.reduce(jnp.maximum, [ref[g, 0:1] for ref in stats])
        weight = [jnp.exp(ref[g, 0:1] - top) for ref in stats]
        inverse = 1.0 / sum(ref[g, 1:2] * w for ref, w in zip(stats, weight))
        delta = sum(ref[g, 2:3] * w for ref, w in zip(stats, weight)) * inverse
        dqt[...] = jnp.zeros_like(dqt)
        for k in range(n_chips):

            @pl.when(k < places.seen)
            def _():
                factor = weight[k] * inverse
                for part in parts:
                    p = e_in[k][g, :, part].astype(F32) * factor[:, part]
                    p_ref[:, part] = p.astype(BF16)
                    ds = p * (dp_in[k][g, :, part].astype(F32) - delta[:, part]) * head_scale
                    ds_ref[:, part] = ds.astype(BF16)
                ds = ds_ref[...]
                dv = dot_nn(p_ref[...], gs[g]).astype(BF16)
                dkv[k][:, at_k] = dot_nn(ds, qs[g]).astype(BF16)
                dkv[k][:, at_v] = dv
                dqt[...] += dot_tn(key_rows(kv[k], rows, at_k), ds)
                at_b = pl.multiple_of(core * KV_HALF + g * HEAD_WIDTH, 128)
                vl[chip - k] += dot_nt(vb_ref[:, pl.ds(at_b, HEAD_WIDTH)], dv)

        at_b = pl.multiple_of(core * Q_HALF + g * GROUP * HEAD_WIDTH, 128)
        for j, part in enumerate(parts):
            up = qb_ref[:, pl.ds(pl.multiple_of(at_b + j * HEAD_WIDTH, 128), HEAD_WIDTH)]
            low_ref[...] += dot_nn(up, dqt[:, part].astype(BF16))
            dq = jnp.transpose(dqt[:, part]).astype(BF16)
            at = pl.ds(pl.multiple_of((g * GROUP + j) * HEAD_WIDTH, 128), HEAD_WIDTH)
            dq_own_ref[:, at] = dq[:rows]
            dq_send_ref[:, at] = dq[rows:]
            ups[:, at] = dot_nn(proj[0, :rank], dq)
        return 0

    lax.fori_loop(0, CORE_HEADS, one_group, 0)
    for k in range(n_chips):

        @pl.when(k < places.seen)
        def _():
            ups[:, Q_HALF : Q_HALF + KV_HALF] += dot_nn(proj[k, rank:], dkv[k][:, KV_HALF:])

    for k in range(n_chips):
        message_out[k][:, :chip_rows] = low_ref[...].astype(BF16)
        for i in range(2):
            message_out[k][:, (i + 1) * chip_rows : (i + 2) * chip_rows] = vl[chip ^ k ^ i].astype(BF16)
        at = pl.multiple_of((chip ^ k) * tail, 128)
        message_out[k][:, 3 * chip_rows :] = ups[:, pl.ds(at, tail)].astype(BF16)


def adapters(n_chips, rank, *refs):
    own, far = refs[:n_chips], refs[n_chips : 2 * n_chips]
    hidden = refs[2 * n_chips : 2 * n_chips + 2]
    out_ref = refs[-1]
    chip_rows, width = hidden[0].shape
    rows = chip_rows // 2
    query, value = jnp.zeros((rank, width), F32), jnp.zeros((rank, width), F32)
    for k in range(2):
        for first, other in ((0, rows), (rows, 0)):
            tokens = hidden[k][first : first + rows]
            low = own[k][:, first : first + rows].astype(F32) + far[k][:, other : other + rows].astype(F32)
            query += dot_nn(low.astype(BF16), tokens)
            at = (k + 1) * chip_rows
            low = sum(ref[:, at + first : at + first + rows].astype(F32) for ref in own)
            low += sum(ref[:, at + other : at + other + rows].astype(F32) for ref in far)
            value += dot_nn(low.astype(BF16), tokens)
    out_ref[:, :width] = (ADAPTER_SCALE * query).astype(BF16)
    out_ref[:, width : 2 * width] = (ADAPTER_SCALE * value).astype(BF16)
    tail = sum(ref[:, 3 * chip_rows :].astype(F32) for ref in own)
    out_ref[:, 2 * width :] = (ADAPTER_SCALE * tail).astype(BF16)


def finish_adapters(n_chips, tail, *refs):
    own, far = refs[:n_chips], refs[n_chips : 2 * n_chips]
    qa_ref, qb_ref, va_ref, vb_ref, buffer = refs[-5:]
    index = lax.axis_index("ctx")
    core, chip = index % 2, index // 2
    width = qa_ref.shape[1] // 4
    for half, pieces in ((core, own), (1 - core, far)):
        for side in (0, 1):
            total = tree_sum([ref[:, : 2 * width].astype(F32) for ref in pieces[side::2]])
            at = pl.ds(pl.multiple_of((2 * half + (chip % 2 ^ side)) * width, 128), width)
            qa_ref[:, at] = total[:, :width]
            va_ref[:, at] = total[:, width:]
        for k in range(n_chips):
            at = pl.ds(pl.multiple_of((chip ^ k) * tail, 128), tail)
            buffer[:, at] = pieces[k][:, 2 * width :].astype(F32)
        qb_ref[:, pl.ds(pl.multiple_of(half * Q_HALF, 128), Q_HALF)] = buffer[:, :Q_HALF]
        vb_ref[:, pl.ds(pl.multiple_of(half * KV_HALF, 128), KV_HALF)] = buffer[:, Q_HALF : Q_HALF + KV_HALF]


def join_rows(own_ref, far_ref, out_ref):
    core = lax.axis_index("ctx") % 2
    width = own_ref.shape[1]
    out_ref[:, pl.ds(pl.multiple_of(core * width, 128), width)] = own_ref[...]
    out_ref[:, pl.ds(pl.multiple_of((1 - core) * width, 128), width)] = far_ref[...]


def join_kv(own_ref, far_ref, dk_ref, dv_ref):
    core = lax.axis_index("ctx") % 2
    rows = far_ref.shape[0]
    for i, ref in enumerate((dk_ref, dv_ref)):
        columns = slice(i * KV_HALF, (i + 1) * KV_HALF)
        ref[:, pl.ds(pl.multiple_of(core * KV_HALF, 128), KV_HALF)] = own_ref[:rows, columns]
        ref[:, pl.ds(pl.multiple_of((1 - core) * KV_HALF, 128), KV_HALF)] = far_ref[:, columns]


def tree_sum(parts):
    while len(parts) > 1:
        parts = [a + b for a, b in zip(parts[::2], parts[1::2])]
    return parts[0]


def step(query, key, value, gradient, hidden, doc_lengths, querya, queryb, valuea, valueb):
    n_ctx, n_dp = lax.axis_size("ctx"), lax.axis_size("dp")
    n_chips = n_ctx // 2
    q, k, v, g, x = query[0], key[0], value[0], gradient[0], hidden[0]
    rows, width = x.shape[0], x.shape[1] // 2
    rank = querya.shape[0]
    chip_rows = 2 * rows
    lanes = GROUP * chip_rows
    sds = jax.ShapeDtypeStruct

    def swap(a):
        return lax.ppermute(a, "ctx", [(i, i ^ 1) for i in range(n_ctx)])

    def up(a, step):
        return lax.ppermute(a, "ctx", [(i, (i + 2 * step) % n_ctx) for i in range(n_ctx)])

    def down(a, step):
        return up(a, -step)

    def across(a, bit):
        return lax.ppermute(a, "dp", [(i, i ^ bit) for i in range(n_dp)])

    def along(a, bit):
        return lax.ppermute(a, "ctx", [(i, i ^ (2 * bit)) for i in range(n_ctx)])

    block = sds((rows + 2 * rank * rows // (2 * KV_HALF), 2 * KV_HALF), BF16)
    kv_own, kv_send = call(
        split_kv,
        [block] * 2,
        (k, v, x, querya, valuea),
        scratch=[
            pltpu.VMEM(x.shape, BF16),
            pltpu.VMEM(querya.shape, BF16),
            pltpu.VMEM(valuea.shape, BF16),
            pltpu.SemaphoreType.DMA((7,)),
        ],
        hbm=range(5),
        limit=VMEM_MOST - (3 << 17),
    )
    kv = [jnp.concatenate([kv_own, swap(kv_send)], axis=0)]
    if n_chips > 1:
        last = up(kv[0], n_chips - 1)
        for _ in range(1, n_chips - 1):
            kv.append(up(kv[-1], 1))
        kv.append(last)

    pack, hidden_far = call(
        split_rest,
        [sds((rows, 2 * Q_HALF), BF16), sds((rows, width), BF16)],
        (q, g, x),
    )
    pack, hidden_far = swap(pack), swap(hidden_far)
    hiddens = call(split_hidden, [sds((chip_rows, width // 2), BF16)] * 2, (x, hidden_far))
    hiddens = [hiddens[0], along(hiddens[1], 1)]

    tail = -(-(Q_HALF + KV_HALF) // (128 * n_chips)) * 128
    tile = (CORE_HEADS, chip_rows, lanes)
    held = F32 if 8 * n_chips * math.prod(tile) <= 32 << 20 else BF16
    chunk = [sds(tile, held)] * 2 + [sds((CORE_HEADS, 8, lanes), F32)]
    stacked = sds((CORE_HEADS, lanes, HEAD_WIDTH), BF16)
    work = 2 * 2 * math.prod(tile) * HEAD_WIDTH
    chunks = [None] * n_chips
    *chunks[0], qs, gs = call(
        functools.partial(chunk_scores, 0, rows),
        chunk + [stacked] * 2,
        (doc_lengths, kv[0], q, g, pack),
        flops=work,
        smem=(0,),
    )
    for c in range(1, n_chips):
        chunks[c] = call(
            functools.partial(chunk_scores, c, rows), chunk, (doc_lengths, kv[c], qs, gs), flops=work, smem=(0,)
        )
    outs = (
        [sds((rows, Q_HALF), BF16)] * 2
        + [sds((chip_rows, 2 * KV_HALF), BF16)] * n_chips
        + [sds((rank, 3 * chip_rows + tail), BF16)] * n_chips
    )
    result = call(
        functools.partial(gradients, n_chips, rank, rows, tail),
        outs,
        (doc_lengths, qs, gs, queryb, valueb, *kv, *(c[i] for i in range(3) for c in chunks)),
        scratch=[
            pltpu.VMEM((n_chips, 2 * rank, chip_rows), BF16),
            pltpu.VMEM((n_chips, rank, chip_rows), F32),
            pltpu.VMEM((chip_rows, lanes), BF16),
            pltpu.VMEM((chip_rows, lanes), BF16),
            pltpu.VMEM((HEAD_WIDTH, lanes), F32),
            pltpu.VMEM((rank, tail * n_chips), F32),
            pltpu.VMEM((rank, chip_rows), F32),
        ],
        flops=3 * n_chips * work // 2,
        smem=(0,),
    )
    dq_own, dq_send = result[:2]
    dkv = result[2 : 2 + n_chips]
    messages = result[2 + n_chips :]

    own = [messages[0]] + [along(messages[bit], bit) for bit in range(1, n_chips)]
    far = [swap(a) for a in own]

    if n_chips > 1:
        last = down(dkv[n_chips - 1], n_chips - 1)
        total = dkv[n_chips - 2]
        for step in range(n_chips - 2, 0, -1):
            total = down(total, 1).astype(F32) + dkv[step - 1].astype(F32)
            total = (total if step > 1 else total + last.astype(F32)).astype(BF16)
    else:
        total = dkv[0]
    (query_grad,) = call(join_rows, [sds((rows, 2 * Q_HALF), BF16)], (dq_own, swap(dq_send)))
    dkv_far = swap(total[rows:])
    key_grad, value_grad = call(join_kv, [sds((rows, 2 * KV_HALF), BF16)] * 2, (total, dkv_far))

    (part,) = call(
        functools.partial(adapters, n_chips, rank),
        [sds((rank, width + tail), BF16)],
        (*own, *far, *hiddens),
    )
    got = [part] + [across(part, bit) for bit in range(1, n_dp)]
    part = tree_sum([a.astype(F32) for a in got]).astype(BF16)
    own = [part] + [along(part, bit) for bit in range(1, n_chips)]
    far = [swap(a) for a in own]
    qa_grad, qb_grad, va_grad, vb_grad = call(
        functools.partial(finish_adapters, n_chips, tail),
        [
            sds((rank, 2 * width), F32),
            sds((rank, 2 * Q_HALF), F32),
            sds((rank, 2 * width), F32),
            sds((rank, 2 * KV_HALF), F32),
        ],
        (*own, *far),
        scratch=[pltpu.VMEM((rank, tail * n_chips), F32)],
    )
    return (
        query_grad[None],
        key_grad[None],
        value_grad[None],
        qa_grad,
        qb_grad,
        va_grad,
        vb_grad,
    )


def solution(mesh):
    tokens = P("dp", "ctx", None)
    return jax.shard_map(
        step,
        mesh=mesh,
        in_specs=(tokens,) * 5 + (P("dp", None),) + (P(),) * 4,
        out_specs=(tokens,) * 3 + (P(),) * 4,
        check_vma=False,
    )
```

time: 92.3 us -> 78.5 us (0.85)
  Pallas kernels: 22.1 us -> 12.4 us
  waiting for transfers between devices: 32.9 us -> 23.6 us
  starting transfers between devices: 30.2 us -> 36.9 us
  local copies, waits for them, and re-layouts: 5.22 us -> 4.27 us
    ppermute x7, waiting for transfers between devices: 16.8 us -> 7.11 us  [along(): return lax.ppermute(a, 'ctx', [(i, i ^ 2 * bit) for i in range(n_ctx)])]
    pallas_call x8 -> x12, Pallas kernels: 22.1 us -> 12.4 us  [kernel_call(): pl.pallas_call(body, out_shape=outs, in_specs=[SM if i in smem else HB if...]
    ppermute x7, starting transfers between devices: 5.91 us -> 15.4 us  [along(): return lax.ppermute(a, 'ctx', [(i, i ^ 2 * bit) for i in range(n_ctx)])]
    ppermute x6, starting transfers between devices: 16.3 us -> 14.7 us  [up(): lax.ppermute(a, 'ctx', [(i, (i + 2 * step) % n_ctx) for i in range(n_ctx)])]
    ppermute x3, starting transfers between devices: 5.28 us -> 4.29 us  [across(): return lax.ppermute(a, 'dp', [(i, i ^ bit) for i in range(n_dp)])]
    unnamed x59 -> x19, local copies, waits for them, and re-layouts: 5.2 us -> 4.25 us
  transfers between devices with their start and end apart: 29 -> 29, of which waited for: 12 -> 12; matrix products, arithmetic and copies ran while one was open for 1% -> 1% of each run, Pallas kernels for 19% -> 11%
where the time goes in v1:
time: 78.5 us; the launch traced here: 78.2 us
  starting transfers between devices  36.9 us (47%)
  waiting for transfers between devices  23.6 us (30%)
  Pallas kernels  12.4 us (16%)
  local copies, waits for them, and re-layouts  4.27 us (5%)
  between operations  0.84 us (1%)
    ppermute x7, starting transfers between devices, along(): return lax.ppermute(a, 'ctx', [(i, i ^ 2 * bit) for i in range(n_ctx)])  15.4 us
    ppermute x6, starting transfers between devices, up(): lax.ppermute(a, 'ctx', [(i, (i + 2 * step) % n_ctx) for i in range(n_ctx)])  14.7 us
    ppermute x6, waiting for transfers between devices, up(): lax.ppermute(a, 'ctx', [(i, (i + 2 * step) % n_ctx) for i in range(n_ctx)])  13.7 us
    pallas_call x12, Pallas kernels, kernel_call(): pl.pallas_call(body, out_shape=outs, in_specs=[SM if i in smem else HB if...  12.4 us
    ppermute x7, waiting for transfers between devices, along(): return lax.ppermute(a, 'ctx', [(i, i ^ 2 * bit) for i in range(n_ctx)])  7.11 us
    ppermute x3, starting transfers between devices, across(): return lax.ppermute(a, 'dp', [(i, i ^ bit) for i in range(n_dp)])  4.29 us
    unnamed x19, local copies, waits for them, and re-layouts  4.25 us
    ppermute x13, starting transfers between devices, swap(): return lax.ppermute(a, 'ctx', [(i, i ^ 1) for i in range(n_ctx)])  2.52 us
  transfers between devices with their start and end apart: 29, of which 12 were waited for; matrix products, arithmetic and copies ran while one was open for 1% of the time, Pallas kernels for 11%

profile of v1, /device:TPU:0, one launch (start us, length us, event | category | flops | bytes accessed | tf_op | source)
XLA Modules:
  0.0 78.2 jit_solution(4593366880646575752)
XLA Ops:
  0.6 2.8 %shard_map.153 = (bf16[136,512]{1,0:T(8,128)(2,1)}, bf16[136,512]{1,0:T(8,128)(2,1)}) custom-call(bf16[128,512]{1,0:T(8,128)(2,1)} %bitcast.16, bf16[128,512]{1,0:T(8,128)(2,1)} %bitcast.17, bf16[128,4096]{1,0:T(8,128)(2,1)} %bitcast.8, bf16[16,4096]{1,0:T(8,128)(2,1)} %qa_hbm.1, bf16[16,4096]{1,0:T(8,128)(2,1)} %va_hbm.1), custom_call_target="tpu_custom_call" | custom-call | bytes 1851392 | tf_op jit(solution)/shard_map/pallas_call | solution.py:61
  3.4 0.6 collective-permute-start
  4.0 1.2 %copy-done = bf16[1,128,4096]{2,1,0:T(8,128)(2,1)S(1)} copy-done((bf16[1,128,4096]{2,1,0:T(8,128)(2,1)S(1)}, bf16[1,128,4096]{2,1,0:T(8,128)(2,1)}, u32[]{:S(2)}) %copy-start) | copy-done | bytes 1048600
  5.2 1.0 %copy-done.2 = bf16[1,128,2048]{2,1,0:T(8,128)(2,1)S(1)} copy-done((bf16[1,128,2048]{2,1,0:T(8,128)(2,1)S(1)}, bf16[1,128,2048]{2,1,0:T(8,128)(2,1)}, u32[]{:S(2)}) %copy-start.2) | copy-done | bytes 524312
  6.3 1.0 %copy-done.4 = bf16[1,128,2048]{2,1,0:T(8,128)(2,1)S(1)} copy-done((bf16[1,128,2048]{2,1,0:T(8,128)(2,1)S(1)}, bf16[1,128,2048]{2,1,0:T(8,128)(2,1)}, u32[]{:S(2)}) %copy-start.4) | copy-done | bytes 524312
  7.3 0.1 shard_map.154
  7.4 0.1 collective-permute-start.1
  7.5 0.5 collective-permute-start.17
  8.0 0.9 %constant_dynamic-update-slice_fusion.1 = bf16[272,512]{1,0:T(8,128)(2,1)S(1)} fusion(bf16[136,512]{1,0:T(8,128)(2,1)} %get-tuple-element.43), kind=kLoop, calls=%fused_computation.4 | loop fusion | bytes 278528
  8.9 2.7 %collective-permute-start.2 = (bf16[272,512]{1,0:T(8,128)(2,1)S(1)}, bf16[272,512]{1,0:T(8,128)(2,1)S(1)}, u32[]{:S(2)}, u32[]{:S(2)}) collective-permute-start(bf16[272,512]{1,0:T(8,128)(2,1)S(1)} %constant_dynamic-update-slice_fusion.kv_ref.refs_5_), channel_id=1, source_target_pairs={{0,2},{1,3},{2,4},{3,5},{4,6},{5,7},{6,0},{7,1},{8,10},{9,11},{10,... | collective-permute-start | bytes 835592 | tf_op jit(solution)/shard_map/ppermute | solution.py:361
  11.6 2.1 %collective-permute-start.4 = (bf16[272,512]{1,0:T(8,128)(2,1)S(1)}, bf16[272,512]{1,0:T(8,128)(2,1)S(1)}, u32[]{:S(2)}, u32[]{:S(2)}) collective-permute-start(bf16[272,512]{1,0:T(8,128)(2,1)S(1)} %constant_dynamic-update-slice_fusion.kv_ref.refs_5_), channel_id=1, source_target_pairs={{0,6},{1,7},{2,0},{3,1},{4,2},{5,3},{6,4},{7,5},{8,14},{9,15},{10,... | collective-permute-start | bytes 835592 | tf_op jit(solution)/shard_map/ppermute | solution.py:361
  13.7 7.5 %collective-permute-done.2.kv_ref.refs_6_ = bf16[272,512]{1,0:T(8,128)(2,1)S(1)} collective-permute-done((bf16[272,512]{1,0:T(8,128)(2,1)S(1)}, bf16[272,512]{1,0:T(8,128)(2,1)S(1)}, u32[]{:S(2)}, u32[]{:S(2)}) %collective-permute-start.2) | collective-permute-done | bytes 278560 | tf_op jit(solution)/shard_map/ppermute | solution.py:361
  21.2 0.1 shard_map.162
  21.3 6.5 %collective-permute-start.18 = (bf16[256,1024]{1,0:T(8,128)(2,1)S(1)}, bf16[256,1024]{1,0:T(8,128)(2,1)S(1)}, u32[]{:S(2)}, u32[]{:S(2)}) collective-permute-start(bf16[256,1024]{1,0:T(8,128)(2,1)S(1)} %get-tuple-element.74), channel_id=1, source_target_pairs={{0,2},{1,3},{2,0},{3,1},{4,6},{5,7},{6,4},{7,5},{8,10},{9,11},{10,... | collective-permute-start | bytes 1572872 | tf_op jit(solution)/shard_map/ppermute | solution.py:370
  27.9 2.1 %shard_map.155 = (f32[2,256,1024]{2,1,0:T(8,128)S(1)}, f32[2,256,1024]{2,1,0:T(8,128)S(1)}, f32[2,8,1024]{2,1,0:T(8,128)S(1)}, bf16[2,1024,128]{2,1,0:T(8,128)(2,1)S(1)}, bf16[2,1024,128]{2,1,0:T(8,128)(2,1)S(1)}) custom-call(s32[1,16]{1,0:T(1,128)S(1)} %copy-done.8, bf16[272,512]{1,0:T(8,128)(2,1)S(1)} %constant_dynamic-update-slice_fusion.kv_ref.refs_5_, ...), custom_call_target="tpu_custom_call" | custom-call | flops 268435456 | bytes 7159872 | tf_op jit(solution)/shard_map/pallas_call | solution.py:61
  30.0 0.0 copy-start.6
  30.0 0.0 copy-start.7
  30.0 0.6 shard_map.156
  30.6 0.0 collective-permute-done.4.kv_ref.refs_8_
  30.6 0.6 shard_map.158
  31.2 4.8 %collective-permute-done.3.kv_ref.refs_7_ = bf16[272,512]{1,0:T(8,128)(2,1)S(1)} collective-permute-done((bf16[272,512]{1,0:T(8,128)(2,1)S(1)}, bf16[272,512]{1,0:T(8,128)(2,1)S(1)}, u32[]{:S(2)}, u32[]{:S(2)}) %collective-permute-start.3) | collective-permute-done | bytes 278560 | tf_op jit(solution)/shard_map/ppermute | solution.py:361
  36.0 0.6 shard_map.157
  36.6 2.7 %shard_map.159 = (bf16[128,1024]{1,0:T(8,128)(2,1)S(1)}, bf16[128,1024]{1,0:T(8,128)(2,1)S(1)}, bf16[256,512]{1,0:T(8,128)(2,1)S(1)}, bf16[256,512]{1,0:T(8,128)...) custom-call(s32[1,16]{1,0:T(1,128)S(1)} %copy-done.8, ...), custom_call_target="tpu_custom_call" | custom-call | flops 1610612736 | bytes 21004352 | tf_op jit(solution)/shard_map/pallas_call | solution.py:61
  39.3 5.9 %collective-permute-start.6 = (bf16[256,512]{1,0:T(8,128)(2,1)S(1)}, bf16[256,512]{1,0:T(8,128)(2,1)S(1)}, u32[]{:S(2)}, u32[]{:S(2)}) collective-permute-start(bf16[256,512]{1,0:T(8,128)(2,1)S(1)} %get-tuple-element.62), channel_id=1, source_target_pairs={{0,6},{1,7},{2,0},{3,1},{4,2},{5,3},{6,4},{7,5},{8,14},{9,15},{10,... | collective-permute-start | bytes 786440 | tf_op jit(solution)/shard_map/ppermute | solution.py:361
  45.2 0.0 collective-permute-start.10
  45.2 0.6 collective-permute-start.11
  45.8 3.7 %collective-permute-start.12 = (bf16[16,1152]{1,0:T(8,128)(2,1)S(1)}, bf16[16,1152]{1,0:T(8,128)(2,1)S(1)}, u32[]{:S(2)}, u32[]{:S(2)}) collective-permute-start(bf16[16,1152]{1,0:T(8,128)(2,1)S(1)} %get-tuple-element.71), channel_id=1, source_target_pairs={{0,6},{1,7},{2,4},{3,5},{4,2},{5,3},{6,0},{7,1},{8,14},{9,15},{10,... | collective-permute-start | bytes 110600 | tf_op jit(solution)/shard_map/ppermute | solution.py:370
  49.6 1.5 %collective-permute-done.10.refs_1_ = bf16[16,1152]{1,0:T(8,128)(2,1)S(1)} collective-permute-done((bf16[16,1152]{1,0:T(8,128)(2,1)S(1)}, bf16[16,1152]{1,0:T(8,128)(2,1)S(1)}, u32[]{:S(2)}, u32[]{:S(2)}) %collective-permute-start.10) | collective-permute-done | bytes 36896 | tf_op jit(solution)/shard_map/ppermute | solution.py:370
  51.1 0.0 collective-permute-start.13
  51.1 0.0 collective-permute-done.11.refs_2_
  51.1 0.5 collective-permute-start.14
  51.6 0.5 collective-permute-done.12.refs_3_
  52.1 0.2 collective-permute-done.13.refs_4_
  52.3 0.3 collective-permute-start.16
  52.6 0.9 %collective-permute-start.8 = (bf16[256,512]{1,0:T(8,128)(2,1)S(1)}, bf16[256,512]{1,0:T(8,128)(2,1)S(1)}, u32[]{:S(2)}, u32[]{:S(2)}) collective-permute-start(bf16[256,512]{1,0:T(8,128)(2,1)S(1)} %get-tuple-element.65), channel_id=1, source_target_pairs={{0,2},{1,3},{2,4},{3,5},{4,6},{5,7},{6,0},{7,1},{8,10},{9,11},{10,... | collective-permute-start | bytes 786440 | tf_op jit(solution)/shard_map/ppermute | solution.py:361
  53.5 0.0 collective-permute-done.15.refs_6_
  53.5 0.0 collective-permute-done.16.refs_7_
  53.5 0.0 collective-permute-done.18.refs_9_
  53.5 0.4 shard_map.163
  53.9 2.7 %collective-permute-start.19 = (bf16[16,2432]{1,0:T(8,128)(2,1)S(1)}, bf16[16,2432]{1,0:T(8,128)(2,1)S(1)}, u32[]{:S(2)}, u32[]{:S(2)}) collective-permute-start(bf16[16,2432]{1,0:T(8,128)(2,1)S(1)} %shard_map.163), channel_id=1, source_target_pairs={{0,8},{8,0},{16,24},{24,16},{1,9},{9,1},{17,25},{25,17},{2,10},{10... | collective-permute-start | bytes 233480 | tf_op jit(solution)/shard_map/ppermute | solution.py:367
  56.7 1.5 %collective-permute-start.20 = (bf16[16,2432]{1,0:T(8,128)(2,1)S(1)}, bf16[16,2432]{1,0:T(8,128)(2,1)S(1)}, u32[]{:S(2)}, u32[]{:S(2)}) collective-permute-start(bf16[16,2432]{1,0:T(8,128)(2,1)S(1)} %shard_map.163), channel_id=1, source_target_pairs={{0,16},{8,24},{16,0},{24,8},{1,17},{9,25},{17,1},{25,9},{2,18},{10... | collective-permute-start | bytes 233480 | tf_op jit(solution)/shard_map/ppermute | solution.py:367
  58.2 0.0 collective-permute-start.21
  58.2 0.1 add_convert_fusion.1
  58.3 1.3 %collective-permute-done.19 = bf16[16,2432]{1,0:T(8,128)(2,1)S(1)} collective-permute-done((bf16[16,2432]{1,0:T(8,128)(2,1)S(1)}, bf16[16,2432]{1,0:T(8,128)(2,1)S(1)}, u32[]{:S(2)}, u32[]{:S(2)}) %collective-permute-start.19) | collective-permute-done | bytes 77856 | tf_op jit(solution)/shard_map/ppermute | solution.py:367
  59.6 3.2 %collective-permute-start.7 = (bf16[256,512]{1,0:T(8,128)(2,1)S(1)}, bf16[256,512]{1,0:T(8,128)(2,1)S(1)}, u32[]{:S(2)}, u32[]{:S(2)}) collective-permute-start(bf16[256,512]{1,0:T(8,128)(2,1)S(1)} %add_convert_fusion.1), channel_id=1, source_target_pairs={{0,6},{1,7},{2,0},{3,1},{4,2},{5,3},{6,4},{7,5},{8,14},{9,15},{10,... | collective-permute-start | bytes 786440 | tf_op jit(solution)/shard_map/ppermute | solution.py:361
  62.8 0.7 collective-permute-done.21
  63.5 1.7 %collective-permute-start.22 = (bf16[16,2432]{1,0:T(8,128)(2,1)S(1)}, bf16[16,2432]{1,0:T(8,128)(2,1)S(1)}, u32[]{:S(2)}, u32[]{:S(2)}) collective-permute-start(bf16[16,2432]{1,0:T(8,128)(2,1)S(1)} %add_convert_fusion.2.refs_0_), channel_id=1, source_target_pairs={{0,2},{1,3},{2,0},{3,1},{4,6},{5,7},{6,4},{7,5},{8,10},{9,11},{10,... | collective-permute-start | bytes 233480 | tf_op jit(solution)/shard_map/ppermute | solution.py:370
  65.2 2.2 %collective-permute-start.23 = (bf16[16,2432]{1,0:T(8,128)(2,1)S(1)}, bf16[16,2432]{1,0:T(8,128)(2,1)S(1)}, u32[]{:S(2)}, u32[]{:S(2)}) collective-permute-start(bf16[16,2432]{1,0:T(8,128)(2,1)S(1)} %add_convert_fusion.2.refs_0_), channel_id=1, source_target_pairs={{0,4},{1,5},{2,6},{3,7},{4,0},{5,1},{6,2},{7,3},{8,12},{9,13},{10,... | collective-permute-start | bytes 233480 | tf_op jit(solution)/shard_map/ppermute | solution.py:370
  67.4 0.0 collective-permute-done.8
  67.4 0.6 collective-permute-start.24
  68.0 1.5 %collective-permute-done.7 = bf16[256,512]{1,0:T(8,128)(2,1)S(1)} collective-permute-done((bf16[256,512]{1,0:T(8,128)(2,1)S(1)}, bf16[256,512]{1,0:T(8,128)(2,1)S(1)}, u32[]{:S(2)}, u32[]{:S(2)}) %collective-permute-start.7) | collective-permute-done | bytes 262176 | tf_op jit(solution)/shard_map/ppermute | solution.py:361
  69.5 0.1 add_convert_fusion.own_ref
  69.6 0.1 collective-permute-start.9
  69.7 0.0 collective-permute-done.5.far_ref
  69.7 0.5 collective-permute-start.25
  70.2 1.4 %collective-permute-done.22.refs_1_ = bf16[16,2432]{1,0:T(8,128)(2,1)S(1)} collective-permute-done((bf16[16,2432]{1,0:T(8,128)(2,1)S(1)}, bf16[16,2432]{1,0:T(8,128)(2,1)S(1)}, u32[]{:S(2)}, u32[]{:S(2)}) %collective-permute-start.22) | collective-permute-done | bytes 77856 | tf_op jit(solution)/shard_map/ppermute | solution.py:370
  71.6 0.9 %collective-permute-done.23.refs_2_ = bf16[16,2432]{1,0:T(8,128)(2,1)S(1)} collective-permute-done((bf16[16,2432]{1,0:T(8,128)(2,1)S(1)}, bf16[16,2432]{1,0:T(8,128)(2,1)S(1)}, u32[]{:S(2)}, u32[]{:S(2)}) %collective-permute-start.23) | collective-permute-done | bytes 77856 | tf_op jit(solution)/shard_map/ppermute | solution.py:370
  72.5 0.0 collective-permute-start.27
  72.5 2.8 %collective-permute-done.24.refs_3_ = bf16[16,2432]{1,0:T(8,128)(2,1)S(1)} collective-permute-done((bf16[16,2432]{1,0:T(8,128)(2,1)S(1)}, bf16[16,2432]{1,0:T(8,128)(2,1)S(1)}, u32[]{:S(2)}, u32[]{:S(2)}) %collective-permute-start.24) | collective-permute-done | bytes 77856 | tf_op jit(solution)/shard_map/ppermute | solution.py:370
  75.3 0.8 %shard_map.160 = bf16[128,2048]{1,0:T(8,128)(2,1)} custom-call(bf16[128,1024]{1,0:T(8,128)(2,1)S(1)} %get-tuple-element.60.own_ref, bf16[128,1024]{1,0:T(8,128)(2,1)S(1)} %collective-permute-done.5.far_ref), custom_call_target="tpu_custom_call" | custom-call | bytes 1048576 | tf_op jit(solution)/shard_map/pallas_call | solution.py:61
  76.2 0.0 collective-permute-done.25.refs_4_
  76.2 0.4 collective-permute-done.28.refs_7_
  76.6 0.9 %shard_map.164 = (f32[16,4096]{1,0:T(8,128)}, f32[16,2048]{1,0:T(8,128)}, f32[16,4096]{1,0:T(8,128)}, f32[16,512]{1,0:T(8,128)}) custom-call(bf16[16,2432]{1,0:T(8,128)(2,1)S(1)} %add_convert_fusion.2.refs_0_, bf16[16,2432]{1,0:T(8,128)(2,1)S(1)} %collective-permute-done.22.refs_1_, bf16[16,2432]{1,0:T(8,128)(2,1)S(1)} %collective-permute-done.23.refs_2_, ...), custom_call_target="tpu_custom_call" | custom-call | bytes 1310720 | tf_op jit(solution)/shard_map/pallas_call | solution.py:61
  77.5 0.7 shard_map.161
  (30 shorter events, 0.1 us)
Async XLA Ops:
  3.4 5.5 %collective-permute-start = (bf16[136,512]{1,0:T(8,128)(2,1)}, bf16[136,512]{1,0:T(8,128)(2,1)S(1)}, u32[]{:S(2)}, u32[]{:S(2)}) collective-permute-start(bf16[136,512]{1,0:T(8,128)(2,1)} %get-tuple-element.44), channel_id=1, source_target_pairs={{0,1},{1,0},{2,3},{3,2},{4,5},{5,4},{6,7},{7,6},{8,9},{9,8},{10,11... | collective-permute-start | bytes 417800 | tf_op jit(solution)/shard_map/ppermute | solution.py:358
  4.0 1.2 %copy-start = (bf16[1,128,4096]{2,1,0:T(8,128)(2,1)S(1)}, bf16[1,128,4096]{2,1,0:T(8,128)(2,1)}, u32[]{:S(2)}) copy-start(bf16[1,128,4096]{2,1,0:T(8,128)(2,1)} %param.14) | copy-start | bytes 3145732
  5.2 1.0 %copy-start.2 = (bf16[1,128,2048]{2,1,0:T(8,128)(2,1)S(1)}, bf16[1,128,2048]{2,1,0:T(8,128)(2,1)}, u32[]{:S(2)}) copy-start(bf16[1,128,2048]{2,1,0:T(8,128)(2,1)} %param.10) | copy-start | bytes 1572868
  6.3 1.0 %copy-start.4 = (bf16[1,128,2048]{2,1,0:T(8,128)(2,1)S(1)}, bf16[1,128,2048]{2,1,0:T(8,128)(2,1)}, u32[]{:S(2)}) copy-start(bf16[1,128,2048]{2,1,0:T(8,128)(2,1)} %param.13) | copy-start | bytes 1572868
  7.3 13.9 %copy-start.1 = (bf16[1,128,4096]{2,1,0:T(8,128)(2,1)S(1)}, bf16[1,128,4096]{2,1,0:T(8,128)(2,1)}, u32[]{:S(2)}) copy-start(bf16[1,128,4096]{2,1,0:T(8,128)(2,1)} %param.14) | copy-start | bytes 3145732
  7.3 20.6 %copy-start.3 = (bf16[1,128,2048]{2,1,0:T(8,128)(2,1)S(1)}, bf16[1,128,2048]{2,1,0:T(8,128)(2,1)}, u32[]{:S(2)}) copy-start(bf16[1,128,2048]{2,1,0:T(8,128)(2,1)} %param.10) | copy-start | bytes 1572868
  7.3 20.6 %copy-start.5 = (bf16[1,128,2048]{2,1,0:T(8,128)(2,1)S(1)}, bf16[1,128,2048]{2,1,0:T(8,128)(2,1)}, u32[]{:S(2)}) copy-start(bf16[1,128,2048]{2,1,0:T(8,128)(2,1)} %param.13) | copy-start | bytes 1572868
  7.3 20.6 %copy-start.8 = (s32[1,16]{1,0:T(1,128)S(1)}, s32[1,16]{1,0:T(1,128)}, u32[]{:S(2)}) copy-start(s32[1,16]{1,0:T(1,128)} %refs_0_.1) | copy-start | bytes 196
  7.4 20.4 %collective-permute-start.1 = (bf16[128,2048]{1,0:T(8,128)(2,1)S(1)}, bf16[128,2048]{1,0:T(8,128)(2,1)S(1)}, u32[]{:S(2)}, u32[]{:S(2)}) collective-permute-start(bf16[128,2048]{1,0:T(8,128)(2,1)S(1)} %get-tuple-element.45), channel_id=1, source_target_pairs={{0,1},{1,0},{2,3},{3,2},{4,5},{5,4},{6,7},{7,6},{8,9},{9,8},{10,11... | collective-permute-start | bytes 1572872 | tf_op jit(solution)/shard_map/ppermute | solution.py:358
  7.5 13.7 %collective-permute-start.17 = (bf16[128,2048]{1,0:T(8,128)(2,1)S(1)}, bf16[128,2048]{1,0:T(8,128)(2,1)S(1)}, u32[]{:S(2)}, u32[]{:S(2)}) collective-permute-start(bf16[128,2048]{1,0:T(8,128)(2,1)S(1)} %get-tuple-element.72), channel_id=1, source_target_pairs={{0,1},{1,0},{2,3},{3,2},{4,5},{5,4},{6,7},{7,6},{8,9},{9,8},{10,11... | collective-permute-start | bytes 1572872 | tf_op jit(solution)/shard_map/ppermute | solution.py:358
  8.9 12.3 %collective-permute-start.2 = (bf16[272,512]{1,0:T(8,128)(2,1)S(1)}, bf16[272,512]{1,0:T(8,128)(2,1)S(1)}, u32[]{:S(2)}, u32[]{:S(2)}) collective-permute-start(bf16[272,512]{1,0:T(8,128)(2,1)S(1)} %constant_dynamic-update-slice_fusion.kv_ref.refs_5_), channel_id=1, source_target_pairs={{0,2},{1,3},{2,4},{3,5},{4,6},{5,7},{6,0},{7,1},{8,10},{9,11},{10,... | collective-permute-start | bytes 835592 | tf_op jit(solution)/shard_map/ppermute | solution.py:361
  11.6 19.0 %collective-permute-start.4 = (bf16[272,512]{1,0:T(8,128)(2,1)S(1)}, bf16[272,512]{1,0:T(8,128)(2,1)S(1)}, u32[]{:S(2)}, u32[]{:S(2)}) collective-permute-start(bf16[272,512]{1,0:T(8,128)(2,1)S(1)} %constant_dynamic-update-slice_fusion.kv_ref.refs_5_), channel_id=1, source_target_pairs={{0,6},{1,7},{2,0},{3,1},{4,2},{5,3},{6,4},{7,5},{8,14},{9,15},{10,... | collective-permute-start | bytes 835592 | tf_op jit(solution)/shard_map/ppermute | solution.py:361
  21.2 14.8 %collective-permute-start.3 = (bf16[272,512]{1,0:T(8,128)(2,1)S(1)}, bf16[272,512]{1,0:T(8,128)(2,1)S(1)}, u32[]{:S(2)}, u32[]{:S(2)}) collective-permute-start(bf16[272,512]{1,0:T(8,128)(2,1)S(1)} %collective-permute-done.2.kv_ref.refs_6_), channel_id=1, source_target_pairs={{0,2},{1,3},{2,4},{3,5},{4,6},{5,7},{6,0},{7,1},{8,10},{9,11},{10,... | collective-permute-start | bytes 835592 | tf_op jit(solution)/shard_map/ppermute | solution.py:361
  21.3 32.2 %collective-permute-start.18 = (bf16[256,1024]{1,0:T(8,128)(2,1)S(1)}, bf16[256,1024]{1,0:T(8,128)(2,1)S(1)}, u32[]{:S(2)}, u32[]{:S(2)}) collective-permute-start(bf16[256,1024]{1,0:T(8,128)(2,1)S(1)} %get-tuple-element.74), channel_id=1, source_target_pairs={{0,2},{1,3},{2,0},{3,1},{4,6},{5,7},{6,4},{7,5},{8,10},{9,11},{10,... | collective-permute-start | bytes 1572872 | tf_op jit(solution)/shard_map/ppermute | solution.py:370
  30.0 6.7 %copy-start.6 = (bf16[16,2048]{1,0:T(8,128)(2,1)S(1)}, bf16[16,2048]{1,0:T(8,128)(2,1)}, u32[]{:S(2)}) copy-start(bf16[16,2048]{1,0:T(8,128)(2,1)} %refs_3_.1) | copy-start | bytes 196612
  30.0 6.6 %copy-start.7 = (bf16[16,512]{1,0:T(8,128)(2,1)S(1)}, bf16[16,512]{1,0:T(8,128)(2,1)}, u32[]{:S(2)}) copy-start(bf16[16,512]{1,0:T(8,128)(2,1)} %refs_4_.1) | copy-start | bytes 49156
  39.3 18.9 %collective-permute-start.6 = (bf16[256,512]{1,0:T(8,128)(2,1)S(1)}, bf16[256,512]{1,0:T(8,128)(2,1)S(1)}, u32[]{:S(2)}, u32[]{:S(2)}) collective-permute-start(bf16[256,512]{1,0:T(8,128)(2,1)S(1)} %get-tuple-element.62), channel_id=1, source_target_pairs={{0,6},{1,7},{2,0},{3,1},{4,2},{5,3},{6,4},{7,5},{8,14},{9,15},{10,... | collective-permute-start | bytes 786440 | tf_op jit(solution)/shard_map/ppermute | solution.py:361
  45.2 5.9 %collective-permute-start.10 = (bf16[16,1152]{1,0:T(8,128)(2,1)S(1)}, bf16[16,1152]{1,0:T(8,128)(2,1)S(1)}, u32[]{:S(2)}, u32[]{:S(2)}) collective-permute-start(bf16[16,1152]{1,0:T(8,128)(2,1)S(1)} %get-tuple-element.69), channel_id=1, source_target_pairs={{0,2},{1,3},{2,0},{3,1},{4,6},{5,7},{6,4},{7,5},{8,10},{9,11},{10,... | collective-permute-start | bytes 110600 | tf_op jit(solution)/shard_map/ppermute | solution.py:370
  45.2 5.9 %collective-permute-start.11 = (bf16[16,1152]{1,0:T(8,128)(2,1)S(1)}, bf16[16,1152]{1,0:T(8,128)(2,1)S(1)}, u32[]{:S(2)}, u32[]{:S(2)}) collective-permute-start(bf16[16,1152]{1,0:T(8,128)(2,1)S(1)} %get-tuple-element.70), channel_id=1, source_target_pairs={{0,4},{1,5},{2,6},{3,7},{4,0},{5,1},{6,2},{7,3},{8,12},{9,13},{10,... | collective-permute-start | bytes 110600 | tf_op jit(solution)/shard_map/ppermute | solution.py:370
  45.8 6.3 %collective-permute-start.12 = (bf16[16,1152]{1,0:T(8,128)(2,1)S(1)}, bf16[16,1152]{1,0:T(8,128)(2,1)S(1)}, u32[]{:S(2)}, u32[]{:S(2)}) collective-permute-start(bf16[16,1152]{1,0:T(8,128)(2,1)S(1)} %get-tuple-element.71), channel_id=1, source_target_pairs={{0,6},{1,7},{2,4},{3,5},{4,2},{5,3},{6,0},{7,1},{8,14},{9,15},{10,... | collective-permute-start | bytes 110600 | tf_op jit(solution)/shard_map/ppermute | solution.py:370
  51.1 1.2 %collective-permute-start.13 = (bf16[16,1152]{1,0:T(8,128)(2,1)S(1)}, bf16[16,1152]{1,0:T(8,128)(2,1)S(1)}, u32[]{:S(2)}, u32[]{:S(2)}) collective-permute-start(bf16[16,1152]{1,0:T(8,128)(2,1)S(1)} %get-tuple-element.68.refs_0_), channel_id=1, source_target_pairs={{0,1},{1,0},{2,3},{3,2},{4,5},{5,4},{6,7},{7,6},{8,9},{9,8},{10,11... | collective-permute-start | bytes 110600 | tf_op jit(solution)/shard_map/ppermute | solution.py:358
  51.1 1.5 %collective-permute-start.14 = (bf16[16,1152]{1,0:T(8,128)(2,1)S(1)}, bf16[16,1152]{1,0:T(8,128)(2,1)S(1)}, u32[]{:S(2)}, u32[]{:S(2)}) collective-permute-start(bf16[16,1152]{1,0:T(8,128)(2,1)S(1)} %collective-permute-done.10.refs_1_), channel_id=1, source_target_pairs={{0,1},{1,0},{2,3},{3,2},{4,5},{5,4},{6,7},{7,6},{8,9},{9,8},{10,11... | collective-permute-start | bytes 110600 | tf_op jit(solution)/shard_map/ppermute | solution.py:358
  52.1 1.4 %collective-permute-start.15 = (bf16[16,1152]{1,0:T(8,128)(2,1)S(1)}, bf16[16,1152]{1,0:T(8,128)(2,1)S(1)}, u32[]{:S(2)}, u32[]{:S(2)}) collective-permute-start(bf16[16,1152]{1,0:T(8,128)(2,1)S(1)} %collective-permute-done.11.refs_2_), channel_id=1, source_target_pairs={{0,1},{1,0},{2,3},{3,2},{4,5},{5,4},{6,7},{7,6},{8,9},{9,8},{10,11... | collective-permute-start | bytes 110600 | tf_op jit(solution)/shard_map/ppermute | solution.py:358
  52.3 1.2 %collective-permute-start.16 = (bf16[16,1152]{1,0:T(8,128)(2,1)S(1)}, bf16[16,1152]{1,0:T(8,128)(2,1)S(1)}, u32[]{:S(2)}, u32[]{:S(2)}) collective-permute-start(bf16[16,1152]{1,0:T(8,128)(2,1)S(1)} %collective-permute-done.12.refs_3_), channel_id=1, source_target_pairs={{0,1},{1,0},{2,3},{3,2},{4,5},{5,4},{6,7},{7,6},{8,9},{9,8},{10,11... | collective-permute-start | bytes 110600 | tf_op jit(solution)/shard_map/ppermute | solution.py:358
  52.6 14.8 %collective-permute-start.8 = (bf16[256,512]{1,0:T(8,128)(2,1)S(1)}, bf16[256,512]{1,0:T(8,128)(2,1)S(1)}, u32[]{:S(2)}, u32[]{:S(2)}) collective-permute-start(bf16[256,512]{1,0:T(8,128)(2,1)S(1)} %get-tuple-element.65), channel_id=1, source_target_pairs={{0,2},{1,3},{2,4},{3,5},{4,6},{5,7},{6,0},{7,1},{8,10},{9,11},{10,... | collective-permute-start | bytes 786440 | tf_op jit(solution)/shard_map/ppermute | solution.py:361
  53.5 16.2 %collective-permute-start.5 = (bf16[128,1024]{1,0:T(8,128)(2,1)S(1)}, bf16[128,1024]{1,0:T(8,128)(2,1)S(1)}, u32[]{:S(2)}, u32[]{:S(2)}) collective-permute-start(bf16[128,1024]{1,0:T(8,128)(2,1)S(1)} %get-tuple-element.61), channel_id=1, source_target_pairs={{0,1},{1,0},{2,3},{3,2},{4,5},{5,4},{6,7},{7,6},{8,9},{9,8},{10,11... | collective-permute-start | bytes 786440 | tf_op jit(solution)/shard_map/ppermute | solution.py:358
  53.9 5.7 %collective-permute-start.19 = (bf16[16,2432]{1,0:T(8,128)(2,1)S(1)}, bf16[16,2432]{1,0:T(8,128)(2,1)S(1)}, u32[]{:S(2)}, u32[]{:S(2)}) collective-permute-start(bf16[16,2432]{1,0:T(8,128)(2,1)S(1)} %shard_map.163), channel_id=1, source_target_pairs={{0,8},{8,0},{16,24},{24,16},{1,9},{9,1},{17,25},{25,17},{2,10},{10... | collective-permute-start | bytes 233480 | tf_op jit(solution)/shard_map/ppermute | solution.py:367
  56.7 6.1 %collective-permute-start.20 = (bf16[16,2432]{1,0:T(8,128)(2,1)S(1)}, bf16[16,2432]{1,0:T(8,128)(2,1)S(1)}, u32[]{:S(2)}, u32[]{:S(2)}) collective-permute-start(bf16[16,2432]{1,0:T(8,128)(2,1)S(1)} %shard_map.163), channel_id=1, source_target_pairs={{0,16},{8,24},{16,0},{24,8},{1,17},{9,25},{17,1},{25,9},{2,18},{10... | collective-permute-start | bytes 233480 | tf_op jit(solution)/shard_map/ppermute | solution.py:367
  58.2 5.3 %collective-permute-start.21 = (bf16[16,2432]{1,0:T(8,128)(2,1)S(1)}, bf16[16,2432]{1,0:T(8,128)(2,1)S(1)}, u32[]{:S(2)}, u32[]{:S(2)}) collective-permute-start(bf16[16,2432]{1,0:T(8,128)(2,1)S(1)} %shard_map.163), channel_id=1, source_target_pairs={{0,24},{8,16},{16,8},{24,0},{1,25},{9,17},{17,9},{25,1},{2,26},{10... | collective-permute-start | bytes 233480 | tf_op jit(solution)/shard_map/ppermute | solution.py:367
  59.6 9.9 %collective-permute-start.7 = (bf16[256,512]{1,0:T(8,128)(2,1)S(1)}, bf16[256,512]{1,0:T(8,128)(2,1)S(1)}, u32[]{:S(2)}, u32[]{:S(2)}) collective-permute-start(bf16[256,512]{1,0:T(8,128)(2,1)S(1)} %add_convert_fusion.1), channel_id=1, source_target_pairs={{0,6},{1,7},{2,0},{3,1},{4,2},{5,3},{6,4},{7,5},{8,14},{9,15},{10,... | collective-permute-start | bytes 786440 | tf_op jit(solution)/shard_map/ppermute | solution.py:361
  63.5 8.1 %collective-permute-start.22 = (bf16[16,2432]{1,0:T(8,128)(2,1)S(1)}, bf16[16,2432]{1,0:T(8,128)(2,1)S(1)}, u32[]{:S(2)}, u32[]{:S(2)}) collective-permute-start(bf16[16,2432]{1,0:T(8,128)(2,1)S(1)} %add_convert_fusion.2.refs_0_), channel_id=1, source_target_pairs={{0,2},{1,3},{2,0},{3,1},{4,6},{5,7},{6,4},{7,5},{8,10},{9,11},{10,... | collective-permute-start | bytes 233480 | tf_op jit(solution)/shard_map/ppermute | solution.py:370
  65.2 7.3 %collective-permute-start.23 = (bf16[16,2432]{1,0:T(8,128)(2,1)S(1)}, bf16[16,2432]{1,0:T(8,128)(2,1)S(1)}, u32[]{:S(2)}, u32[]{:S(2)}) collective-permute-start(bf16[16,2432]{1,0:T(8,128)(2,1)S(1)} %add_convert_fusion.2.refs_0_), channel_id=1, source_target_pairs={{0,4},{1,5},{2,6},{3,7},{4,0},{5,1},{6,2},{7,3},{8,12},{9,13},{10,... | collective-permute-start | bytes 233480 | tf_op jit(solution)/shard_map/ppermute | solution.py:370
  67.4 7.9 %collective-permute-start.24 = (bf16[16,2432]{1,0:T(8,128)(2,1)S(1)}, bf16[16,2432]{1,0:T(8,128)(2,1)S(1)}, u32[]{:S(2)}, u32[]{:S(2)}) collective-permute-start(bf16[16,2432]{1,0:T(8,128)(2,1)S(1)} %add_convert_fusion.2.refs_0_), channel_id=1, source_target_pairs={{0,6},{1,7},{2,4},{3,5},{4,2},{5,3},{6,0},{7,1},{8,14},{9,15},{10,... | collective-permute-start | bytes 233480 | tf_op jit(solution)/shard_map/ppermute | solution.py:370
  69.6 7.9 %collective-permute-start.9 = (bf16[128,512]{1,0:T(8,128)(2,1)S(1)}, bf16[128,512]{1,0:T(8,128)(2,1)S(1)}, u32[]{:S(2)}, u32[]{:S(2)}) collective-permute-start(bf16[128,512]{1,0:T(8,128)(2,1)S(1)} %slice.4), channel_id=1, source_target_pairs={{0,1},{1,0},{2,3},{3,2},{4,5},{5,4},{6,7},{7,6},{8,9},{9,8},{10,11... | collective-permute-start | bytes 393224 | tf_op jit(solution)/shard_map/ppermute | solution.py:358
  69.7 6.4 %collective-permute-start.25 = (bf16[16,2432]{1,0:T(8,128)(2,1)S(1)}, bf16[16,2432]{1,0:T(8,128)(2,1)S(1)}, u32[]{:S(2)}, u32[]{:S(2)}) collective-permute-start(bf16[16,2432]{1,0:T(8,128)(2,1)S(1)} %add_convert_fusion.2.refs_0_), channel_id=1, source_target_pairs={{0,1},{1,0},{2,3},{3,2},{4,5},{5,4},{6,7},{7,6},{8,9},{9,8},{10,11... | collective-permute-start | bytes 233480 | tf_op jit(solution)/shard_map/ppermute | solution.py:358
  71.6 4.6 %collective-permute-start.26 = (bf16[16,2432]{1,0:T(8,128)(2,1)S(1)}, bf16[16,2432]{1,0:T(8,128)(2,1)S(1)}, u32[]{:S(2)}, u32[]{:S(2)}) collective-permute-start(bf16[16,2432]{1,0:T(8,128)(2,1)S(1)} %collective-permute-done.22.refs_1_), channel_id=1, source_target_pairs={{0,1},{1,0},{2,3},{3,2},{4,5},{5,4},{6,7},{7,6},{8,9},{9,8},{10,11... | collective-permute-start | bytes 233480 | tf_op jit(solution)/shard_map/ppermute | solution.py:358
  72.5 3.7 %collective-permute-start.27 = (bf16[16,2432]{1,0:T(8,128)(2,1)S(1)}, bf16[16,2432]{1,0:T(8,128)(2,1)S(1)}, u32[]{:S(2)}, u32[]{:S(2)}) collective-permute-start(bf16[16,2432]{1,0:T(8,128)(2,1)S(1)} %collective-permute-done.23.refs_2_), channel_id=1, source_target_pairs={{0,1},{1,0},{2,3},{3,2},{4,5},{5,4},{6,7},{7,6},{8,9},{9,8},{10,11... | collective-permute-start | bytes 233480 | tf_op jit(solution)/shard_map/ppermute | solution.py:358
  75.3 1.3 %collective-permute-start.28 = (bf16[16,2432]{1,0:T(8,128)(2,1)S(1)}, bf16[16,2432]{1,0:T(8,128)(2,1)S(1)}, u32[]{:S(2)}, u32[]{:S(2)}) collective-permute-start(bf16[16,2432]{1,0:T(8,128)(2,1)S(1)} %collective-permute-done.24.refs_3_), channel_id=1, source_target_pairs={{0,1},{1,0},{2,3},{3,2},{4,5},{5,4},{6,7},{7,6},{8,9},{9,8},{10,11... | collective-permute-start | bytes 233480 | tf_op jit(solution)/shard_map/ppermute | solution.py:358

commit v2 on v1

--- a/solution.py
+++ b/solution.py
@@ -150,49 +150,47 @@
             out[g, first + rows : first + 2 * rows] = pack_ref[:, far]
 
 
-def key_rows(kv_ref, rows, columns):
-    block_rows = kv_ref.shape[0] // 2
-    halves = [kv_ref[first : first + rows, columns] for first in (0, block_rows)]
-    return jnp.concatenate(halves, axis=0)
+def key_rows(halves, rows, columns):
+    return jnp.concatenate([ref[:rows, columns] for ref in halves], axis=0)
 
 
 def head_parts(chip_rows):
     return [slice(j * chip_rows, (j + 1) * chip_rows) for j in range(GROUP)]
 
 
-def chunk_scores(k, rows, lens_ref, kv_ref, *refs):
+def chunk_scores(k, rows, lens_ref, *refs):
+    kv_ref, refs = refs[:2], refs[2:]
     if k == 0:
         stack_heads(*refs[:3], *refs[6:8])
         (e_ref, dp_ref, stats_ref), (qs_ref, gs_ref) = refs[3:6], refs[6:8]
     else:
         qs_ref, gs_ref, e_ref, dp_ref, stats_ref = refs
     places = Places(lens_ref, rows)
-    head_scale = HEAD_WIDTH ** (-0.5)
+    scale = HEAD_WIDTH ** (-0.5) * math.log2(math.e)
 
     @pl.when(k < places.seen)
     def _():
         visible = places.visible(k)
 
-        def one_group(g, _):
-            keys = key_rows(kv_ref, rows, pl.ds(pl.multiple_of(g * HEAD_WIDTH, 128), HEAD_WIDTH))
-            values = key_rows(kv_ref, rows, pl.ds(pl.multiple_of(KV_HALF + g * HEAD_WIDTH, 128), HEAD_WIDTH))
+        for g in range(CORE_HEADS):
+            keys = key_rows(kv_ref, rows, slice(g * HEAD_WIDTH, (g + 1) * HEAD_WIDTH))
+            values = key_rows(kv_ref, rows, slice(KV_HALF + g * HEAD_WIDTH, KV_HALF + (g + 1) * HEAD_WIDTH))
             for part in head_parts(2 * rows):
-                s = dot_nt(keys, qs_ref[g, part]) * head_scale
+                s = dot_nt(keys, qs_ref[g, part]) * scale
                 s = jnp.where(visible, s, NEG_FILL)
                 top = jnp.max(s, axis=0, keepdims=True)
-                e = jnp.exp(s - top)
+                e = jnp.exp2(s - top)
                 dp = dot_nt(values, gs_ref[g, part])
                 e_ref[g, :, part] = e.astype(e_ref.dtype)
                 dp_ref[g, :, part] = dp.astype(dp_ref.dtype)
                 stats_ref[g, 0:1, part] = top
                 stats_ref[g, 1:2, part] = jnp.sum(e, axis=0, keepdims=True)
                 stats_ref[g, 2:3, part] = jnp.sum(e * dp, axis=0, keepdims=True)
-            return 0
-
-        lax.fori_loop(0, CORE_HEADS, one_group, 0)
 
     @pl.when(k >= places.seen)
     def _():
+        e_ref[...] = jnp.zeros_like(e_ref)
+        dp_ref[...] = jnp.zeros_like(dp_ref)
         stats_ref[:, 0:1] = jnp.full_like(stats_ref[:, 0:1], NEG_FILL)
         stats_ref[:, 1:3] = jnp.zeros_like(stats_ref[:, 1:3])
 
@@ -200,8 +198,10 @@
 def gradients(n_chips, rank, rows, tail, *refs):
     lens_ref, qs, gs, qb_ref, vb_ref = refs[:5]
     refs = refs[5:]
-    kv, e_in, dp_in, stats = (refs[i * n_chips : (i + 1) * n_chips] for i in range(4))
-    refs = refs[4 * n_chips :]
+    kv = [refs[2 * i : 2 * i + 2] for i in range(n_chips)]
+    refs = refs[2 * n_chips :]
+    e_in, dp_in, stats = (refs[i * n_chips : (i + 1) * n_chips] for i in range(3))
+    refs = refs[3 * n_chips :]
     dq_own_ref, dq_send_ref = refs[:2]
     dkv = refs[2 : 2 + n_chips]
     message_out = refs[2 + n_chips : 2 + 2 * n_chips]
@@ -210,21 +210,13 @@
     core, chip, chip_rows = places.core, places.chip, places.chip_rows
     head_scale = HEAD_WIDTH ** (-0.5)
     parts = head_parts(chip_rows)
-    block_rows = kv[0].shape[0] // 2
 
     for k in range(n_chips):
         for side in (0, 1):
-            first = side * block_rows + rows
             for i in range(2 * rank // 8):
-                proj[k, 8 * i : 8 * i + 8, side * rows : (side + 1) * rows] = kv[k][
-                    first : first + 8, i * rows : (i + 1) * rows
+                proj[k, 8 * i : 8 * i + 8, side * rows : (side + 1) * rows] = kv[k][side][
+                    rows:, i * rows : (i + 1) * rows
                 ]
-        if k:
-
-            @pl.when(k >= places.seen)
-            def _():
-                dkv[k][...] = jnp.zeros_like(dkv[k])
-
     vl[...] = jnp.zeros_like(vl)
     low_ref[...] = jnp.zeros_like(low_ref)
     ups[...] = jnp.zeros_like(ups)
@@ -233,27 +225,29 @@
         at_k = pl.ds(pl.multiple_of(g * HEAD_WIDTH, 128), HEAD_WIDTH)
         at_v = pl.ds(pl.multiple_of(KV_HALF + g * HEAD_WIDTH, 128), HEAD_WIDTH)
         top = functools.reduce(jnp.maximum, [ref[g, 0:1] for ref in stats])
-        weight = [jnp.exp(ref[g, 0:1] - top) for ref in stats]
+        weight = [jnp.exp2(ref[g, 0:1] - top) for ref in stats]
         inverse = 1.0 / sum(ref[g, 1:2] * w for ref, w in zip(stats, weight))
         delta = sum(ref[g, 2:3] * w for ref, w in zip(stats, weight)) * inverse
-        dqt[...] = jnp.zeros_like(dqt)
+        at_b = pl.multiple_of(core * KV_HALF + g * HEAD_WIDTH, 128)
         for k in range(n_chips):
-
-            @pl.when(k < places.seen)
-            def _():
-                factor = weight[k] * inverse
-                for part in parts:
-                    p = e_in[k][g, :, part].astype(F32) * factor[:, part]
-                    p_ref[:, part] = p.astype(BF16)
-                    ds = p * (dp_in[k][g, :, part].astype(F32) - delta[:, part]) * head_scale
-                    ds_ref[:, part] = ds.astype(BF16)
-                ds = ds_ref[...]
-                dv = dot_nn(p_ref[...], gs[g]).astype(BF16)
-                dkv[k][:, at_k] = dot_nn(ds, qs[g]).astype(BF16)
-                dkv[k][:, at_v] = dv
+            factor = weight[k] * inverse
+            slot = k % 2
+            for part in parts:
+                p = e_in[k][g, :, part].astype(F32) * factor[:, part]
+                p_ref[slot, :, part] = p.astype(BF16)
+                ds = p * (dp_in[k][g, :, part].astype(F32) - delta[:, part])
+                ds_ref[slot, :, part] = ds.astype(BF16)
+            ds = ds_ref[slot]
+            dv = dot_nn(p_ref[slot], gs[g]).astype(BF16)
+            dkv[k][:, at_k] = (dot_nn(ds, qs[g]) * head_scale).astype(BF16)
+            dkv[k][:, at_v] = dv
+            if k == 0:
+                dqt[...] = dot_tn(key_rows(kv[k], rows, at_k), ds)
+            else:
                 dqt[...] += dot_tn(key_rows(kv[k], rows, at_k), ds)
-                at_b = pl.multiple_of(core * KV_HALF + g * HEAD_WIDTH, 128)
-                vl[chip - k] += dot_nt(vb_ref[:, pl.ds(at_b, HEAD_WIDTH)], dv)
+            low = dot_nt(vb_ref[:, pl.ds(at_b, HEAD_WIDTH)], dv)
+            vl[(chip - k + n_chips) % n_chips] += low
+        dqt[...] *= head_scale
 
         at_b = pl.multiple_of(core * Q_HALF + g * GROUP * HEAD_WIDTH, 128)
         for j, part in enumerate(parts):
@@ -267,11 +261,10 @@
         return 0
 
     lax.fori_loop(0, CORE_HEADS, one_group, 0)
+    total = jnp.zeros((rank, KV_HALF), F32)
     for k in range(n_chips):
-
-        @pl.when(k < places.seen)
-        def _():
-            ups[:, Q_HALF : Q_HALF + KV_HALF] += dot_nn(proj[k, rank:], dkv[k][:, KV_HALF:])
+        total = total + dot_nn(proj[k, rank:], dkv[k][:, KV_HALF:])
+    ups[:, Q_HALF : Q_HALF + KV_HALF] = total
 
     for k in range(n_chips):
         message_out[k][:, :chip_rows] = low_ref[...].astype(BF16)
@@ -383,12 +376,16 @@
         hbm=range(5),
         limit=VMEM_MOST - (3 << 17),
     )
-    kv = [jnp.concatenate([kv_own, swap(kv_send)], axis=0)]
-    if n_chips > 1:
-        last = up(kv[0], n_chips - 1)
-        for _ in range(1, n_chips - 1):
-            kv.append(up(kv[-1], 1))
-        kv.append(last)
+    kv = []
+    for block in (kv_own, swap(kv_send)):
+        chain = [block]
+        if n_chips > 1:
+            last = up(block, n_chips - 1)
+            for _ in range(1, n_chips - 1):
+                chain.append(up(chain[-1], 1))
+            chain.append(last)
+        kv.append(chain)
+    kv = list(zip(*kv))
 
     pack, hidden_far = call(
         split_rest,
@@ -409,13 +406,13 @@
     *chunks[0], qs, gs = call(
         functools.partial(chunk_scores, 0, rows),
         chunk + [stacked] * 2,
-        (doc_lengths, kv[0], q, g, pack),
+        (doc_lengths, *kv[0], q, g, pack),
         flops=work,
         smem=(0,),
     )
     for c in range(1, n_chips):
         chunks[c] = call(
-            functools.partial(chunk_scores, c, rows), chunk, (doc_lengths, kv[c], qs, gs), flops=work, smem=(0,)
+            functools.partial(chunk_scores, c, rows), chunk, (doc_lengths, *kv[c], qs, gs), flops=work, smem=(0,)
         )
     outs = (
         [sds((rows, Q_HALF), BF16)] * 2
@@ -425,12 +422,12 @@
     result = call(
         functools.partial(gradients, n_chips, rank, rows, tail),
         outs,
-        (doc_lengths, qs, gs, queryb, valueb, *kv, *(c[i] for i in range(3) for c in chunks)),
+        (doc_lengths, qs, gs, queryb, valueb, *sum(kv, ()), *(c[i] for i in range(3) for c in chunks)),
         scratch=[
             pltpu.VMEM((n_chips, 2 * rank, chip_rows), BF16),
             pltpu.VMEM((n_chips, rank, chip_rows), F32),
-            pltpu.VMEM((chip_rows, lanes), BF16),
-            pltpu.VMEM((chip_rows, lanes), BF16),
+            pltpu.VMEM((2, chip_rows, lanes), BF16),
+            pltpu.VMEM((2, chip_rows, lanes), BF16),
             pltpu.VMEM((HEAD_WIDTH, lanes), F32),
             pltpu.VMEM((rank, tail * n_chips), F32),
             pltpu.VMEM((rank, chip_rows), F32),

time: 78.5 us -> 79 us (level)
  starting transfers between devices: 36.9 us -> 29.7 us
  Pallas kernels: 12.4 us -> 17.4 us
  local copies, waits for them, and re-layouts: 4.27 us -> 7.55 us
  waiting for transfers between devices: 23.6 us -> 22.8 us
    ppermute x7, starting transfers between devices: 15.4 us -> 10.5 us  [along(): return lax.ppermute(a, 'ctx', [(i, i ^ 2 * bit) for i in range(n_ctx)])]
    pallas_call x12, Pallas kernels: 12.4 us -> 17.4 us  [kernel_call(): pl.pallas_call(body, out_shape=outs, in_specs=[SM if i in smem else HB if...]
    ppermute x6 -> x9, waiting for transfers between devices: 13.7 us -> 10 us  [up(): lax.ppermute(a, 'ctx', [(i, (i + 2 * step) % n_ctx) for i in range(n_ctx)])]
    unnamed x19 -> x22, local copies, waits for them, and re-layouts: 4.25 us -> 7.54 us
    ppermute x7, waiting for transfers between devices: 7.11 us -> 10.2 us  [along(): return lax.ppermute(a, 'ctx', [(i, i ^ 2 * bit) for i in range(n_ctx)])]
    ppermute x6 -> x9, starting transfers between devices: 14.7 us -> 12.7 us  [up(): lax.ppermute(a, 'ctx', [(i, (i + 2 * step) % n_ctx) for i in range(n_ctx)])]
  transfers between devices with their start and end apart: 29 -> 32, of which waited for: 12 -> 10; matrix products, arithmetic and copies ran while one was open for 1% -> 0% of each run, Pallas kernels for 11% -> 20%
where the time goes in v2:
time: 79 us; the launch traced here: 78.4 us
  starting transfers between devices  29.7 us (38%)
  waiting for transfers between devices  22.8 us (29%)
  Pallas kernels  17.4 us (22%)
  local copies, waits for them, and re-layouts  7.55 us (10%)
  between operations  0.86 us (1%)
    pallas_call x12, Pallas kernels, kernel_call(): pl.pallas_call(body, out_shape=outs, in_specs=[SM if i in smem else HB if...  17.4 us
    ppermute x9, starting transfers between devices, up(): lax.ppermute(a, 'ctx', [(i, (i + 2 * step) % n_ctx) for i in range(n_ctx)])  12.7 us
    ppermute x7, starting transfers between devices, along(): return lax.ppermute(a, 'ctx', [(i, i ^ 2 * bit) for i in range(n_ctx)])  10.5 us
    ppermute x7, waiting for transfers between devices, along(): return lax.ppermute(a, 'ctx', [(i, i ^ 2 * bit) for i in range(n_ctx)])  10.2 us
    ppermute x9, waiting for transfers between devices, up(): lax.ppermute(a, 'ctx', [(i, (i + 2 * step) % n_ctx) for i in range(n_ctx)])  10 us
    unnamed x22, local copies, waits for them, and re-layouts  7.54 us
    ppermute x3, starting transfers between devices, across(): return lax.ppermute(a, 'dp', [(i, i ^ bit) for i in range(n_dp)])  3.54 us
    ppermute x13, starting transfers between devices, swap(): return lax.ppermute(a, 'ctx', [(i, i ^ 1) for i in range(n_ctx)])  2.95 us
  transfers between devices with their start and end apart: 32, of which 10 were waited for; matrix products, arithmetic and copies ran while one was open for 0% of the time, Pallas kernels for 20%

profile of v2, /device:TPU:0, one launch (start us, length us, event | category | flops | bytes accessed | tf_op | source)
XLA Modules:
  0.0 78.4 jit_solution(8376238775565808618)
XLA Ops:
  0.6 0.0 copy-start
  0.6 1.2 %copy-done = bf16[1,128,4096]{2,1,0:T(8,128)(2,1)S(1)} copy-done((bf16[1,128,4096]{2,1,0:T(8,128)(2,1)S(1)}, bf16[1,128,4096]{2,1,0:T(8,128)(2,1)}, u32[]{:S(2)}) %copy-start) | copy-done | bytes 1048600
  1.9 1.0 %copy-done.2 = bf16[1,128,2048]{2,1,0:T(8,128)(2,1)S(1)} copy-done((bf16[1,128,2048]{2,1,0:T(8,128)(2,1)S(1)}, bf16[1,128,2048]{2,1,0:T(8,128)(2,1)}, u32[]{:S(2)}) %copy-start.2) | copy-done | bytes 524312
  2.9 1.0 %copy-done.4 = bf16[1,128,2048]{2,1,0:T(8,128)(2,1)S(1)} copy-done((bf16[1,128,2048]{2,1,0:T(8,128)(2,1)S(1)}, bf16[1,128,2048]{2,1,0:T(8,128)(2,1)}, u32[]{:S(2)}) %copy-start.4) | copy-done | bytes 524312
  3.9 1.0 %shard_map.154 = (bf16[128,2048]{1,0:T(8,128)(2,1)}, bf16[128,2048]{1,0:T(8,128)(2,1)}) custom-call(bf16[128,2048]{1,0:T(8,128)(2,1)S(1)} %bitcast.11, bf16[128,2048]{1,0:T(8,128)(2,1)S(1)} %bitcast.13, bf16[128,4096]{1,0:T(8,128)(2,1)S(1)} %bitcast.9), custom_call_target="tpu_custom_call" | custom-call | bytes 3145728 | tf_op jit(solution)/shard_map/pallas_call | solution.py:61
  5.0 0.5 collective-permute-start.20
  5.5 0.0 collective-permute-start.1
  5.5 2.7 %shard_map.153 = (bf16[136,512]{1,0:T(8,128)(2,1)}, bf16[136,512]{1,0:T(8,128)(2,1)}) custom-call(bf16[128,512]{1,0:T(8,128)(2,1)} %bitcast.16, bf16[128,512]{1,0:T(8,128)(2,1)} %bitcast.17, bf16[128,4096]{1,0:T(8,128)(2,1)} %bitcast.8, bf16[16,4096]{1,0:T(8,128)(2,1)} %qa_hbm.1, bf16[16,4096]{1,0:T(8,128)(2,1)} %va_hbm.1), custom_call_target="tpu_custom_call" | custom-call | bytes 1851392 | tf_op jit(solution)/shard_map/pallas_call | solution.py:61
  8.2 0.6 collective-permute-start
  8.8 2.6 %collective-permute-start.2 = (bf16[136,512]{1,0:T(8,128)(2,1)}, bf16[136,512]{1,0:T(8,128)(2,1)S(1)}, u32[]{:S(2)}, u32[]{:S(2)}) collective-permute-start(bf16[136,512]{1,0:T(8,128)(2,1)} %get-tuple-element.43.refs_0_.refs_5_), channel_id=1, source_target_pairs={{0,2},{1,3},{2,4},{3,5},{4,6},{5,7},{6,0},{7,1},{8,10},{9,11},{10,... | collective-permute-start | bytes 417800 | tf_op jit(solution)/shard_map/ppermute | solution.py:354
  11.4 1.6 %collective-permute-start.3 = (bf16[136,512]{1,0:T(8,128)(2,1)S(1)}, bf16[136,512]{1,0:T(8,128)(2,1)S(1)}, u32[]{:S(2)}, u32[]{:S(2)}) collective-permute-start(bf16[136,512]{1,0:T(8,128)(2,1)S(1)} %collective-permute-done.refs_1_.refs_6_), channel_id=1, source_target_pairs={{0,2},{1,3},{2,4},{3,5},{4,6},{5,7},{6,0},{7,1},{8,10},{9,11},{10,... | collective-permute-start | bytes 417800 | tf_op jit(solution)/shard_map/ppermute | solution.py:354
  13.0 5.2 %collective-permute-done.2.refs_0_.refs_7_ = bf16[136,512]{1,0:T(8,128)(2,1)S(1)} collective-permute-done((bf16[136,512]{1,0:T(8,128)(2,1)}, bf16[136,512]{1,0:T(8,128)(2,1)S(1)}, u32[]{:S(2)}, u32[]{:S(2)}) %collective-permute-start.2) | collective-permute-done | bytes 139296 | tf_op jit(solution)/shard_map/ppermute | solution.py:354
  18.2 2.7 %collective-permute-done.3.refs_1_.refs_8_ = bf16[136,512]{1,0:T(8,128)(2,1)S(1)} collective-permute-done((bf16[136,512]{1,0:T(8,128)(2,1)S(1)}, bf16[136,512]{1,0:T(8,128)(2,1)S(1)}, u32[]{:S(2)}, u32[]{:S(2)}) %collective-permute-start.3) | collective-permute-done | bytes 139296 | tf_op jit(solution)/shard_map/ppermute | solution.py:354
  20.9 0.0 collective-permute-start.5
  20.9 3.8 %collective-permute-start.6 = (bf16[136,512]{1,0:T(8,128)(2,1)}, bf16[136,512]{1,0:T(8,128)(2,1)S(1)}, u32[]{:S(2)}, u32[]{:S(2)}) collective-permute-start(bf16[136,512]{1,0:T(8,128)(2,1)} %get-tuple-element.43.refs_0_.refs_5_), channel_id=1, source_target_pairs={{0,6},{1,7},{2,0},{3,1},{4,2},{5,3},{6,4},{7,5},{8,14},{9,15},{10,... | collective-permute-start | bytes 417800 | tf_op jit(solution)/shard_map/ppermute | solution.py:354
  24.7 0.5 collective-permute-start.7
  25.2 1.2 %copy-done.1 = bf16[1,128,4096]{2,1,0:T(8,128)(2,1)S(1)} copy-done((bf16[1,128,4096]{2,1,0:T(8,128)(2,1)S(1)}, bf16[1,128,4096]{2,1,0:T(8,128)(2,1)}, u32[]{:S(2)}) %copy-start.1) | copy-done | bytes 1048600
  26.4 1.1 %shard_map.162 = (bf16[256,1024]{1,0:T(8,128)(2,1)S(1)}, bf16[256,1024]{1,0:T(8,128)(2,1)S(1)}) custom-call(bf16[128,4096]{1,0:T(8,128)(2,1)S(1)} %bitcast.10, bf16[128,2048]{1,0:T(8,128)(2,1)} %collective-permute-done.20.far_ref), custom_call_target="tpu_custom_call" | custom-call | bytes 2621440 | tf_op jit(solution)/shard_map/pallas_call | solution.py:61
  27.5 1.6 %collective-permute-start.21 = (bf16[256,1024]{1,0:T(8,128)(2,1)S(1)}, bf16[256,1024]{1,0:T(8,128)(2,1)S(1)}, u32[]{:S(2)}, u32[]{:S(2)}) collective-permute-start(bf16[256,1024]{1,0:T(8,128)(2,1)S(1)} %get-tuple-element.74), channel_id=1, source_target_pairs={{0,2},{1,3},{2,0},{3,1},{4,6},{5,7},{6,4},{7,5},{8,10},{9,11},{10,... | collective-permute-start | bytes 1572872 | tf_op jit(solution)/shard_map/ppermute | solution.py:363
  29.2 1.0 %copy-done.3 = bf16[1,128,2048]{2,1,0:T(8,128)(2,1)S(1)} copy-done((bf16[1,128,2048]{2,1,0:T(8,128)(2,1)S(1)}, bf16[1,128,2048]{2,1,0:T(8,128)(2,1)}, u32[]{:S(2)}) %copy-start.3) | copy-done | bytes 524312
  30.2 1.0 %copy-done.5 = bf16[1,128,2048]{2,1,0:T(8,128)(2,1)S(1)} copy-done((bf16[1,128,2048]{2,1,0:T(8,128)(2,1)S(1)}, bf16[1,128,2048]{2,1,0:T(8,128)(2,1)}, u32[]{:S(2)}) %copy-start.5) | copy-done | bytes 524312
  31.3 0.9 %copy-done.6 = bf16[136,512]{1,0:T(8,128)(2,1)S(1)} copy-done((bf16[136,512]{1,0:T(8,128)(2,1)S(1)}, bf16[136,512]{1,0:T(8,128)(2,1)}, u32[]{:S(2)}) %copy-start.6) | copy-done | bytes 139288
  32.2 2.3 %shard_map.155 = (f32[2,256,1024]{2,1,0:T(8,128)S(1)}, f32[2,256,1024]{2,1,0:T(8,128)S(1)}, f32[2,8,1024]{2,1,0:T(8,128)S(1)}, bf16[2,1024,128]{2,1,0:T(8,128)(2,1)S(1)}, bf16[2,1024,128]{2,1,0:T(8,128)(2,1)S(1)}) custom-call(s32[1,16]{1,0:T(1,128)S(1)} %copy-done.10, bf16[136,512]{1,0:T(8,128)(2,1)S(1)} %copy-done.6, ...), custom_call_target="tpu_custom_call" | custom-call | flops 268435456 | bytes 7159872 | tf_op jit(solution)/shard_map/pallas_call | solution.py:61
  34.5 0.0 copy-start.7
  34.5 0.0 copy-start.8
  34.5 0.0 copy-start.9
  34.5 0.9 %shard_map.156 = (f32[2,256,1024]{2,1,0:T(8,128)S(1)}, f32[2,256,1024]{2,1,0:T(8,128)S(1)}, f32[2,8,1024]{2,1,0:T(8,128)S(1)}) custom-call(s32[1,16]{1,0:T(1,128)S(1)} %copy-done.10, bf16[136,512]{1,0:T(8,128)(2,1)S(1)} %collective-permute-done.2.refs_0_.refs_7_, bf16[136,512]{1,0:T(8,128)(2,1)S(1)} %collective-permute-done.3.refs_1_.refs_8_, ...), custom_call_target="tpu_custom_call" | custom-call | flops 268435456 | bytes 5587008 | tf_op jit(solution)/shard_map/pallas_call | solution.py:61
  35.4 0.9 %shard_map.157 = (f32[2,256,1024]{2,1,0:T(8,128)S(1)}, f32[2,256,1024]{2,1,0:T(8,128)S(1)}, f32[2,8,1024]{2,1,0:T(8,128)S(1)}) custom-call(s32[1,16]{1,0:T(1,128)S(1)} %copy-done.10, bf16[136,512]{1,0:T(8,128)(2,1)S(1)} %collective-permute-done.4.refs_0_.refs_9_, bf16[136,512]{1,0:T(8,128)(2,1)S(1)} %collective-permute-done.5.refs_1_.refs_10_, ...), custom_call_target="tpu_custom_call" | custom-call | flops 268435456 | bytes 5587008 | tf_op jit(solution)/shard_map/pallas_call | solution.py:61
  36.3 0.9 %shard_map.158 = (f32[2,256,1024]{2,1,0:T(8,128)S(1)}, f32[2,256,1024]{2,1,0:T(8,128)S(1)}, f32[2,8,1024]{2,1,0:T(8,128)S(1)}) custom-call(s32[1,16]{1,0:T(1,128)S(1)} %copy-done.10, bf16[136,512]{1,0:T(8,128)(2,1)S(1)} %collective-permute-done.6.refs_0_.refs_11_, bf16[136,512]{1,0:T(8,128)(2,1)S(1)} %collective-permute-done.7.refs_1_.refs_12_, ...), custom_call_target="tpu_custom_call" | custom-call | flops 268435456 | bytes 5587008 | tf_op jit(solution)/shard_map/pallas_call | solution.py:61
  37.2 4.7 %shard_map.159 = (bf16[128,1024]{1,0:T(8,128)(2,1)S(1)}, bf16[128,1024]{1,0:T(8,128)(2,1)S(1)}, bf16[256,512]{1,0:T(8,128)(2,1)S(1)}, bf16[256,512]{1,0:T(8,128)...) custom-call(s32[1,16]{1,0:T(1,128)S(1)} %copy-done.10, ...), custom_call_target="tpu_custom_call" | custom-call | flops 1610612736 | bytes 21004352 | tf_op jit(solution)/shard_map/pallas_call | solution.py:61
  42.0 0.7 collective-permute-start.9
  42.6 1.4 %collective-permute-start.13 = (bf16[16,1152]{1,0:T(8,128)(2,1)S(1)}, bf16[16,1152]{1,0:T(8,128)(2,1)S(1)}, u32[]{:S(2)}, u32[]{:S(2)}) collective-permute-start(bf16[16,1152]{1,0:T(8,128)(2,1)S(1)} %get-tuple-element.69), channel_id=1, source_target_pairs={{0,2},{1,3},{2,0},{3,1},{4,6},{5,7},{6,4},{7,5},{8,10},{9,11},{10,... | collective-permute-start | bytes 110600 | tf_op jit(solution)/shard_map/ppermute | solution.py:363
  44.0 0.2 collective-permute-start.14
  44.2 2.8 %collective-permute-start.15 = (bf16[16,1152]{1,0:T(8,128)(2,1)S(1)}, bf16[16,1152]{1,0:T(8,128)(2,1)S(1)}, u32[]{:S(2)}, u32[]{:S(2)}) collective-permute-start(bf16[16,1152]{1,0:T(8,128)(2,1)S(1)} %get-tuple-element.71), channel_id=1, source_target_pairs={{0,6},{1,7},{2,4},{3,5},{4,2},{5,3},{6,0},{7,1},{8,14},{9,15},{10,... | collective-permute-start | bytes 110600 | tf_op jit(solution)/shard_map/ppermute | solution.py:363
  47.0 5.9 %collective-permute-done.13.refs_1_ = bf16[16,1152]{1,0:T(8,128)(2,1)S(1)} collective-permute-done((bf16[16,1152]{1,0:T(8,128)(2,1)S(1)}, bf16[16,1152]{1,0:T(8,128)(2,1)S(1)}, u32[]{:S(2)}, u32[]{:S(2)}) %collective-permute-start.13) | collective-permute-done | bytes 36896 | tf_op jit(solution)/shard_map/ppermute | solution.py:363
  52.9 0.5 collective-permute-start.17
  53.5 0.1 collective-permute-start.18
  53.5 0.6 collective-permute-done.16.refs_4_
  54.1 0.2 collective-permute-start.19
  54.3 0.0 collective-permute-done.17.refs_5_
  54.3 0.4 collective-permute-start.11
  54.8 0.1 collective-permute-start.8
  54.8 0.5 collective-permute-done.19.refs_7_
  55.4 0.4 shard_map.163
  55.7 1.3 %collective-permute-start.22 = (bf16[16,2432]{1,0:T(8,128)(2,1)S(1)}, bf16[16,2432]{1,0:T(8,128)(2,1)S(1)}, u32[]{:S(2)}, u32[]{:S(2)}) collective-permute-start(bf16[16,2432]{1,0:T(8,128)(2,1)S(1)} %shard_map.163), channel_id=1, source_target_pairs={{0,8},{8,0},{16,24},{24,16},{1,9},{9,1},{17,25},{25,17},{2,10},{10... | collective-permute-start | bytes 233480 | tf_op jit(solution)/shard_map/ppermute | solution.py:360
  57.1 1.5 %collective-permute-start.23 = (bf16[16,2432]{1,0:T(8,128)(2,1)S(1)}, bf16[16,2432]{1,0:T(8,128)(2,1)S(1)}, u32[]{:S(2)}, u32[]{:S(2)}) collective-permute-start(bf16[16,2432]{1,0:T(8,128)(2,1)S(1)} %shard_map.163), channel_id=1, source_target_pairs={{0,16},{8,24},{16,0},{24,8},{1,17},{9,25},{17,1},{25,9},{2,18},{10... | collective-permute-start | bytes 233480 | tf_op jit(solution)/shard_map/ppermute | solution.py:360
  58.6 0.7 collective-permute-start.24
  59.3 0.1 add_convert_fusion.1
  59.4 0.9 %collective-permute-done.22 = bf16[16,2432]{1,0:T(8,128)(2,1)S(1)} collective-permute-done((bf16[16,2432]{1,0:T(8,128)(2,1)S(1)}, bf16[16,2432]{1,0:T(8,128)(2,1)S(1)}, u32[]{:S(2)}, u32[]{:S(2)}) %collective-permute-start.22) | collective-permute-done | bytes 77856 | tf_op jit(solution)/shard_map/ppermute | solution.py:360
  60.2 3.1 %collective-permute-start.10 = (bf16[256,512]{1,0:T(8,128)(2,1)S(1)}, bf16[256,512]{1,0:T(8,128)(2,1)S(1)}, u32[]{:S(2)}, u32[]{:S(2)}) collective-permute-start(bf16[256,512]{1,0:T(8,128)(2,1)S(1)} %add_convert_fusion.1), channel_id=1, source_target_pairs={{0,6},{1,7},{2,0},{3,1},{4,2},{5,3},{6,4},{7,5},{8,14},{9,15},{10,... | collective-permute-start | bytes 786440 | tf_op jit(solution)/shard_map/ppermute | solution.py:354
  63.4 0.5 collective-permute-done.24
  63.9 0.5 collective-permute-start.25
  64.4 3.0 %collective-permute-start.26 = (bf16[16,2432]{1,0:T(8,128)(2,1)S(1)}, bf16[16,2432]{1,0:T(8,128)(2,1)S(1)}, u32[]{:S(2)}, u32[]{:S(2)}) collective-permute-start(bf16[16,2432]{1,0:T(8,128)(2,1)S(1)} %add_convert_fusion.2.refs_0_), channel_id=1, source_target_pairs={{0,4},{1,5},{2,6},{3,7},{4,0},{5,1},{6,2},{7,3},{8,12},{9,13},{10,... | collective-permute-start | bytes 233480 | tf_op jit(solution)/shard_map/ppermute | solution.py:363
  67.4 1.0 %collective-permute-start.27 = (bf16[16,2432]{1,0:T(8,128)(2,1)S(1)}, bf16[16,2432]{1,0:T(8,128)(2,1)S(1)}, u32[]{:S(2)}, u32[]{:S(2)}) collective-permute-start(bf16[16,2432]{1,0:T(8,128)(2,1)S(1)} %add_convert_fusion.2.refs_0_), channel_id=1, source_target_pairs={{0,6},{1,7},{2,4},{3,5},{4,2},{5,3},{6,0},{7,1},{8,14},{9,15},{10,... | collective-permute-start | bytes 233480 | tf_op jit(solution)/shard_map/ppermute | solution.py:363
  68.4 2.1 %collective-permute-done.10 = bf16[256,512]{1,0:T(8,128)(2,1)S(1)} collective-permute-done((bf16[256,512]{1,0:T(8,128)(2,1)S(1)}, bf16[256,512]{1,0:T(8,128)(2,1)S(1)}, u32[]{:S(2)}, u32[]{:S(2)}) %collective-permute-start.10) | collective-permute-done | bytes 262176 | tf_op jit(solution)/shard_map/ppermute | solution.py:354
  70.5 0.1 add_convert_fusion.own_ref
  70.6 0.1 collective-permute-start.12
  70.7 0.5 collective-permute-start.28
  71.2 2.9 %collective-permute-done.25.refs_1_ = bf16[16,2432]{1,0:T(8,128)(2,1)S(1)} collective-permute-done((bf16[16,2432]{1,0:T(8,128)(2,1)S(1)}, bf16[16,2432]{1,0:T(8,128)(2,1)S(1)}, u32[]{:S(2)}, u32[]{:S(2)}) %collective-permute-start.25) | collective-permute-done | bytes 77856 | tf_op jit(solution)/shard_map/ppermute | solution.py:363
  74.1 1.3 %collective-permute-done.26.refs_2_ = bf16[16,2432]{1,0:T(8,128)(2,1)S(1)} collective-permute-done((bf16[16,2432]{1,0:T(8,128)(2,1)S(1)}, bf16[16,2432]{1,0:T(8,128)(2,1)S(1)}, u32[]{:S(2)}, u32[]{:S(2)}) %collective-permute-start.26) | collective-permute-done | bytes 77856 | tf_op jit(solution)/shard_map/ppermute | solution.py:363
  75.4 0.5 collective-permute-start.31
  75.9 0.8 %shard_map.160 = bf16[128,2048]{1,0:T(8,128)(2,1)} custom-call(bf16[128,1024]{1,0:T(8,128)(2,1)S(1)} %get-tuple-element.60.own_ref, bf16[128,1024]{1,0:T(8,128)(2,1)S(1)} %collective-permute-done.8.far_ref), custom_call_target="tpu_custom_call" | custom-call | bytes 1048576 | tf_op jit(solution)/shard_map/pallas_call | solution.py:61
  76.8 0.7 shard_map.161
  77.5 0.9 %shard_map.164 = (f32[16,4096]{1,0:T(8,128)}, f32[16,2048]{1,0:T(8,128)}, f32[16,4096]{1,0:T(8,128)}, f32[16,512]{1,0:T(8,128)}) custom-call(bf16[16,2432]{1,0:T(8,128)(2,1)S(1)} %add_convert_fusion.2.refs_0_, bf16[16,2432]{1,0:T(8,128)(2,1)S(1)} %collective-permute-done.25.refs_1_, bf16[16,2432]{1,0:T(8,128)(2,1)S(1)} %collective-permute-done.26.refs_2_, ...), custom_call_target="tpu_custom_call" | custom-call | bytes 1310720 | tf_op jit(solution)/shard_map/pallas_call | solution.py:61
  (38 shorter events, 0.1 us)
Async XLA Ops:
  0.6 1.2 %copy-start = (bf16[1,128,4096]{2,1,0:T(8,128)(2,1)S(1)}, bf16[1,128,4096]{2,1,0:T(8,128)(2,1)}, u32[]{:S(2)}) copy-start(bf16[1,128,4096]{2,1,0:T(8,128)(2,1)} %param.14) | copy-start | bytes 3145732
  1.9 1.0 %copy-start.2 = (bf16[1,128,2048]{2,1,0:T(8,128)(2,1)S(1)}, bf16[1,128,2048]{2,1,0:T(8,128)(2,1)}, u32[]{:S(2)}) copy-start(bf16[1,128,2048]{2,1,0:T(8,128)(2,1)} %param.10) | copy-start | bytes 1572868
  2.9 1.0 %copy-start.4 = (bf16[1,128,2048]{2,1,0:T(8,128)(2,1)S(1)}, bf16[1,128,2048]{2,1,0:T(8,128)(2,1)}, u32[]{:S(2)}) copy-start(bf16[1,128,2048]{2,1,0:T(8,128)(2,1)} %param.13) | copy-start | bytes 1572868
  5.0 24.2 %copy-start.10 = (s32[1,16]{1,0:T(1,128)S(1)}, s32[1,16]{1,0:T(1,128)}, u32[]{:S(2)}) copy-start(s32[1,16]{1,0:T(1,128)} %refs_0_.1) | copy-start | bytes 196
  5.0 19.7 %collective-permute-start.20 = (bf16[128,2048]{1,0:T(8,128)(2,1)}, bf16[128,2048]{1,0:T(8,128)(2,1)}, u32[]{:S(2)}, u32[]{:S(2)}) collective-permute-start(bf16[128,2048]{1,0:T(8,128)(2,1)} %get-tuple-element.72), channel_id=1, source_target_pairs={{0,1},{1,0},{2,3},{3,2},{4,5},{5,4},{6,7},{7,6},{8,9},{9,8},{10,11... | collective-permute-start | bytes 1572872 | tf_op jit(solution)/shard_map/ppermute | solution.py:351
  5.5 22.1 %collective-permute-start.1 = (bf16[128,2048]{1,0:T(8,128)(2,1)}, bf16[128,2048]{1,0:T(8,128)(2,1)}, u32[]{:S(2)}, u32[]{:S(2)}) collective-permute-start(bf16[128,2048]{1,0:T(8,128)(2,1)} %get-tuple-element.45), channel_id=1, source_target_pairs={{0,1},{1,0},{2,3},{3,2},{4,5},{5,4},{6,7},{7,6},{8,9},{9,8},{10,11... | collective-permute-start | bytes 1572872 | tf_op jit(solution)/shard_map/ppermute | solution.py:351
  8.2 3.2 %collective-permute-start = (bf16[136,512]{1,0:T(8,128)(2,1)}, bf16[136,512]{1,0:T(8,128)(2,1)S(1)}, u32[]{:S(2)}, u32[]{:S(2)}) collective-permute-start(bf16[136,512]{1,0:T(8,128)(2,1)} %get-tuple-element.44), channel_id=1, source_target_pairs={{0,1},{1,0},{2,3},{3,2},{4,5},{5,4},{6,7},{7,6},{8,9},{9,8},{10,11... | collective-permute-start | bytes 417800 | tf_op jit(solution)/shard_map/ppermute | solution.py:351
  8.8 9.4 %collective-permute-start.2 = (bf16[136,512]{1,0:T(8,128)(2,1)}, bf16[136,512]{1,0:T(8,128)(2,1)S(1)}, u32[]{:S(2)}, u32[]{:S(2)}) collective-permute-start(bf16[136,512]{1,0:T(8,128)(2,1)} %get-tuple-element.43.refs_0_.refs_5_), channel_id=1, source_target_pairs={{0,2},{1,3},{2,4},{3,5},{4,6},{5,7},{6,0},{7,1},{8,10},{9,11},{10,... | collective-permute-start | bytes 417800 | tf_op jit(solution)/shard_map/ppermute | solution.py:354
  11.4 9.5 %collective-permute-start.3 = (bf16[136,512]{1,0:T(8,128)(2,1)S(1)}, bf16[136,512]{1,0:T(8,128)(2,1)S(1)}, u32[]{:S(2)}, u32[]{:S(2)}) collective-permute-start(bf16[136,512]{1,0:T(8,128)(2,1)S(1)} %collective-permute-done.refs_1_.refs_6_), channel_id=1, source_target_pairs={{0,2},{1,3},{2,4},{3,5},{4,6},{5,7},{6,0},{7,1},{8,10},{9,11},{10,... | collective-permute-start | bytes 417800 | tf_op jit(solution)/shard_map/ppermute | solution.py:354
  18.2 17.2 %collective-permute-start.4 = (bf16[136,512]{1,0:T(8,128)(2,1)S(1)}, bf16[136,512]{1,0:T(8,128)(2,1)S(1)}, u32[]{:S(2)}, u32[]{:S(2)}) collective-permute-start(bf16[136,512]{1,0:T(8,128)(2,1)S(1)} %collective-permute-done.2.refs_0_.refs_7_), channel_id=1, source_target_pairs={{0,2},{1,3},{2,4},{3,5},{4,6},{5,7},{6,0},{7,1},{8,10},{9,11},{10,... | collective-permute-start | bytes 417800 | tf_op jit(solution)/shard_map/ppermute | solution.py:354
  20.9 14.5 %collective-permute-start.5 = (bf16[136,512]{1,0:T(8,128)(2,1)S(1)}, bf16[136,512]{1,0:T(8,128)(2,1)S(1)}, u32[]{:S(2)}, u32[]{:S(2)}) collective-permute-start(bf16[136,512]{1,0:T(8,128)(2,1)S(1)} %collective-permute-done.3.refs_1_.refs_8_), channel_id=1, source_target_pairs={{0,2},{1,3},{2,4},{3,5},{4,6},{5,7},{6,0},{7,1},{8,10},{9,11},{10,... | collective-permute-start | bytes 417800 | tf_op jit(solution)/shard_map/ppermute | solution.py:354
  20.9 15.4 %collective-permute-start.6 = (bf16[136,512]{1,0:T(8,128)(2,1)}, bf16[136,512]{1,0:T(8,128)(2,1)S(1)}, u32[]{:S(2)}, u32[]{:S(2)}) collective-permute-start(bf16[136,512]{1,0:T(8,128)(2,1)} %get-tuple-element.43.refs_0_.refs_5_), channel_id=1, source_target_pairs={{0,6},{1,7},{2,0},{3,1},{4,2},{5,3},{6,4},{7,5},{8,14},{9,15},{10,... | collective-permute-start | bytes 417800 | tf_op jit(solution)/shard_map/ppermute | solution.py:354
  24.7 11.6 %collective-permute-start.7 = (bf16[136,512]{1,0:T(8,128)(2,1)S(1)}, bf16[136,512]{1,0:T(8,128)(2,1)S(1)}, u32[]{:S(2)}, u32[]{:S(2)}) collective-permute-start(bf16[136,512]{1,0:T(8,128)(2,1)S(1)} %collective-permute-done.refs_1_.refs_6_), channel_id=1, source_target_pairs={{0,6},{1,7},{2,0},{3,1},{4,2},{5,3},{6,4},{7,5},{8,14},{9,15},{10,... | collective-permute-start | bytes 417800 | tf_op jit(solution)/shard_map/ppermute | solution.py:354
  25.2 1.2 %copy-start.1 = (bf16[1,128,4096]{2,1,0:T(8,128)(2,1)S(1)}, bf16[1,128,4096]{2,1,0:T(8,128)(2,1)}, u32[]{:S(2)}) copy-start(bf16[1,128,4096]{2,1,0:T(8,128)(2,1)} %param.14) | copy-start | bytes 3145732
  27.5 27.8 %collective-permute-start.21 = (bf16[256,1024]{1,0:T(8,128)(2,1)S(1)}, bf16[256,1024]{1,0:T(8,128)(2,1)S(1)}, u32[]{:S(2)}, u32[]{:S(2)}) collective-permute-start(bf16[256,1024]{1,0:T(8,128)(2,1)S(1)} %get-tuple-element.74), channel_id=1, source_target_pairs={{0,2},{1,3},{2,0},{3,1},{4,6},{5,7},{6,4},{7,5},{8,10},{9,11},{10,... | collective-permute-start | bytes 1572872 | tf_op jit(solution)/shard_map/ppermute | solution.py:363
  29.2 1.0 %copy-start.3 = (bf16[1,128,2048]{2,1,0:T(8,128)(2,1)S(1)}, bf16[1,128,2048]{2,1,0:T(8,128)(2,1)}, u32[]{:S(2)}) copy-start(bf16[1,128,2048]{2,1,0:T(8,128)(2,1)} %param.10) | copy-start | bytes 1572868
  30.2 1.0 %copy-start.5 = (bf16[1,128,2048]{2,1,0:T(8,128)(2,1)S(1)}, bf16[1,128,2048]{2,1,0:T(8,128)(2,1)}, u32[]{:S(2)}) copy-start(bf16[1,128,2048]{2,1,0:T(8,128)(2,1)} %param.13) | copy-start | bytes 1572868
  31.3 0.9 %copy-start.6 = (bf16[136,512]{1,0:T(8,128)(2,1)S(1)}, bf16[136,512]{1,0:T(8,128)(2,1)}, u32[]{:S(2)}) copy-start(bf16[136,512]{1,0:T(8,128)(2,1)} %get-tuple-element.43.refs_0_.refs_5_) | copy-start | bytes 417796
  34.5 2.8 %copy-start.7 = (bf16[136,512]{1,0:T(8,128)(2,1)S(1)}, bf16[136,512]{1,0:T(8,128)(2,1)}, u32[]{:S(2)}) copy-start(bf16[136,512]{1,0:T(8,128)(2,1)} %get-tuple-element.43.refs_0_.refs_5_) | copy-start | bytes 417796
  34.5 2.7 %copy-start.8 = (bf16[16,2048]{1,0:T(8,128)(2,1)S(1)}, bf16[16,2048]{1,0:T(8,128)(2,1)}, u32[]{:S(2)}) copy-start(bf16[16,2048]{1,0:T(8,128)(2,1)} %refs_3_.1) | copy-start | bytes 196612
  34.5 2.7 %copy-start.9 = (bf16[16,512]{1,0:T(8,128)(2,1)S(1)}, bf16[16,512]{1,0:T(8,128)(2,1)}, u32[]{:S(2)}) copy-start(bf16[16,512]{1,0:T(8,128)(2,1)} %refs_4_.1) | copy-start | bytes 49156
  42.0 16.6 %collective-permute-start.9 = (bf16[256,512]{1,0:T(8,128)(2,1)S(1)}, bf16[256,512]{1,0:T(8,128)(2,1)S(1)}, u32[]{:S(2)}, u32[]{:S(2)}) collective-permute-start(bf16[256,512]{1,0:T(8,128)(2,1)S(1)} %get-tuple-element.62), channel_id=1, source_target_pairs={{0,6},{1,7},{2,0},{3,1},{4,2},{5,3},{6,4},{7,5},{8,14},{9,15},{10,... | collective-permute-start | bytes 786440 | tf_op jit(solution)/shard_map/ppermute | solution.py:354
  42.6 10.3 %collective-permute-start.13 = (bf16[16,1152]{1,0:T(8,128)(2,1)S(1)}, bf16[16,1152]{1,0:T(8,128)(2,1)S(1)}, u32[]{:S(2)}, u32[]{:S(2)}) collective-permute-start(bf16[16,1152]{1,0:T(8,128)(2,1)S(1)} %get-tuple-element.69), channel_id=1, source_target_pairs={{0,2},{1,3},{2,0},{3,1},{4,6},{5,7},{6,4},{7,5},{8,10},{9,11},{10,... | collective-permute-start | bytes 110600 | tf_op jit(solution)/shard_map/ppermute | solution.py:363
  44.0 8.9 %collective-permute-start.14 = (bf16[16,1152]{1,0:T(8,128)(2,1)S(1)}, bf16[16,1152]{1,0:T(8,128)(2,1)S(1)}, u32[]{:S(2)}, u32[]{:S(2)}) collective-permute-start(bf16[16,1152]{1,0:T(8,128)(2,1)S(1)} %get-tuple-element.70), channel_id=1, source_target_pairs={{0,4},{1,5},{2,6},{3,7},{4,0},{5,1},{6,2},{7,3},{8,12},{9,13},{10,... | collective-permute-start | bytes 110600 | tf_op jit(solution)/shard_map/ppermute | solution.py:363
  44.2 9.2 %collective-permute-start.15 = (bf16[16,1152]{1,0:T(8,128)(2,1)S(1)}, bf16[16,1152]{1,0:T(8,128)(2,1)S(1)}, u32[]{:S(2)}, u32[]{:S(2)}) collective-permute-start(bf16[16,1152]{1,0:T(8,128)(2,1)S(1)} %get-tuple-element.71), channel_id=1, source_target_pairs={{0,6},{1,7},{2,4},{3,5},{4,2},{5,3},{6,0},{7,1},{8,14},{9,15},{10,... | collective-permute-start | bytes 110600 | tf_op jit(solution)/shard_map/ppermute | solution.py:363
  52.9 1.2 %collective-permute-start.16 = (bf16[16,1152]{1,0:T(8,128)(2,1)S(1)}, bf16[16,1152]{1,0:T(8,128)(2,1)S(1)}, u32[]{:S(2)}, u32[]{:S(2)}) collective-permute-start(bf16[16,1152]{1,0:T(8,128)(2,1)S(1)} %get-tuple-element.68.refs_0_), channel_id=1, source_target_pairs={{0,1},{1,0},{2,3},{3,2},{4,5},{5,4},{6,7},{7,6},{8,9},{9,8},{10,11... | collective-permute-start | bytes 110600 | tf_op jit(solution)/shard_map/ppermute | solution.py:351
  52.9 1.4 %collective-permute-start.17 = (bf16[16,1152]{1,0:T(8,128)(2,1)S(1)}, bf16[16,1152]{1,0:T(8,128)(2,1)S(1)}, u32[]{:S(2)}, u32[]{:S(2)}) collective-permute-start(bf16[16,1152]{1,0:T(8,128)(2,1)S(1)} %collective-permute-done.13.refs_1_), channel_id=1, source_target_pairs={{0,1},{1,0},{2,3},{3,2},{4,5},{5,4},{6,7},{7,6},{8,9},{9,8},{10,11... | collective-permute-start | bytes 110600 | tf_op jit(solution)/shard_map/ppermute | solution.py:351
  53.5 1.3 %collective-permute-start.18 = (bf16[16,1152]{1,0:T(8,128)(2,1)S(1)}, bf16[16,1152]{1,0:T(8,128)(2,1)S(1)}, u32[]{:S(2)}, u32[]{:S(2)}) collective-permute-start(bf16[16,1152]{1,0:T(8,128)(2,1)S(1)} %collective-permute-done.14.refs_2_), channel_id=1, source_target_pairs={{0,1},{1,0},{2,3},{3,2},{4,5},{5,4},{6,7},{7,6},{8,9},{9,8},{10,11... | collective-permute-start | bytes 110600 | tf_op jit(solution)/shard_map/ppermute | solution.py:351
  54.1 1.2 %collective-permute-start.19 = (bf16[16,1152]{1,0:T(8,128)(2,1)S(1)}, bf16[16,1152]{1,0:T(8,128)(2,1)S(1)}, u32[]{:S(2)}, u32[]{:S(2)}) collective-permute-start(bf16[16,1152]{1,0:T(8,128)(2,1)S(1)} %collective-permute-done.15.refs_3_), channel_id=1, source_target_pairs={{0,1},{1,0},{2,3},{3,2},{4,5},{5,4},{6,7},{7,6},{8,9},{9,8},{10,11... | collective-permute-start | bytes 110600 | tf_op jit(solution)/shard_map/ppermute | solution.py:351
  54.3 13.1 %collective-permute-start.11 = (bf16[256,512]{1,0:T(8,128)(2,1)S(1)}, bf16[256,512]{1,0:T(8,128)(2,1)S(1)}, u32[]{:S(2)}, u32[]{:S(2)}) collective-permute-start(bf16[256,512]{1,0:T(8,128)(2,1)S(1)} %get-tuple-element.65), channel_id=1, source_target_pairs={{0,2},{1,3},{2,4},{3,5},{4,6},{5,7},{6,0},{7,1},{8,10},{9,11},{10,... | collective-permute-start | bytes 786440 | tf_op jit(solution)/shard_map/ppermute | solution.py:354
  54.8 15.9 %collective-permute-start.8 = (bf16[128,1024]{1,0:T(8,128)(2,1)S(1)}, bf16[128,1024]{1,0:T(8,128)(2,1)S(1)}, u32[]{:S(2)}, u32[]{:S(2)}) collective-permute-start(bf16[128,1024]{1,0:T(8,128)(2,1)S(1)} %get-tuple-element.61), channel_id=1, source_target_pairs={{0,1},{1,0},{2,3},{3,2},{4,5},{5,4},{6,7},{7,6},{8,9},{9,8},{10,11... | collective-permute-start | bytes 786440 | tf_op jit(solution)/shard_map/ppermute | solution.py:351
  55.7 4.5 %collective-permute-start.22 = (bf16[16,2432]{1,0:T(8,128)(2,1)S(1)}, bf16[16,2432]{1,0:T(8,128)(2,1)S(1)}, u32[]{:S(2)}, u32[]{:S(2)}) collective-permute-start(bf16[16,2432]{1,0:T(8,128)(2,1)S(1)} %shard_map.163), channel_id=1, source_target_pairs={{0,8},{8,0},{16,24},{24,16},{1,9},{9,1},{17,25},{25,17},{2,10},{10... | collective-permute-start | bytes 233480 | tf_op jit(solution)/shard_map/ppermute | solution.py:360
  57.1 6.3 %collective-permute-start.23 = (bf16[16,2432]{1,0:T(8,128)(2,1)S(1)}, bf16[16,2432]{1,0:T(8,128)(2,1)S(1)}, u32[]{:S(2)}, u32[]{:S(2)}) collective-permute-start(bf16[16,2432]{1,0:T(8,128)(2,1)S(1)} %shard_map.163), channel_id=1, source_target_pairs={{0,16},{8,24},{16,0},{24,8},{1,17},{9,25},{17,1},{25,9},{2,18},{10... | collective-permute-start | bytes 233480 | tf_op jit(solution)/shard_map/ppermute | solution.py:360
  58.6 5.3 %collective-permute-start.24 = (bf16[16,2432]{1,0:T(8,128)(2,1)S(1)}, bf16[16,2432]{1,0:T(8,128)(2,1)S(1)}, u32[]{:S(2)}, u32[]{:S(2)}) collective-permute-start(bf16[16,2432]{1,0:T(8,128)(2,1)S(1)} %shard_map.163), channel_id=1, source_target_pairs={{0,24},{8,16},{16,8},{24,0},{1,25},{9,17},{17,9},{25,1},{2,26},{10... | collective-permute-start | bytes 233480 | tf_op jit(solution)/shard_map/ppermute | solution.py:360
  60.2 10.3 %collective-permute-start.10 = (bf16[256,512]{1,0:T(8,128)(2,1)S(1)}, bf16[256,512]{1,0:T(8,128)(2,1)S(1)}, u32[]{:S(2)}, u32[]{:S(2)}) collective-permute-start(bf16[256,512]{1,0:T(8,128)(2,1)S(1)} %add_convert_fusion.1), channel_id=1, source_target_pairs={{0,6},{1,7},{2,0},{3,1},{4,2},{5,3},{6,4},{7,5},{8,14},{9,15},{10,... | collective-permute-start | bytes 786440 | tf_op jit(solution)/shard_map/ppermute | solution.py:354
  63.9 10.2 %collective-permute-start.25 = (bf16[16,2432]{1,0:T(8,128)(2,1)S(1)}, bf16[16,2432]{1,0:T(8,128)(2,1)S(1)}, u32[]{:S(2)}, u32[]{:S(2)}) collective-permute-start(bf16[16,2432]{1,0:T(8,128)(2,1)S(1)} %add_convert_fusion.2.refs_0_), channel_id=1, source_target_pairs={{0,2},{1,3},{2,0},{3,1},{4,6},{5,7},{6,4},{7,5},{8,10},{9,11},{10,... | collective-permute-start | bytes 233480 | tf_op jit(solution)/shard_map/ppermute | solution.py:363
  64.4 11.0 %collective-permute-start.26 = (bf16[16,2432]{1,0:T(8,128)(2,1)S(1)}, bf16[16,2432]{1,0:T(8,128)(2,1)S(1)}, u32[]{:S(2)}, u32[]{:S(2)}) collective-permute-start(bf16[16,2432]{1,0:T(8,128)(2,1)S(1)} %add_convert_fusion.2.refs_0_), channel_id=1, source_target_pairs={{0,4},{1,5},{2,6},{3,7},{4,0},{5,1},{6,2},{7,3},{8,12},{9,13},{10,... | collective-permute-start | bytes 233480 | tf_op jit(solution)/shard_map/ppermute | solution.py:363
  67.4 8.0 %collective-permute-start.27 = (bf16[16,2432]{1,0:T(8,128)(2,1)S(1)}, bf16[16,2432]{1,0:T(8,128)(2,1)S(1)}, u32[]{:S(2)}, u32[]{:S(2)}) collective-permute-start(bf16[16,2432]{1,0:T(8,128)(2,1)S(1)} %add_convert_fusion.2.refs_0_), channel_id=1, source_target_pairs={{0,6},{1,7},{2,4},{3,5},{4,2},{5,3},{6,0},{7,1},{8,14},{9,15},{10,... | collective-permute-start | bytes 233480 | tf_op jit(solution)/shard_map/ppermute | solution.py:363
  70.6 6.2 %collective-permute-start.12 = (bf16[128,512]{1,0:T(8,128)(2,1)S(1)}, bf16[128,512]{1,0:T(8,128)(2,1)S(1)}, u32[]{:S(2)}, u32[]{:S(2)}) collective-permute-start(bf16[128,512]{1,0:T(8,128)(2,1)S(1)} %slice.4), channel_id=1, source_target_pairs={{0,1},{1,0},{2,3},{3,2},{4,5},{5,4},{6,7},{7,6},{8,9},{9,8},{10,11... | collective-permute-start | bytes 393224 | tf_op jit(solution)/shard_map/ppermute | solution.py:351
  70.7 6.8 %collective-permute-start.28 = (bf16[16,2432]{1,0:T(8,128)(2,1)S(1)}, bf16[16,2432]{1,0:T(8,128)(2,1)S(1)}, u32[]{:S(2)}, u32[]{:S(2)}) collective-permute-start(bf16[16,2432]{1,0:T(8,128)(2,1)S(1)} %add_convert_fusion.2.refs_0_), channel_id=1, source_target_pairs={{0,1},{1,0},{2,3},{3,2},{4,5},{5,4},{6,7},{7,6},{8,9},{9,8},{10,11... | collective-permute-start | bytes 233480 | tf_op jit(solution)/shard_map/ppermute | solution.py:351
  74.1 3.4 %collective-permute-start.29 = (bf16[16,2432]{1,0:T(8,128)(2,1)S(1)}, bf16[16,2432]{1,0:T(8,128)(2,1)S(1)}, u32[]{:S(2)}, u32[]{:S(2)}) collective-permute-start(bf16[16,2432]{1,0:T(8,128)(2,1)S(1)} %collective-permute-done.25.refs_1_), channel_id=1, source_target_pairs={{0,1},{1,0},{2,3},{3,2},{4,5},{5,4},{6,7},{7,6},{8,9},{9,8},{10,11... | collective-permute-start | bytes 233480 | tf_op jit(solution)/shard_map/ppermute | solution.py:351
  75.4 2.1 %collective-permute-start.30 = (bf16[16,2432]{1,0:T(8,128)(2,1)S(1)}, bf16[16,2432]{1,0:T(8,128)(2,1)S(1)}, u32[]{:S(2)}, u32[]{:S(2)}) collective-permute-start(bf16[16,2432]{1,0:T(8,128)(2,1)S(1)} %collective-permute-done.26.refs_2_), channel_id=1, source_target_pairs={{0,1},{1,0},{2,3},{3,2},{4,5},{5,4},{6,7},{7,6},{8,9},{9,8},{10,11... | collective-permute-start | bytes 233480 | tf_op jit(solution)/shard_map/ppermute | solution.py:351
  75.4 2.1 %collective-permute-start.31 = (bf16[16,2432]{1,0:T(8,128)(2,1)S(1)}, bf16[16,2432]{1,0:T(8,128)(2,1)S(1)}, u32[]{:S(2)}, u32[]{:S(2)}) collective-permute-start(bf16[16,2432]{1,0:T(8,128)(2,1)S(1)} %collective-permute-done.27.refs_3_), channel_id=1, source_target_pairs={{0,1},{1,0},{2,3},{3,2},{4,5},{5,4},{6,7},{7,6},{8,9},{9,8},{10,11... | collective-permute-start | bytes 233480 | tf_op jit(solution)/shard_map/ppermute | solution.py:351

commit v3 on v2

--- a/solution.py
+++ b/solution.py
@@ -69,27 +69,36 @@
     )(*args)
 
 
-def split_kv(k_hbm, v_hbm, hidden_hbm, qa_hbm, va_hbm, own_ref, send_ref, hidden_ref, qa_ref, va_ref, sems):
+def split_kv(k_hbm, v_hbm, hidden_hbm, qa_hbm, va_hbm, own_ref, send_ref, hidden_ref, maps_ref, sems):
     core = lax.axis_index("ctx") % 2
     rows = k_hbm.shape[0]
-    copies = [(hidden_hbm, hidden_ref), (qa_hbm, qa_ref), (va_hbm, va_ref)]
+    rank, width = qa_hbm.shape
+    piece = width // 4
+    moves = [(qa_hbm, maps_ref.at[pl.ds(0, rank)]), (va_hbm, maps_ref.at[pl.ds(rank, rank)])]
+    for i in range(4):
+        columns = pl.ds(i * piece, piece)
+        moves.append((hidden_hbm.at[:, columns], hidden_ref.at[:, columns]))
     for i, source in enumerate((k_hbm, v_hbm)):
         columns = pl.ds(i * KV_HALF, KV_HALF)
         for half, target in ((core, own_ref), (1 - core, send_ref)):
             at = pl.ds(pl.multiple_of(half * KV_HALF, 128), KV_HALF)
-            copies.append((source.at[:, at], target.at[pl.ds(0, rows), columns]))
-    copies = [pltpu.make_async_copy(a, b, sems.at[i]) for i, (a, b) in enumerate(copies)]
+            moves.append((source.at[:, at], target.at[pl.ds(0, rows), columns]))
+    copies = [pltpu.make_async_copy(a, b, sems.at[i]) for i, (a, b) in enumerate(moves)]
     for copy in copies:
         copy.start()
-    for copy in copies:
+    for copy in copies[:2]:
         copy.wait()
-    at = 0
-    for ref in (qa_ref, va_ref):
-        down = dot_nt(ref[...], hidden_ref[...]).astype(BF16)
-        for first in range(0, ref.shape[0], 8):
-            own_ref[rows:, at : at + rows] = down[first : first + 8]
-            send_ref[rows:, at : at + rows] = down[first : first + 8]
-            at += rows
+    down = jnp.zeros((2 * rank, rows), F32)
+    for i in range(4):
+        copies[2 + i].wait()
+        columns = slice(i * piece, (i + 1) * piece)
+        down += dot_nt(maps_ref[:, columns], hidden_ref[:, columns])
+    down = down.astype(BF16)
+    for i in range(2 * rank // 8):
+        own_ref[rows:, i * rows : (i + 1) * rows] = down[8 * i : 8 * i + 8]
+        send_ref[rows:, i * rows : (i + 1) * rows] = down[8 * i : 8 * i + 8]
+    for copy in copies[6:]:
+        copy.wait()
 
 
 def split_rest(q_ref, g_ref, hidden_ref, pack_ref, send_ref):
@@ -353,8 +362,11 @@
     def up(a, step):
         return lax.ppermute(a, "ctx", [(i, (i + 2 * step) % n_ctx) for i in range(n_ctx)])
 
-    def down(a, step):
-        return up(a, -step)
+    def down(a, step, first=1):
+        if step > 1 or first > 1:
+            return up(a, -step)
+        chips = range(1, n_chips)
+        return lax.ppermute(a, "ctx", [(2 * i + c, 2 * (i - 1) + c) for i in chips for c in (0, 1)])
 
     def across(a, bit):
         return lax.ppermute(a, "dp", [(i, i ^ bit) for i in range(n_dp)])
@@ -369,9 +381,8 @@
         (k, v, x, querya, valuea),
         scratch=[
             pltpu.VMEM(x.shape, BF16),
-            pltpu.VMEM(querya.shape, BF16),
-            pltpu.VMEM(valuea.shape, BF16),
-            pltpu.SemaphoreType.DMA((7,)),
+            pltpu.VMEM((2 * rank, x.shape[1]), BF16),
+            pltpu.SemaphoreType.DMA((10,)),
         ],
         hbm=range(5),
         limit=VMEM_MOST - (3 << 17),
@@ -446,7 +457,7 @@
         last = down(dkv[n_chips - 1], n_chips - 1)
         total = dkv[n_chips - 2]
         for step in range(n_chips - 2, 0, -1):
-            total = down(total, 1).astype(F32) + dkv[step - 1].astype(F32)
+            total = down(total, 1, step).astype(F32) + dkv[step - 1].astype(F32)
             total = (total if step > 1 else total + last.astype(F32)).astype(BF16)
     else:
         total = dkv[0]

time: 79 us -> 79.3 us (level)
  waiting for transfers between devices: 22.8 us -> 24.8 us
  starting transfers between devices: 29.7 us -> 27.8 us
    ppermute x0 -> x1, waiting for transfers between devices: none -> 4.07 us  [down(): lax.ppermute(a, 'ctx', [(2 * i + c, 2 * (i - 1) + c) for i in chips for c...]
    ppermute x9 -> x8, starting transfers between devices: 12.7 us -> 9.58 us  [up(): lax.ppermute(a, 'ctx', [(i, (i + 2 * step) % n_ctx) for i in range(n_ctx)])]
    ppermute x9 -> x8, waiting for transfers between devices: 10 us -> 7.93 us  [up(): lax.ppermute(a, 'ctx', [(i, (i + 2 * step) % n_ctx) for i in range(n_ctx)])]
    ppermute x3, waiting for transfers between devices: 1.4 us -> 3.24 us  [across(): return lax.ppermute(a, 'dp', [(i, i ^ bit) for i in range(n_dp)])]
    ppermute x7, waiting for transfers between devices: 10.2 us -> 8.4 us  [along(): return lax.ppermute(a, 'ctx', [(i, i ^ 2 * bit) for i in range(n_ctx)])]
    ppermute x0 -> x1, starting transfers between devices: none -> 1.28 us  [down(): lax.ppermute(a, 'ctx', [(2 * i + c, 2 * (i - 1) + c) for i in chips for c...]
  transfers between devices with their start and end apart: 32 -> 32, of which waited for: 10 -> 11; matrix products, arithmetic and copies ran while one was open for 0% -> 0% of each run, Pallas kernels for 20% -> 20%
where the time goes in v3:
time: 79.3 us; the launch traced here: 78.7 us
  starting transfers between devices  27.8 us (35%)
  waiting for transfers between devices  24.8 us (31%)
  Pallas kernels  17.4 us (22%)
  local copies, waits for them, and re-layouts  7.55 us (10%)
  between operations  0.86 us (1%)
    pallas_call x12, Pallas kernels, kernel_call(): pl.pallas_call(body, out_shape=outs, in_specs=[SM if i in smem else HB if...  17.4 us
    ppermute x7, starting transfers between devices, along(): return lax.ppermute(a, 'ctx', [(i, i ^ 2 * bit) for i in range(n_ctx)])  10.5 us
    ppermute x8, starting transfers between devices, up(): lax.ppermute(a, 'ctx', [(i, (i + 2 * step) % n_ctx) for i in range(n_ctx)])  9.58 us
    ppermute x7, waiting for transfers between devices, along(): return lax.ppermute(a, 'ctx', [(i, i ^ 2 * bit) for i in range(n_ctx)])  8.4 us
    ppermute x8, waiting for transfers between devices, up(): lax.ppermute(a, 'ctx', [(i, (i + 2 * step) % n_ctx) for i in range(n_ctx)])  7.93 us
    unnamed x22, local copies, waits for them, and re-layouts  7.54 us
    ppermute x1, waiting for transfers between devices, down(): lax.ppermute(a, 'ctx', [(2 * i + c, 2 * (i - 1) + c) for i in chips for c...  4.07 us
    ppermute x3, starting transfers between devices, across(): return lax.ppermute(a, 'dp', [(i, i ^ bit) for i in range(n_dp)])  3.54 us
  transfers between devices with their start and end apart: 32, of which 11 were waited for; matrix products, arithmetic and copies ran while one was open for 0% of the time, Pallas kernels for 20%

profile of v3, /device:TPU:0, one launch (start us, length us, event | category | flops | bytes accessed | tf_op | source)
XLA Modules:
  0.0 78.7 jit_solution(10939465573578835462)
XLA Ops:
  0.6 0.0 copy-start
  0.6 1.2 %copy-done = bf16[1,128,4096]{2,1,0:T(8,128)(2,1)S(1)} copy-done((bf16[1,128,4096]{2,1,0:T(8,128)(2,1)S(1)}, bf16[1,128,4096]{2,1,0:T(8,128)(2,1)}, u32[]{:S(2)}) %copy-start) | copy-done | bytes 1048600
  1.9 1.0 %copy-done.2 = bf16[1,128,2048]{2,1,0:T(8,128)(2,1)S(1)} copy-done((bf16[1,128,2048]{2,1,0:T(8,128)(2,1)S(1)}, bf16[1,128,2048]{2,1,0:T(8,128)(2,1)}, u32[]{:S(2)}) %copy-start.2) | copy-done | bytes 524312
  2.9 1.0 %copy-done.4 = bf16[1,128,2048]{2,1,0:T(8,128)(2,1)S(1)} copy-done((bf16[1,128,2048]{2,1,0:T(8,128)(2,1)S(1)}, bf16[1,128,2048]{2,1,0:T(8,128)(2,1)}, u32[]{:S(2)}) %copy-start.4) | copy-done | bytes 524312
  3.9 1.0 %shard_map.154 = (bf16[128,2048]{1,0:T(8,128)(2,1)}, bf16[128,2048]{1,0:T(8,128)(2,1)}) custom-call(bf16[128,2048]{1,0:T(8,128)(2,1)S(1)} %bitcast.11, bf16[128,2048]{1,0:T(8,128)(2,1)S(1)} %bitcast.13, bf16[128,4096]{1,0:T(8,128)(2,1)S(1)} %bitcast.9), custom_call_target="tpu_custom_call" | custom-call | bytes 3145728 | tf_op jit(solution)/shard_map/pallas_call | solution.py:61
  5.0 0.5 collective-permute-start.20
  5.5 0.0 collective-permute-start.1
  5.5 2.8 %shard_map.153 = (bf16[136,512]{1,0:T(8,128)(2,1)}, bf16[136,512]{1,0:T(8,128)(2,1)}) custom-call(bf16[128,512]{1,0:T(8,128)(2,1)} %bitcast.16, bf16[128,512]{1,0:T(8,128)(2,1)} %bitcast.17, bf16[128,4096]{1,0:T(8,128)(2,1)} %bitcast.8, bf16[16,4096]{1,0:T(8,128)(2,1)} %qa_hbm.1, bf16[16,4096]{1,0:T(8,128)(2,1)} %va_hbm.1), custom_call_target="tpu_custom_call" | custom-call | bytes 1851392 | tf_op jit(solution)/shard_map/pallas_call | solution.py:61
  8.3 0.6 collective-permute-start
  8.8 2.6 %collective-permute-start.2 = (bf16[136,512]{1,0:T(8,128)(2,1)}, bf16[136,512]{1,0:T(8,128)(2,1)S(1)}, u32[]{:S(2)}, u32[]{:S(2)}) collective-permute-start(bf16[136,512]{1,0:T(8,128)(2,1)} %get-tuple-element.43.refs_0_.refs_5_), channel_id=1, source_target_pairs={{0,2},{1,3},{2,4},{3,5},{4,6},{5,7},{6,0},{7,1},{8,10},{9,11},{10,... | collective-permute-start | bytes 417800 | tf_op jit(solution)/shard_map/ppermute | solution.py:363
  11.4 1.6 %collective-permute-start.3 = (bf16[136,512]{1,0:T(8,128)(2,1)S(1)}, bf16[136,512]{1,0:T(8,128)(2,1)S(1)}, u32[]{:S(2)}, u32[]{:S(2)}) collective-permute-start(bf16[136,512]{1,0:T(8,128)(2,1)S(1)} %collective-permute-done.refs_1_.refs_6_), channel_id=1, source_target_pairs={{0,2},{1,3},{2,4},{3,5},{4,6},{5,7},{6,0},{7,1},{8,10},{9,11},{10,... | collective-permute-start | bytes 417800 | tf_op jit(solution)/shard_map/ppermute | solution.py:363
  13.0 5.2 %collective-permute-done.2.refs_0_.refs_7_ = bf16[136,512]{1,0:T(8,128)(2,1)S(1)} collective-permute-done((bf16[136,512]{1,0:T(8,128)(2,1)}, bf16[136,512]{1,0:T(8,128)(2,1)S(1)}, u32[]{:S(2)}, u32[]{:S(2)}) %collective-permute-start.2) | collective-permute-done | bytes 139296 | tf_op jit(solution)/shard_map/ppermute | solution.py:363
  18.2 2.7 %collective-permute-done.3.refs_1_.refs_8_ = bf16[136,512]{1,0:T(8,128)(2,1)S(1)} collective-permute-done((bf16[136,512]{1,0:T(8,128)(2,1)S(1)}, bf16[136,512]{1,0:T(8,128)(2,1)S(1)}, u32[]{:S(2)}, u32[]{:S(2)}) %collective-permute-start.3) | collective-permute-done | bytes 139296 | tf_op jit(solution)/shard_map/ppermute | solution.py:363
  20.9 3.8 %collective-permute-start.6 = (bf16[136,512]{1,0:T(8,128)(2,1)}, bf16[136,512]{1,0:T(8,128)(2,1)S(1)}, u32[]{:S(2)}, u32[]{:S(2)}) collective-permute-start(bf16[136,512]{1,0:T(8,128)(2,1)} %get-tuple-element.43.refs_0_.refs_5_), channel_id=1, source_target_pairs={{0,6},{1,7},{2,0},{3,1},{4,2},{5,3},{6,4},{7,5},{8,14},{9,15},{10,... | collective-permute-start | bytes 417800 | tf_op jit(solution)/shard_map/ppermute | solution.py:363
  24.8 0.5 collective-permute-start.7
  25.2 1.2 %copy-done.1 = bf16[1,128,4096]{2,1,0:T(8,128)(2,1)S(1)} copy-done((bf16[1,128,4096]{2,1,0:T(8,128)(2,1)S(1)}, bf16[1,128,4096]{2,1,0:T(8,128)(2,1)}, u32[]{:S(2)}) %copy-start.1) | copy-done | bytes 1048600
  26.5 1.1 %shard_map.162 = (bf16[256,1024]{1,0:T(8,128)(2,1)S(1)}, bf16[256,1024]{1,0:T(8,128)(2,1)S(1)}) custom-call(bf16[128,4096]{1,0:T(8,128)(2,1)S(1)} %bitcast.10, bf16[128,2048]{1,0:T(8,128)(2,1)} %collective-permute-done.20.far_ref), custom_call_target="tpu_custom_call" | custom-call | bytes 2621440 | tf_op jit(solution)/shard_map/pallas_call | solution.py:61
  27.6 1.6 %collective-permute-start.21 = (bf16[256,1024]{1,0:T(8,128)(2,1)S(1)}, bf16[256,1024]{1,0:T(8,128)(2,1)S(1)}, u32[]{:S(2)}, u32[]{:S(2)}) collective-permute-start(bf16[256,1024]{1,0:T(8,128)(2,1)S(1)} %get-tuple-element.74), channel_id=1, source_target_pairs={{0,2},{1,3},{2,0},{3,1},{4,6},{5,7},{6,4},{7,5},{8,10},{9,11},{10,... | collective-permute-start | bytes 1572872 | tf_op jit(solution)/shard_map/ppermute | solution.py:375
  29.2 1.0 %copy-done.3 = bf16[1,128,2048]{2,1,0:T(8,128)(2,1)S(1)} copy-done((bf16[1,128,2048]{2,1,0:T(8,128)(2,1)S(1)}, bf16[1,128,2048]{2,1,0:T(8,128)(2,1)}, u32[]{:S(2)}) %copy-start.3) | copy-done | bytes 524312
  30.3 1.0 %copy-done.5 = bf16[1,128,2048]{2,1,0:T(8,128)(2,1)S(1)} copy-done((bf16[1,128,2048]{2,1,0:T(8,128)(2,1)S(1)}, bf16[1,128,2048]{2,1,0:T(8,128)(2,1)}, u32[]{:S(2)}) %copy-start.5) | copy-done | bytes 524312
  31.3 0.9 %copy-done.6 = bf16[136,512]{1,0:T(8,128)(2,1)S(1)} copy-done((bf16[136,512]{1,0:T(8,128)(2,1)S(1)}, bf16[136,512]{1,0:T(8,128)(2,1)}, u32[]{:S(2)}) %copy-start.6) | copy-done | bytes 139288
  32.2 2.3 %shard_map.155 = (f32[2,256,1024]{2,1,0:T(8,128)S(1)}, f32[2,256,1024]{2,1,0:T(8,128)S(1)}, f32[2,8,1024]{2,1,0:T(8,128)S(1)}, bf16[2,1024,128]{2,1,0:T(8,128)(2,1)S(1)}, bf16[2,1024,128]{2,1,0:T(8,128)(2,1)S(1)}) custom-call(s32[1,16]{1,0:T(1,128)S(1)} %copy-done.10, bf16[136,512]{1,0:T(8,128)(2,1)S(1)} %copy-done.6, ...), custom_call_target="tpu_custom_call" | custom-call | flops 268435456 | bytes 7159872 | tf_op jit(solution)/shard_map/pallas_call | solution.py:61
  34.5 0.0 copy-start.7
  34.5 0.0 copy-start.8
  34.5 0.0 copy-start.9
  34.5 0.9 %shard_map.156 = (f32[2,256,1024]{2,1,0:T(8,128)S(1)}, f32[2,256,1024]{2,1,0:T(8,128)S(1)}, f32[2,8,1024]{2,1,0:T(8,128)S(1)}) custom-call(s32[1,16]{1,0:T(1,128)S(1)} %copy-done.10, bf16[136,512]{1,0:T(8,128)(2,1)S(1)} %collective-permute-done.2.refs_0_.refs_7_, bf16[136,512]{1,0:T(8,128)(2,1)S(1)} %collective-permute-done.3.refs_1_.refs_8_, ...), custom_call_target="tpu_custom_call" | custom-call | flops 268435456 | bytes 5587008 | tf_op jit(solution)/shard_map/pallas_call | solution.py:61
  35.4 0.9 %shard_map.157 = (f32[2,256,1024]{2,1,0:T(8,128)S(1)}, f32[2,256,1024]{2,1,0:T(8,128)S(1)}, f32[2,8,1024]{2,1,0:T(8,128)S(1)}) custom-call(s32[1,16]{1,0:T(1,128)S(1)} %copy-done.10, bf16[136,512]{1,0:T(8,128)(2,1)S(1)} %collective-permute-done.4.refs_0_.refs_9_, bf16[136,512]{1,0:T(8,128)(2,1)S(1)} %collective-permute-done.5.refs_1_.refs_10_, ...), custom_call_target="tpu_custom_call" | custom-call | flops 268435456 | bytes 5587008 | tf_op jit(solution)/shard_map/pallas_call | solution.py:61
  36.4 0.9 %shard_map.158 = (f32[2,256,1024]{2,1,0:T(8,128)S(1)}, f32[2,256,1024]{2,1,0:T(8,128)S(1)}, f32[2,8,1024]{2,1,0:T(8,128)S(1)}) custom-call(s32[1,16]{1,0:T(1,128)S(1)} %copy-done.10, bf16[136,512]{1,0:T(8,128)(2,1)S(1)} %collective-permute-done.6.refs_0_.refs_11_, bf16[136,512]{1,0:T(8,128)(2,1)S(1)} %collective-permute-done.7.refs_1_.refs_12_, ...), custom_call_target="tpu_custom_call" | custom-call | flops 268435456 | bytes 5587008 | tf_op jit(solution)/shard_map/pallas_call | solution.py:61
  37.3 4.7 %shard_map.159 = (bf16[128,1024]{1,0:T(8,128)(2,1)S(1)}, bf16[128,1024]{1,0:T(8,128)(2,1)S(1)}, bf16[256,512]{1,0:T(8,128)(2,1)S(1)}, bf16[256,512]{1,0:T(8,128)...) custom-call(s32[1,16]{1,0:T(1,128)S(1)} %copy-done.10, ...), custom_call_target="tpu_custom_call" | custom-call | flops 1610612736 | bytes 21004352 | tf_op jit(solution)/shard_map/pallas_call | solution.py:61
  42.0 0.6 collective-permute-start.9
  42.7 1.4 %collective-permute-start.13 = (bf16[16,1152]{1,0:T(8,128)(2,1)S(1)}, bf16[16,1152]{1,0:T(8,128)(2,1)S(1)}, u32[]{:S(2)}, u32[]{:S(2)}) collective-permute-start(bf16[16,1152]{1,0:T(8,128)(2,1)S(1)} %get-tuple-element.69), channel_id=1, source_target_pairs={{0,2},{1,3},{2,0},{3,1},{4,6},{5,7},{6,4},{7,5},{8,10},{9,11},{10,... | collective-permute-start | bytes 110600 | tf_op jit(solution)/shard_map/ppermute | solution.py:375
  44.1 0.2 collective-permute-start.14
  44.3 2.8 %collective-permute-start.15 = (bf16[16,1152]{1,0:T(8,128)(2,1)S(1)}, bf16[16,1152]{1,0:T(8,128)(2,1)S(1)}, u32[]{:S(2)}, u32[]{:S(2)}) collective-permute-start(bf16[16,1152]{1,0:T(8,128)(2,1)S(1)} %get-tuple-element.71), channel_id=1, source_target_pairs={{0,6},{1,7},{2,4},{3,5},{4,2},{5,3},{6,0},{7,1},{8,14},{9,15},{10,... | collective-permute-start | bytes 110600 | tf_op jit(solution)/shard_map/ppermute | solution.py:375
  47.0 5.9 %collective-permute-done.13.refs_1_ = bf16[16,1152]{1,0:T(8,128)(2,1)S(1)} collective-permute-done((bf16[16,1152]{1,0:T(8,128)(2,1)S(1)}, bf16[16,1152]{1,0:T(8,128)(2,1)S(1)}, u32[]{:S(2)}, u32[]{:S(2)}) %collective-permute-start.13) | collective-permute-done | bytes 36896 | tf_op jit(solution)/shard_map/ppermute | solution.py:375
  53.0 0.5 collective-permute-start.17
  53.5 0.1 collective-permute-start.18
  53.6 0.6 collective-permute-done.16.refs_4_
  54.2 0.2 collective-permute-start.19
  54.3 0.0 collective-permute-done.17.refs_5_
  54.4 0.4 collective-permute-start.11
  54.8 0.1 collective-permute-start.8
  54.9 0.5 collective-permute-done.19.refs_7_
  55.4 0.4 shard_map.163
  55.8 1.3 %collective-permute-start.22 = (bf16[16,2432]{1,0:T(8,128)(2,1)S(1)}, bf16[16,2432]{1,0:T(8,128)(2,1)S(1)}, u32[]{:S(2)}, u32[]{:S(2)}) collective-permute-start(bf16[16,2432]{1,0:T(8,128)(2,1)S(1)} %shard_map.163), channel_id=1, source_target_pairs={{0,8},{8,0},{16,24},{24,16},{1,9},{9,1},{17,25},{25,17},{2,10},{10... | collective-permute-start | bytes 233480 | tf_op jit(solution)/shard_map/ppermute | solution.py:372
  57.1 1.5 %collective-permute-start.23 = (bf16[16,2432]{1,0:T(8,128)(2,1)S(1)}, bf16[16,2432]{1,0:T(8,128)(2,1)S(1)}, u32[]{:S(2)}, u32[]{:S(2)}) collective-permute-start(bf16[16,2432]{1,0:T(8,128)(2,1)S(1)} %shard_map.163), channel_id=1, source_target_pairs={{0,16},{8,24},{16,0},{24,8},{1,17},{9,25},{17,1},{25,9},{2,18},{10... | collective-permute-start | bytes 233480 | tf_op jit(solution)/shard_map/ppermute | solution.py:372
  58.6 0.7 collective-permute-start.24
  59.3 0.1 add_convert_fusion.1
  59.4 0.9 %collective-permute-done.22 = bf16[16,2432]{1,0:T(8,128)(2,1)S(1)} collective-permute-done((bf16[16,2432]{1,0:T(8,128)(2,1)S(1)}, bf16[16,2432]{1,0:T(8,128)(2,1)S(1)}, u32[]{:S(2)}, u32[]{:S(2)}) %collective-permute-start.22) | collective-permute-done | bytes 77856 | tf_op jit(solution)/shard_map/ppermute | solution.py:372
  60.3 1.3 %collective-permute-start.10 = (bf16[256,512]{1,0:T(8,128)(2,1)S(1)}, bf16[256,512]{1,0:T(8,128)(2,1)S(1)}, u32[]{:S(2)}, u32[]{:S(2)}) collective-permute-start(bf16[256,512]{1,0:T(8,128)(2,1)S(1)} %add_convert_fusion.1), channel_id=1, source_target_pairs={{2,0},{3,1},{4,2},{5,3},{6,4},{7,5},{10,8},{11,9},{12,10},{13,11},... | collective-permute-start | bytes 786440 | tf_op jit(solution)/shard_map/ppermute | solution.py:369
  61.5 0.7 collective-permute-done.23
  62.3 1.7 %collective-permute-done.24 = bf16[16,2432]{1,0:T(8,128)(2,1)S(1)} collective-permute-done((bf16[16,2432]{1,0:T(8,128)(2,1)S(1)}, bf16[16,2432]{1,0:T(8,128)(2,1)S(1)}, u32[]{:S(2)}, u32[]{:S(2)}) %collective-permute-start.24) | collective-permute-done | bytes 77856 | tf_op jit(solution)/shard_map/ppermute | solution.py:372
  64.0 0.5 collective-permute-start.25
  64.5 3.0 %collective-permute-start.26 = (bf16[16,2432]{1,0:T(8,128)(2,1)S(1)}, bf16[16,2432]{1,0:T(8,128)(2,1)S(1)}, u32[]{:S(2)}, u32[]{:S(2)}) collective-permute-start(bf16[16,2432]{1,0:T(8,128)(2,1)S(1)} %add_convert_fusion.2.refs_0_), channel_id=1, source_target_pairs={{0,4},{1,5},{2,6},{3,7},{4,0},{5,1},{6,2},{7,3},{8,12},{9,13},{10,... | collective-permute-start | bytes 233480 | tf_op jit(solution)/shard_map/ppermute | solution.py:375
  67.5 1.0 %collective-permute-start.27 = (bf16[16,2432]{1,0:T(8,128)(2,1)S(1)}, bf16[16,2432]{1,0:T(8,128)(2,1)S(1)}, u32[]{:S(2)}, u32[]{:S(2)}) collective-permute-start(bf16[16,2432]{1,0:T(8,128)(2,1)S(1)} %add_convert_fusion.2.refs_0_), channel_id=1, source_target_pairs={{0,6},{1,7},{2,4},{3,5},{4,2},{5,3},{6,0},{7,1},{8,14},{9,15},{10,... | collective-permute-start | bytes 233480 | tf_op jit(solution)/shard_map/ppermute | solution.py:375
  68.4 4.1 %collective-permute-done.10 = bf16[256,512]{1,0:T(8,128)(2,1)S(1)} collective-permute-done((bf16[256,512]{1,0:T(8,128)(2,1)S(1)}, bf16[256,512]{1,0:T(8,128)(2,1)S(1)}, u32[]{:S(2)}, u32[]{:S(2)}) %collective-permute-start.10) | collective-permute-done | bytes 262176 | tf_op jit(solution)/shard_map/ppermute | solution.py:369
  72.5 0.1 add_convert_fusion.own_ref
  72.6 0.1 collective-permute-start.12
  72.7 0.5 collective-permute-start.28
  73.2 0.7 collective-permute-done.25.refs_1_
  73.9 0.5 collective-permute-start.30
  74.4 1.8 %collective-permute-done.27.refs_3_ = bf16[16,2432]{1,0:T(8,128)(2,1)S(1)} collective-permute-done((bf16[16,2432]{1,0:T(8,128)(2,1)S(1)}, bf16[16,2432]{1,0:T(8,128)(2,1)S(1)}, u32[]{:S(2)}, u32[]{:S(2)}) %collective-permute-start.27) | collective-permute-done | bytes 77856 | tf_op jit(solution)/shard_map/ppermute | solution.py:375
  76.2 0.8 %shard_map.160 = bf16[128,2048]{1,0:T(8,128)(2,1)} custom-call(bf16[128,1024]{1,0:T(8,128)(2,1)S(1)} %get-tuple-element.60.own_ref, bf16[128,1024]{1,0:T(8,128)(2,1)S(1)} %collective-permute-done.8.far_ref), custom_call_target="tpu_custom_call" | custom-call | bytes 1048576 | tf_op jit(solution)/shard_map/pallas_call | solution.py:61
  77.0 0.7 shard_map.161
  77.8 0.9 %shard_map.164 = (f32[16,4096]{1,0:T(8,128)}, f32[16,2048]{1,0:T(8,128)}, f32[16,4096]{1,0:T(8,128)}, f32[16,512]{1,0:T(8,128)}) custom-call(bf16[16,2432]{1,0:T(8,128)(2,1)S(1)} %add_convert_fusion.2.refs_0_, bf16[16,2432]{1,0:T(8,128)(2,1)S(1)} %collective-permute-done.25.refs_1_, bf16[16,2432]{1,0:T(8,128)(2,1)S(1)} %collective-permute-done.26.refs_2_, ...), custom_call_target="tpu_custom_call" | custom-call | bytes 1310720 | tf_op jit(solution)/shard_map/pallas_call | solution.py:61
  (38 shorter events, 0.1 us)
Async XLA Ops:
  0.6 1.2 %copy-start = (bf16[1,128,4096]{2,1,0:T(8,128)(2,1)S(1)}, bf16[1,128,4096]{2,1,0:T(8,128)(2,1)}, u32[]{:S(2)}) copy-start(bf16[1,128,4096]{2,1,0:T(8,128)(2,1)} %param.14) | copy-start | bytes 3145732
  1.9 1.0 %copy-start.2 = (bf16[1,128,2048]{2,1,0:T(8,128)(2,1)S(1)}, bf16[1,128,2048]{2,1,0:T(8,128)(2,1)}, u32[]{:S(2)}) copy-start(bf16[1,128,2048]{2,1,0:T(8,128)(2,1)} %param.10) | copy-start | bytes 1572868
  2.9 1.0 %copy-start.4 = (bf16[1,128,2048]{2,1,0:T(8,128)(2,1)S(1)}, bf16[1,128,2048]{2,1,0:T(8,128)(2,1)}, u32[]{:S(2)}) copy-start(bf16[1,128,2048]{2,1,0:T(8,128)(2,1)} %param.13) | copy-start | bytes 1572868
  5.0 24.2 %copy-start.10 = (s32[1,16]{1,0:T(1,128)S(1)}, s32[1,16]{1,0:T(1,128)}, u32[]{:S(2)}) copy-start(s32[1,16]{1,0:T(1,128)} %refs_0_.1) | copy-start | bytes 196
  5.0 19.8 %collective-permute-start.20 = (bf16[128,2048]{1,0:T(8,128)(2,1)}, bf16[128,2048]{1,0:T(8,128)(2,1)}, u32[]{:S(2)}, u32[]{:S(2)}) collective-permute-start(bf16[128,2048]{1,0:T(8,128)(2,1)} %get-tuple-element.72), channel_id=1, source_target_pairs={{0,1},{1,0},{2,3},{3,2},{4,5},{5,4},{6,7},{7,6},{8,9},{9,8},{10,11... | collective-permute-start | bytes 1572872 | tf_op jit(solution)/shard_map/ppermute | solution.py:360
  5.5 22.1 %collective-permute-start.1 = (bf16[128,2048]{1,0:T(8,128)(2,1)}, bf16[128,2048]{1,0:T(8,128)(2,1)}, u32[]{:S(2)}, u32[]{:S(2)}) collective-permute-start(bf16[128,2048]{1,0:T(8,128)(2,1)} %get-tuple-element.45), channel_id=1, source_target_pairs={{0,1},{1,0},{2,3},{3,2},{4,5},{5,4},{6,7},{7,6},{8,9},{9,8},{10,11... | collective-permute-start | bytes 1572872 | tf_op jit(solution)/shard_map/ppermute | solution.py:360
  8.3 3.2 %collective-permute-start = (bf16[136,512]{1,0:T(8,128)(2,1)}, bf16[136,512]{1,0:T(8,128)(2,1)S(1)}, u32[]{:S(2)}, u32[]{:S(2)}) collective-permute-start(bf16[136,512]{1,0:T(8,128)(2,1)} %get-tuple-element.44), channel_id=1, source_target_pairs={{0,1},{1,0},{2,3},{3,2},{4,5},{5,4},{6,7},{7,6},{8,9},{9,8},{10,11... | collective-permute-start | bytes 417800 | tf_op jit(solution)/shard_map/ppermute | solution.py:360
  8.8 9.4 %collective-permute-start.2 = (bf16[136,512]{1,0:T(8,128)(2,1)}, bf16[136,512]{1,0:T(8,128)(2,1)S(1)}, u32[]{:S(2)}, u32[]{:S(2)}) collective-permute-start(bf16[136,512]{1,0:T(8,128)(2,1)} %get-tuple-element.43.refs_0_.refs_5_), channel_id=1, source_target_pairs={{0,2},{1,3},{2,4},{3,5},{4,6},{5,7},{6,0},{7,1},{8,10},{9,11},{10,... | collective-permute-start | bytes 417800 | tf_op jit(solution)/shard_map/ppermute | solution.py:363
  11.4 9.5 %collective-permute-start.3 = (bf16[136,512]{1,0:T(8,128)(2,1)S(1)}, bf16[136,512]{1,0:T(8,128)(2,1)S(1)}, u32[]{:S(2)}, u32[]{:S(2)}) collective-permute-start(bf16[136,512]{1,0:T(8,128)(2,1)S(1)} %collective-permute-done.refs_1_.refs_6_), channel_id=1, source_target_pairs={{0,2},{1,3},{2,4},{3,5},{4,6},{5,7},{6,0},{7,1},{8,10},{9,11},{10,... | collective-permute-start | bytes 417800 | tf_op jit(solution)/shard_map/ppermute | solution.py:363
  18.2 17.2 %collective-permute-start.4 = (bf16[136,512]{1,0:T(8,128)(2,1)S(1)}, bf16[136,512]{1,0:T(8,128)(2,1)S(1)}, u32[]{:S(2)}, u32[]{:S(2)}) collective-permute-start(bf16[136,512]{1,0:T(8,128)(2,1)S(1)} %collective-permute-done.2.refs_0_.refs_7_), channel_id=1, source_target_pairs={{0,2},{1,3},{2,4},{3,5},{4,6},{5,7},{6,0},{7,1},{8,10},{9,11},{10,... | collective-permute-start | bytes 417800 | tf_op jit(solution)/shard_map/ppermute | solution.py:363
  20.9 14.5 %collective-permute-start.5 = (bf16[136,512]{1,0:T(8,128)(2,1)S(1)}, bf16[136,512]{1,0:T(8,128)(2,1)S(1)}, u32[]{:S(2)}, u32[]{:S(2)}) collective-permute-start(bf16[136,512]{1,0:T(8,128)(2,1)S(1)} %collective-permute-done.3.refs_1_.refs_8_), channel_id=1, source_target_pairs={{0,2},{1,3},{2,4},{3,5},{4,6},{5,7},{6,0},{7,1},{8,10},{9,11},{10,... | collective-permute-start | bytes 417800 | tf_op jit(solution)/shard_map/ppermute | solution.py:363
  20.9 15.4 %collective-permute-start.6 = (bf16[136,512]{1,0:T(8,128)(2,1)}, bf16[136,512]{1,0:T(8,128)(2,1)S(1)}, u32[]{:S(2)}, u32[]{:S(2)}) collective-permute-start(bf16[136,512]{1,0:T(8,128)(2,1)} %get-tuple-element.43.refs_0_.refs_5_), channel_id=1, source_target_pairs={{0,6},{1,7},{2,0},{3,1},{4,2},{5,3},{6,4},{7,5},{8,14},{9,15},{10,... | collective-permute-start | bytes 417800 | tf_op jit(solution)/shard_map/ppermute | solution.py:363
  24.8 11.6 %collective-permute-start.7 = (bf16[136,512]{1,0:T(8,128)(2,1)S(1)}, bf16[136,512]{1,0:T(8,128)(2,1)S(1)}, u32[]{:S(2)}, u32[]{:S(2)}) collective-permute-start(bf16[136,512]{1,0:T(8,128)(2,1)S(1)} %collective-permute-done.refs_1_.refs_6_), channel_id=1, source_target_pairs={{0,6},{1,7},{2,0},{3,1},{4,2},{5,3},{6,4},{7,5},{8,14},{9,15},{10,... | collective-permute-start | bytes 417800 | tf_op jit(solution)/shard_map/ppermute | solution.py:363
  25.2 1.2 %copy-start.1 = (bf16[1,128,4096]{2,1,0:T(8,128)(2,1)S(1)}, bf16[1,128,4096]{2,1,0:T(8,128)(2,1)}, u32[]{:S(2)}) copy-start(bf16[1,128,4096]{2,1,0:T(8,128)(2,1)} %param.14) | copy-start | bytes 3145732
  27.6 27.8 %collective-permute-start.21 = (bf16[256,1024]{1,0:T(8,128)(2,1)S(1)}, bf16[256,1024]{1,0:T(8,128)(2,1)S(1)}, u32[]{:S(2)}, u32[]{:S(2)}) collective-permute-start(bf16[256,1024]{1,0:T(8,128)(2,1)S(1)} %get-tuple-element.74), channel_id=1, source_target_pairs={{0,2},{1,3},{2,0},{3,1},{4,6},{5,7},{6,4},{7,5},{8,10},{9,11},{10,... | collective-permute-start | bytes 1572872 | tf_op jit(solution)/shard_map/ppermute | solution.py:375
  29.2 1.0 %copy-start.3 = (bf16[1,128,2048]{2,1,0:T(8,128)(2,1)S(1)}, bf16[1,128,2048]{2,1,0:T(8,128)(2,1)}, u32[]{:S(2)}) copy-start(bf16[1,128,2048]{2,1,0:T(8,128)(2,1)} %param.10) | copy-start | bytes 1572868
  30.2 1.0 %copy-start.5 = (bf16[1,128,2048]{2,1,0:T(8,128)(2,1)S(1)}, bf16[1,128,2048]{2,1,0:T(8,128)(2,1)}, u32[]{:S(2)}) copy-start(bf16[1,128,2048]{2,1,0:T(8,128)(2,1)} %param.13) | copy-start | bytes 1572868
  31.3 0.9 %copy-start.6 = (bf16[136,512]{1,0:T(8,128)(2,1)S(1)}, bf16[136,512]{1,0:T(8,128)(2,1)}, u32[]{:S(2)}) copy-start(bf16[136,512]{1,0:T(8,128)(2,1)} %get-tuple-element.43.refs_0_.refs_5_) | copy-start | bytes 417796
  34.5 2.8 %copy-start.7 = (bf16[136,512]{1,0:T(8,128)(2,1)S(1)}, bf16[136,512]{1,0:T(8,128)(2,1)}, u32[]{:S(2)}) copy-start(bf16[136,512]{1,0:T(8,128)(2,1)} %get-tuple-element.43.refs_0_.refs_5_) | copy-start | bytes 417796
  34.5 2.7 %copy-start.8 = (bf16[16,2048]{1,0:T(8,128)(2,1)S(1)}, bf16[16,2048]{1,0:T(8,128)(2,1)}, u32[]{:S(2)}) copy-start(bf16[16,2048]{1,0:T(8,128)(2,1)} %refs_3_.1) | copy-start | bytes 196612
  34.5 2.7 %copy-start.9 = (bf16[16,512]{1,0:T(8,128)(2,1)S(1)}, bf16[16,512]{1,0:T(8,128)(2,1)}, u32[]{:S(2)}) copy-start(bf16[16,512]{1,0:T(8,128)(2,1)} %refs_4_.1) | copy-start | bytes 49156
  42.0 16.6 %collective-permute-start.9 = (bf16[256,512]{1,0:T(8,128)(2,1)S(1)}, bf16[256,512]{1,0:T(8,128)(2,1)S(1)}, u32[]{:S(2)}, u32[]{:S(2)}) collective-permute-start(bf16[256,512]{1,0:T(8,128)(2,1)S(1)} %get-tuple-element.62), channel_id=1, source_target_pairs={{0,6},{1,7},{2,0},{3,1},{4,2},{5,3},{6,4},{7,5},{8,14},{9,15},{10,... | collective-permute-start | bytes 786440 | tf_op jit(solution)/shard_map/ppermute | solution.py:363
  42.7 10.3 %collective-permute-start.13 = (bf16[16,1152]{1,0:T(8,128)(2,1)S(1)}, bf16[16,1152]{1,0:T(8,128)(2,1)S(1)}, u32[]{:S(2)}, u32[]{:S(2)}) collective-permute-start(bf16[16,1152]{1,0:T(8,128)(2,1)S(1)} %get-tuple-element.69), channel_id=1, source_target_pairs={{0,2},{1,3},{2,0},{3,1},{4,6},{5,7},{6,4},{7,5},{8,10},{9,11},{10,... | collective-permute-start | bytes 110600 | tf_op jit(solution)/shard_map/ppermute | solution.py:375
  44.1 8.9 %collective-permute-start.14 = (bf16[16,1152]{1,0:T(8,128)(2,1)S(1)}, bf16[16,1152]{1,0:T(8,128)(2,1)S(1)}, u32[]{:S(2)}, u32[]{:S(2)}) collective-permute-start(bf16[16,1152]{1,0:T(8,128)(2,1)S(1)} %get-tuple-element.70), channel_id=1, source_target_pairs={{0,4},{1,5},{2,6},{3,7},{4,0},{5,1},{6,2},{7,3},{8,12},{9,13},{10,... | collective-permute-start | bytes 110600 | tf_op jit(solution)/shard_map/ppermute | solution.py:375
  44.3 9.2 %collective-permute-start.15 = (bf16[16,1152]{1,0:T(8,128)(2,1)S(1)}, bf16[16,1152]{1,0:T(8,128)(2,1)S(1)}, u32[]{:S(2)}, u32[]{:S(2)}) collective-permute-start(bf16[16,1152]{1,0:T(8,128)(2,1)S(1)} %get-tuple-element.71), channel_id=1, source_target_pairs={{0,6},{1,7},{2,4},{3,5},{4,2},{5,3},{6,0},{7,1},{8,14},{9,15},{10,... | collective-permute-start | bytes 110600 | tf_op jit(solution)/shard_map/ppermute | solution.py:375
  53.0 1.2 %collective-permute-start.16 = (bf16[16,1152]{1,0:T(8,128)(2,1)S(1)}, bf16[16,1152]{1,0:T(8,128)(2,1)S(1)}, u32[]{:S(2)}, u32[]{:S(2)}) collective-permute-start(bf16[16,1152]{1,0:T(8,128)(2,1)S(1)} %get-tuple-element.68.refs_0_), channel_id=1, source_target_pairs={{0,1},{1,0},{2,3},{3,2},{4,5},{5,4},{6,7},{7,6},{8,9},{9,8},{10,11... | collective-permute-start | bytes 110600 | tf_op jit(solution)/shard_map/ppermute | solution.py:360
  53.0 1.4 %collective-permute-start.17 = (bf16[16,1152]{1,0:T(8,128)(2,1)S(1)}, bf16[16,1152]{1,0:T(8,128)(2,1)S(1)}, u32[]{:S(2)}, u32[]{:S(2)}) collective-permute-start(bf16[16,1152]{1,0:T(8,128)(2,1)S(1)} %collective-permute-done.13.refs_1_), channel_id=1, source_target_pairs={{0,1},{1,0},{2,3},{3,2},{4,5},{5,4},{6,7},{7,6},{8,9},{9,8},{10,11... | collective-permute-start | bytes 110600 | tf_op jit(solution)/shard_map/ppermute | solution.py:360
  53.5 1.3 %collective-permute-start.18 = (bf16[16,1152]{1,0:T(8,128)(2,1)S(1)}, bf16[16,1152]{1,0:T(8,128)(2,1)S(1)}, u32[]{:S(2)}, u32[]{:S(2)}) collective-permute-start(bf16[16,1152]{1,0:T(8,128)(2,1)S(1)} %collective-permute-done.14.refs_2_), channel_id=1, source_target_pairs={{0,1},{1,0},{2,3},{3,2},{4,5},{5,4},{6,7},{7,6},{8,9},{9,8},{10,11... | collective-permute-start | bytes 110600 | tf_op jit(solution)/shard_map/ppermute | solution.py:360
  54.2 1.2 %collective-permute-start.19 = (bf16[16,1152]{1,0:T(8,128)(2,1)S(1)}, bf16[16,1152]{1,0:T(8,128)(2,1)S(1)}, u32[]{:S(2)}, u32[]{:S(2)}) collective-permute-start(bf16[16,1152]{1,0:T(8,128)(2,1)S(1)} %collective-permute-done.15.refs_3_), channel_id=1, source_target_pairs={{0,1},{1,0},{2,3},{3,2},{4,5},{5,4},{6,7},{7,6},{8,9},{9,8},{10,11... | collective-permute-start | bytes 110600 | tf_op jit(solution)/shard_map/ppermute | solution.py:360
  54.4 13.1 %collective-permute-start.11 = (bf16[256,512]{1,0:T(8,128)(2,1)S(1)}, bf16[256,512]{1,0:T(8,128)(2,1)S(1)}, u32[]{:S(2)}, u32[]{:S(2)}) collective-permute-start(bf16[256,512]{1,0:T(8,128)(2,1)S(1)} %get-tuple-element.65), channel_id=1, source_target_pairs={{0,2},{1,3},{2,4},{3,5},{4,6},{5,7},{6,0},{7,1},{8,10},{9,11},{10,... | collective-permute-start | bytes 786440 | tf_op jit(solution)/shard_map/ppermute | solution.py:363
  54.8 17.9 %collective-permute-start.8 = (bf16[128,1024]{1,0:T(8,128)(2,1)S(1)}, bf16[128,1024]{1,0:T(8,128)(2,1)S(1)}, u32[]{:S(2)}, u32[]{:S(2)}) collective-permute-start(bf16[128,1024]{1,0:T(8,128)(2,1)S(1)} %get-tuple-element.61), channel_id=1, source_target_pairs={{0,1},{1,0},{2,3},{3,2},{4,5},{5,4},{6,7},{7,6},{8,9},{9,8},{10,11... | collective-permute-start | bytes 786440 | tf_op jit(solution)/shard_map/ppermute | solution.py:360
  55.8 4.5 %collective-permute-start.22 = (bf16[16,2432]{1,0:T(8,128)(2,1)S(1)}, bf16[16,2432]{1,0:T(8,128)(2,1)S(1)}, u32[]{:S(2)}, u32[]{:S(2)}) collective-permute-start(bf16[16,2432]{1,0:T(8,128)(2,1)S(1)} %shard_map.163), channel_id=1, source_target_pairs={{0,8},{8,0},{16,24},{24,16},{1,9},{9,1},{17,25},{25,17},{2,10},{10... | collective-permute-start | bytes 233480 | tf_op jit(solution)/shard_map/ppermute | solution.py:372
  57.1 5.1 %collective-permute-start.23 = (bf16[16,2432]{1,0:T(8,128)(2,1)S(1)}, bf16[16,2432]{1,0:T(8,128)(2,1)S(1)}, u32[]{:S(2)}, u32[]{:S(2)}) collective-permute-start(bf16[16,2432]{1,0:T(8,128)(2,1)S(1)} %shard_map.163), channel_id=1, source_target_pairs={{0,16},{8,24},{16,0},{24,8},{1,17},{9,25},{17,1},{25,9},{2,18},{10... | collective-permute-start | bytes 233480 | tf_op jit(solution)/shard_map/ppermute | solution.py:372
  58.6 5.3 %collective-permute-start.24 = (bf16[16,2432]{1,0:T(8,128)(2,1)S(1)}, bf16[16,2432]{1,0:T(8,128)(2,1)S(1)}, u32[]{:S(2)}, u32[]{:S(2)}) collective-permute-start(bf16[16,2432]{1,0:T(8,128)(2,1)S(1)} %shard_map.163), channel_id=1, source_target_pairs={{0,24},{8,16},{16,8},{24,0},{1,25},{9,17},{17,9},{25,1},{2,26},{10... | collective-permute-start | bytes 233480 | tf_op jit(solution)/shard_map/ppermute | solution.py:372
  60.3 12.3 %collective-permute-start.10 = (bf16[256,512]{1,0:T(8,128)(2,1)S(1)}, bf16[256,512]{1,0:T(8,128)(2,1)S(1)}, u32[]{:S(2)}, u32[]{:S(2)}) collective-permute-start(bf16[256,512]{1,0:T(8,128)(2,1)S(1)} %add_convert_fusion.1), channel_id=1, source_target_pairs={{2,0},{3,1},{4,2},{5,3},{6,4},{7,5},{10,8},{11,9},{12,10},{13,11},... | collective-permute-start | bytes 786440 | tf_op jit(solution)/shard_map/ppermute | solution.py:369
  64.0 9.9 %collective-permute-start.25 = (bf16[16,2432]{1,0:T(8,128)(2,1)S(1)}, bf16[16,2432]{1,0:T(8,128)(2,1)S(1)}, u32[]{:S(2)}, u32[]{:S(2)}) collective-permute-start(bf16[16,2432]{1,0:T(8,128)(2,1)S(1)} %add_convert_fusion.2.refs_0_), channel_id=1, source_target_pairs={{0,2},{1,3},{2,0},{3,1},{4,6},{5,7},{6,4},{7,5},{8,10},{9,11},{10,... | collective-permute-start | bytes 233480 | tf_op jit(solution)/shard_map/ppermute | solution.py:375
  64.5 9.4 %collective-permute-start.26 = (bf16[16,2432]{1,0:T(8,128)(2,1)S(1)}, bf16[16,2432]{1,0:T(8,128)(2,1)S(1)}, u32[]{:S(2)}, u32[]{:S(2)}) collective-permute-start(bf16[16,2432]{1,0:T(8,128)(2,1)S(1)} %add_convert_fusion.2.refs_0_), channel_id=1, source_target_pairs={{0,4},{1,5},{2,6},{3,7},{4,0},{5,1},{6,2},{7,3},{8,12},{9,13},{10,... | collective-permute-start | bytes 233480 | tf_op jit(solution)/shard_map/ppermute | solution.py:375
  67.5 8.7 %collective-permute-start.27 = (bf16[16,2432]{1,0:T(8,128)(2,1)S(1)}, bf16[16,2432]{1,0:T(8,128)(2,1)S(1)}, u32[]{:S(2)}, u32[]{:S(2)}) collective-permute-start(bf16[16,2432]{1,0:T(8,128)(2,1)S(1)} %add_convert_fusion.2.refs_0_), channel_id=1, source_target_pairs={{0,6},{1,7},{2,4},{3,5},{4,2},{5,3},{6,0},{7,1},{8,14},{9,15},{10,... | collective-permute-start | bytes 233480 | tf_op jit(solution)/shard_map/ppermute | solution.py:375
  72.6 4.4 %collective-permute-start.12 = (bf16[128,512]{1,0:T(8,128)(2,1)S(1)}, bf16[128,512]{1,0:T(8,128)(2,1)S(1)}, u32[]{:S(2)}, u32[]{:S(2)}) collective-permute-start(bf16[128,512]{1,0:T(8,128)(2,1)S(1)} %slice.4), channel_id=1, source_target_pairs={{0,1},{1,0},{2,3},{3,2},{4,5},{5,4},{6,7},{7,6},{8,9},{9,8},{10,11... | collective-permute-start | bytes 393224 | tf_op jit(solution)/shard_map/ppermute | solution.py:360
  72.7 5.0 %collective-permute-start.28 = (bf16[16,2432]{1,0:T(8,128)(2,1)S(1)}, bf16[16,2432]{1,0:T(8,128)(2,1)S(1)}, u32[]{:S(2)}, u32[]{:S(2)}) collective-permute-start(bf16[16,2432]{1,0:T(8,128)(2,1)S(1)} %add_convert_fusion.2.refs_0_), channel_id=1, source_target_pairs={{0,1},{1,0},{2,3},{3,2},{4,5},{5,4},{6,7},{7,6},{8,9},{9,8},{10,11... | collective-permute-start | bytes 233480 | tf_op jit(solution)/shard_map/ppermute | solution.py:360
  73.9 3.9 %collective-permute-start.29 = (bf16[16,2432]{1,0:T(8,128)(2,1)S(1)}, bf16[16,2432]{1,0:T(8,128)(2,1)S(1)}, u32[]{:S(2)}, u32[]{:S(2)}) collective-permute-start(bf16[16,2432]{1,0:T(8,128)(2,1)S(1)} %collective-permute-done.25.refs_1_), channel_id=1, source_target_pairs={{0,1},{1,0},{2,3},{3,2},{4,5},{5,4},{6,7},{7,6},{8,9},{9,8},{10,11... | collective-permute-start | bytes 233480 | tf_op jit(solution)/shard_map/ppermute | solution.py:360
  73.9 3.9 %collective-permute-start.30 = (bf16[16,2432]{1,0:T(8,128)(2,1)S(1)}, bf16[16,2432]{1,0:T(8,128)(2,1)S(1)}, u32[]{:S(2)}, u32[]{:S(2)}) collective-permute-start(bf16[16,2432]{1,0:T(8,128)(2,1)S(1)} %collective-permute-done.26.refs_2_), channel_id=1, source_target_pairs={{0,1},{1,0},{2,3},{3,2},{4,5},{5,4},{6,7},{7,6},{8,9},{9,8},{10,11... | collective-permute-start | bytes 233480 | tf_op jit(solution)/shard_map/ppermute | solution.py:360
  76.2 1.6 %collective-permute-start.31 = (bf16[16,2432]{1,0:T(8,128)(2,1)S(1)}, bf16[16,2432]{1,0:T(8,128)(2,1)S(1)}, u32[]{:S(2)}, u32[]{:S(2)}) collective-permute-start(bf16[16,2432]{1,0:T(8,128)(2,1)S(1)} %collective-permute-done.27.refs_3_), channel_id=1, source_target_pairs={{0,1},{1,0},{2,3},{3,2},{4,5},{5,4},{6,7},{7,6},{8,9},{9,8},{10,11... | collective-permute-start | bytes 233480 | tf_op jit(solution)/shard_map/ppermute | solution.py:360
